TPU v7x, 512 devices: a whole 4x4x16 slice. The times are simulated.
512 devices in a mesh: dp: 32 (over z_lo, y, core), expert: 16 (over z_hi, x).
Axes of the slice: x: 4, y: 4, z: 16 (z_hi: 4, z_lo: 4; z = z_hi * 4 + z_lo), core: 2. Of those that a mesh axis runs over, the one named last changes fastest.
Arguments:
- grad_out: bfloat16 [65536, 7168], P(('dp', 'expert')), may hold values from -6 to 6
- gate_weights: float32 [65536, 8], P(('dp', 'expert')), may hold values from 0.05 to 1
- route_ids: int32 [65536, 8], P(('dp', 'expert')), may hold values from 0 to 255, all different within a row
- replica_pick: int32 [65536, 8], P(('dp', 'expert')), may hold values from 0 to 1
- placement: int32 [32], replicated, may hold values from 0 to 255, as said below
- hidden_act: bfloat16 [32, 16, 32, 4, 1024], P('dp', None, 'expert'), may hold values from -6 to 6
- down_proj: bfloat16 [32, 7168, 1024], P('expert', 'dp'), may hold values from -0.1875 to 0.1875
Outputs:
- grad_w: bfloat16 [32, 7168, 1024], P('expert', 'dp')
- grad_gate: float32 [65536, 8], P(('dp', 'expert'))
Inputs may be any that keep to these rules, and one draw needn't show every extreme that they name: `placement`: the 32 entries name 24 distinct experts; instance e * 2 and instance (e + 8) * 2 hold the same expert for e < 8; every other held expert is held by exactly one instance. `route_ids`: the 8 ids of a token differ.
All inputs are finite; a program needn't handle non-finite values.
Results may differ from a plain program's by a relative error of at most 0.0056.
Values may be sent and summed in bfloat16 or wider, within the bound.
No kernel may reach another device: no remote copies, remote signals or barrier semaphores. Data moves between devices by JAX's collectives and lax.ppermute only.
A program may use at most 128 MiB of HBM per device.

v0:
```python
import jax
import jax.numpy as jnp
from jax import lax
from jax.sharding import PartitionSpec as P


def swapped(block, axis, bit):
    count = lax.axis_size(axis)
    route = []
    for low in range(count):
        high = low | 1 << bit
        if high != low and high < count:
            route += [(low, high), (high, low)]
    return lax.ppermute(block, axis, route)


def route_slots(flat_ids, flat_pick, placement, capacity):
    instances = placement.shape[0]
    numbers = jnp.arange(instances, dtype=jnp.int32)
    matches = placement[None, :] == flat_ids[:, None]
    held = jnp.any(matches, axis=1)
    first_copy = jnp.min(jnp.where(matches, numbers[None, :], instances), axis=1)
    last_copy = jnp.max(jnp.where(matches, numbers[None, :], -1), axis=1)
    target = jnp.where(flat_pick == 0, first_copy, last_copy)
    onehot = (target[:, None] == numbers[None, :]).astype(jnp.int32)
    earlier = jnp.cumsum(onehot, axis=0) - onehot
    slot_rank = jnp.sum(earlier * onehot, axis=1)
    kept_route = jnp.logical_and(held, slot_rank < capacity)
    position = jnp.where(kept_route, target * capacity + slot_rank, instances * capacity)
    return (position, kept_route)


def per_device(grad_out, gate_weights, route_ids, replica_pick, placement, hidden_act, down_proj):
    expert_count = lax.axis_size("expert")
    tokens_here, top_count = route_ids.shape
    slots_here = hidden_act.shape[2]
    capacity = hidden_act.shape[3]
    model_width = grad_out.shape[1]
    position, kept_route = route_slots(
        route_ids.reshape(-1), replica_pick.reshape(-1), placement, capacity
    )
    total_slots = placement.shape[0] * capacity
    numbers = jnp.arange(total_slots, dtype=jnp.int32)
    selector = (position[:, None] == numbers[None, :]).astype(jnp.float32)
    token_select = jnp.sum(selector.reshape(tokens_here, top_count, total_slots), axis=1).astype(
        jnp.bfloat16
    )
    gate_low = gate_weights.astype(jnp.bfloat16).reshape(-1)
    send_rows = jnp.dot(token_select.T, grad_out, preferred_element_type=jnp.float32).astype(
        jnp.bfloat16
    )
    send_rows = send_rows.reshape(expert_count, slots_here, capacity, model_width)
    send_gates = jnp.sum(selector * gate_low.astype(jnp.float32)[:, None], axis=0).astype(
        jnp.bfloat16
    )
    send_gates = send_gates.reshape(expert_count, slots_here, capacity)
    recv_rows, recv_gates = (
        lax.all_to_all(send_rows, "expert", split_axis=0, concat_axis=0, tiled=True),
        lax.all_to_all(send_gates, "expert", split_axis=0, concat_axis=0, tiled=True),
    )
    local_hidden = hidden_act[0]
    partner_bit = expert_count.bit_length() - 2
    partner_rows, partner_gates, partner_hidden = swapped(
        (recv_rows[:, 0], recv_gates[:, 0], local_hidden[:, 0]), "expert", partner_bit
    )
    recv_rows = jnp.concatenate([recv_rows, partner_rows[:, None]], axis=1)
    recv_gates = jnp.concatenate([recv_gates, partner_gates[:, None]], axis=1)
    local_hidden = jnp.concatenate([local_hidden, partner_hidden[:, None]], axis=1)
    split_rows = lax.all_to_all(recv_rows[None], "dp", split_axis=4, concat_axis=0, tiled=True)
    hidden_piece = lax.all_gather(local_hidden[None], "dp", axis=0, tiled=True)
    gate_piece = lax.all_gather(recv_gates[None], "dp", axis=0, tiled=True)
    scaled = (gate_piece.astype(jnp.float32)[..., None] * split_rows.astype(jnp.float32)).astype(
        jnp.bfloat16
    )
    weight_acc = jnp.einsum(
        "gsicd,gsicf->idf", scaled, hidden_piece, preferred_element_type=jnp.float32
    )
    outputs = jnp.einsum(
        "gsicf,idf->gsicd",
        hidden_piece[:, :, :slots_here],
        down_proj,
        preferred_element_type=jnp.float32,
    )
    partial_dot = jnp.sum(outputs * split_rows[:, :, :slots_here].astype(jnp.float32), axis=4)
    gate_acc = partial_dot
    weight_acc, gate_acc = (weight_acc, gate_acc)
    gate_own = lax.psum_scatter(gate_acc, "dp", scatter_dimension=0, tiled=True)
    gate_back = lax.all_to_all(gate_own[0], "expert", split_axis=0, concat_axis=0, tiled=True)
    grad_gate = jnp.sum(selector * gate_back.reshape(-1)[None, :], axis=1).reshape(
        tokens_here, top_count
    )
    hot_grad = weight_acc[0] + weight_acc[slots_here]
    grad_w = jnp.concatenate([hot_grad[None], weight_acc[1:slots_here]], axis=0).astype(
        jnp.bfloat16
    )
    return (grad_w, grad_gate)


def solution(mesh):
    return jax.shard_map(
        per_device,
        mesh=mesh,
        in_specs=(
            P(("dp", "expert"), None),
            P(("dp", "expert"), None),
            P(("dp", "expert"), None),
            P(("dp", "expert"), None),
            P(),
            P("dp", None, "expert", None, None),
            P("expert", "dp", None),
        ),
        out_specs=(P("expert", "dp", None), P(("dp", "expert"), None)),
        check_vma=False,
    )
```

profile of v0, /device:TPU:1, one launch (start us, length us, event | category | flops | bytes accessed | tf_op | source)
XLA Modules:
  0.0 711.0 jit_solution(18239391606070907371)
XLA Ops:
  8.5 16.3 %collective-permute-start.2 = (bf16[16,4,1024]{2,0,1:T(8,128)(2,1)S(1)}, bf16[16,4,1024]{2,0,1:T(8,128)(2,1)S(1)}, u32[]{:S(2)}, u32[]{:S(2)}) collective-permute-start(bf16[16,4,1024]{2,0,1:T(8,128)(2,1)S(1)} %slice_bitcast_fusion.1), channel_id=1, source_target_pairs={{0,8},{8,0},{1,9},{9,1},{2,10},{10,2},{3,11},{11,3},{4,12},{12,4},... | collective-permute-start | bytes 393224 | tf_op jit(solution)/shard_map/ppermute | solution.py:14
  24.7 2.6 collective-permute-done.2
  31.1 9.0 %reduce-window.6 = s32[32,8,128]{2,1,0:T(8,128)S(1)} reduce-window(s32[32,8,128]{2,1,0:T(8,128)S(1)} %fusion.20, s32[]{:T(128)} %constant.10.clone.1), window={size=1x1x128 pad=0_0x0_0x127_0}, to_apply=%region_3.4 | reduce-window | flops 4161536 | bytes 262148 | tf_op jit(solution)/shard_map/reduce-window
  41.2 1.9 convolution_convert_fusion
  43.1 4.1 reshape.89
  47.2 121.0 %all_to_all.33 = bf16[16,2,4,7168]{3,2,1,0:T(4,128)(2,1)S(1)} all-to-all(bf16[16,2,4,7168]{3,2,1,0:T(4,128)(2,1)} %reshape.89), channel_id=1, replica_groups=mesh['dp'=32,'expert'=16] {'expert'}, dimensions={0} | all-to-all | bytes 3670016 | tf_op jit(solution)/shard_map/all_to_all | solution.py:58
  168.5 2.8 collective-permute-start.1
  171.3 69.7 %collective-permute-done.1 = bf16[16,4,7168]{2,1,0:T(4,128)(2,1)S(1)} collective-permute-done((bf16[16,4,7168]{2,1,0:T(4,128)(2,1)S(1)}, bf16[16,4,7168]{2,1,0:T(4,128)(2,1)S(1)}, u32[]{:S(2)}, u32[]{:S(2)}) %collective-permute-start.1) | collective-permute-done | bytes 917536 | tf_op jit(solution)/shard_map/ppermute | solution.py:14
  240.9 3.4 maximum_bitcast_fusion
  244.3 29.1 %copy.63 = bf16[1,16,3,4,7168]{1,3,2,0,4:T(4,128)(2,1)} copy(bf16[1,16,3,4,7168]{4,3,2,1,0:T(4,128)(2,1)} %maximum_bitcast_fusion) | data formatting | bytes 5505024 | tf_op jit(solution)/shard_map/broadcast_in_dim | solution.py:69
  273.3 24.9 %reshape.98 = bf16[32,2,21504]{2,1,0:T(2,128)(2,1)} reshape(bf16[7168,1,3,4,16]{4,3,2,1,0:T(4,128)(2,1)} %bitcast.68) | data formatting | bytes 5505024
  298.2 54.9 %all-to-all-start.2 = ((bf16[32,2,21504]{2,1,0:T(2,128)(2,1)}), bf16[32,2,21504]{2,1,0:T(2,128)(2,1)}, u32[]{:S(2)}, u32[]{:S(2)}) async-start(bf16[32,2,21504]{2,1,0:T(2,128)(2,1)} %reshape.98), calls=%async_computation.2 | async-start | bytes 5505024 | tf_op jit(solution)/shard_map/all_to_all | solution.py:69
  354.4 60.8 %all-to-all-done.2 = bf16[32,2,21504]{2,1,0:T(2,128)(2,1)} async-done(((bf16[32,2,21504]{2,1,0:T(2,128)(2,1)}), bf16[32,2,21504]{2,1,0:T(2,128)(2,1)}, u32[]{:S(2)}, u32[]{:S(2)}) %all-to-all-start.2) | async-done | bytes 2752544 | tf_op jit(solution)/shard_map/all_to_all | solution.py:69
  415.2 19.0 %reshape.99 = bf16[7168,1,3,4,16]{4,3,2,1,0:T(4,128)(2,1)} reshape(bf16[32,2,21504]{2,1,0:T(2,128)(2,1)} %all-to-all-done.2) | data formatting | bytes 5505024
  434.2 25.1 %copy.65 = bf16[1,16,3,4,32,224]{5,1,3,4,2,0:T(8,128)(2,1)} copy(bf16[1,16,3,4,32,224]{1,3,2,5,4,0:T(4,128)(2,1)} %bitcast.69) | data formatting | bytes 5505024 | tf_op jit(solution)/shard_map/all_to_all | solution.py:69
  459.3 6.7 fusion.4
  466.0 131.1 %all-reduce = f32[32,16,2,4]{1,3,2,0:T(4,128)S(1)} all-reduce(f32[32,16,2,4]{1,3,2,0:T(4,128)S(1)} %copy.70), channel_id=4, replica_groups=mesh['dp'=32,'expert'=16] {'dp'}, use_global_device_ids=true, to_apply=%region_9.10.clone | all-reduce | flops 4096 | bytes 32768
  598.5 3.7 all-to-all-start.3
  602.4 13.4 %all-to-all-done.3 = f32[16,2,4]{2,1,0:T(2,128)S(1)} async-done(((f32[16,2,4]{2,1,0:T(2,128)}), f32[16,2,4]{2,1,0:T(2,128)S(1)}, u32[]{:S(2)}, u32[]{:S(2)}) %all-to-all-start.3) | async-done | bytes 544 | tf_op jit(solution)/shard_map/all_to_all | solution.py:88
  616.5 16.2 %all_to_all.34 = bf16[16,2,4]{2,1,0:T(2,128)(2,1)S(1)} all-to-all(bf16[16,2,4]{2,1,0:T(2,128)(2,1)S(1)} %convert_element_type.56), channel_id=1, replica_groups=mesh['dp'=32,'expert'=16] {'expert'}, dimensions={0} | all-to-all | bytes 512 | tf_op jit(solution)/shard_map/all_to_all | solution.py:59
  632.8 2.2 collective-permute-start
  635.8 10.1 %collective-permute-done = bf16[16,4]{0,1:T(4,128)(2,1)S(1)} collective-permute-done((bf16[16,4]{0,1:T(4,128)(2,1)S(1)}, bf16[16,4]{0,1:T(4,128)(2,1)S(1)}, u32[]{:S(2)}, u32[]{:S(2)}) %collective-permute-start) | collective-permute-done | bytes 160 | tf_op jit(solution)/shard_map/ppermute | solution.py:14
  646.0 48.5 %all-gather = bf16[512,3,4]{2,1,0:T(4,128)(2,1)S(1)} all-gather(bf16[16,3,4]{2,1,0:T(4,128)(2,1)S(1)} %pad_maximum_fusion.2), channel_id=2, replica_groups=mesh['dp'=32,'expert'=16] {'dp'}, dimensions={0}, use_global_device_ids=true | all-gather | bytes 12672 | tf_op jit(solution)/shard_map/all_gather | solution.py:71
  695.2 7.8 %fusion.8 = f32[3,224,1024]{2,1,0:T(8,128)S(1)} fusion(bf16[32,16,3,4,1024]{4,1,0,3,2:T(8,128)(2,1)} %bitcast.82, f32[32,16,3,4]{1,3,0,2:T(4,128)S(1)} %copy.61, bf16[1,16,3,4,32,224]{5,1,3,4,2,0:T(8,128)(2,1)} %copy.65), kind=kOutput, calls=%fused_computation.10 | convolution fusion | flops 2822701056 | bytes 18112512 | tf_op jit(solution)/shard_map/gsicd,gsicf->idf/dot_general | solution.py:75
  (61 shorter events, 12.7 us)
Async XLA Ops:
  7.2 34.0 %copy-start = (bf16[128,7168]{1,0:T(8,128)(2,1)S(1)}, bf16[128,7168]{1,0:T(8,128)(2,1)}, u32[]{:S(2)}) copy-start(bf16[128,7168]{1,0:T(8,128)(2,1)} %param.7) | copy-start | bytes 5505028
  7.2 33.5 %copy-start.3 = (s32[32]{0:T(128)S(1)}, s32[32]{0:T(128)}, u32[]{:S(2)}) copy-start(s32[32]{0:T(128)} %param.11) | copy-start | bytes 388
  7.2 452.1 %all-gather.4.cloned.1.call-start = ((), (), s32[]{:S(2)}) async-start(), calls=%async_computation.4 | async-start | bytes 12976128 | tf_op jit(solution)/shard_map/all_gather | solution.py:70
  8.5 18.9 %collective-permute-start.2 = (bf16[16,4,1024]{2,0,1:T(8,128)(2,1)S(1)}, bf16[16,4,1024]{2,0,1:T(8,128)(2,1)S(1)}, u32[]{:S(2)}, u32[]{:S(2)}) collective-permute-start(bf16[16,4,1024]{2,0,1:T(8,128)(2,1)S(1)} %slice_bitcast_fusion.1), channel_id=1, source_target_pairs={{0,8},{8,0},{1,9},{9,1},{2,10},{10,2},{3,11},{11,3},{4,12},{12,4},... | collective-permute-start | bytes 393224 | tf_op jit(solution)/shard_map/ppermute | solution.py:14
  168.5 72.5 %collective-permute-start.1 = (bf16[16,4,7168]{2,1,0:T(4,128)(2,1)S(1)}, bf16[16,4,7168]{2,1,0:T(4,128)(2,1)S(1)}, u32[]{:S(2)}, u32[]{:S(2)}) collective-permute-start(bf16[16,4,7168]{2,1,0:T(4,128)(2,1)S(1)} %slice_bitcast_fusion), channel_id=1, source_target_pairs={{0,8},{8,0},{1,9},{9,1},{2,10},{10,2},{3,11},{11,3},{4,12},{12,4},... | collective-permute-start | bytes 2752520 | tf_op jit(solution)/shard_map/ppermute | solution.py:14
  298.2 117.0 %all-to-all-start.2 = ((bf16[32,2,21504]{2,1,0:T(2,128)(2,1)}), bf16[32,2,21504]{2,1,0:T(2,128)(2,1)}, u32[]{:S(2)}, u32[]{:S(2)}) async-start(bf16[32,2,21504]{2,1,0:T(2,128)(2,1)} %reshape.98), calls=%async_computation.2 | async-start | bytes 5505024 | tf_op jit(solution)/shard_map/all_to_all | solution.py:69
  434.2 25.1 %copy-start.4 = (bf16[2,224,1024]{2,1,0:T(8,128)(2,1)S(1)}, bf16[2,224,1024]{2,1,0:T(8,128)(2,1)}, u32[]{:S(2)}) copy-start(bf16[2,224,1024]{2,1,0:T(8,128)(2,1)} %param.13) | copy-start | bytes 2752516
  459.3 142.9 %copy-start.2 = (f32[128,8]{0,1:T(8,128)S(1)}, f32[128,8]{0,1:T(8,128)}, u32[]{:S(2)}) copy-start(f32[128,8]{0,1:T(8,128)} %param.8) | copy-start | bytes 12292
  598.5 17.3 %all-to-all-start.3 = ((f32[16,2,4]{2,1,0:T(2,128)}), f32[16,2,4]{2,1,0:T(2,128)S(1)}, u32[]{:S(2)}, u32[]{:S(2)}) async-start(f32[16,2,4]{2,1,0:T(2,128)} %copy.71), calls=%async_computation.3 | async-start | bytes 32768 | tf_op jit(solution)/shard_map/all_to_all | solution.py:88
  632.8 13.0 %collective-permute-start = (bf16[16,4]{0,1:T(4,128)(2,1)S(1)}, bf16[16,4]{0,1:T(4,128)(2,1)S(1)}, u32[]{:S(2)}, u32[]{:S(2)}) collective-permute-start(bf16[16,4]{0,1:T(4,128)(2,1)S(1)} %bitcast.80), channel_id=1, source_target_pairs={{0,8},{8,0},{1,9},{9,1},{2,10},{10,2},{3,11},{11,3},{4,12},{12,4},... | collective-permute-start | bytes 392 | tf_op jit(solution)/shard_map/ppermute | solution.py:14
  695.2 9.0 %copy-start.1 = (bf16[128,7168]{1,0:T(8,128)(2,1)S(1)}, bf16[128,7168]{1,0:T(8,128)(2,1)}, u32[]{:S(2)}) copy-start(bf16[128,7168]{1,0:T(8,128)(2,1)} %param.7) | copy-start | bytes 5505028
Sparse Core Ops, SparseCore 0:
  28.3 287.6 all-gather.3
where the time goes:
time: 715 us; the launch traced here: 711 us
  blocking collectives  317 us (44%)
  waiting for transfers between devices  157 us (22%)
  local copies, waits for them, and re-layouts  111 us (16%)
  starting transfers between devices  79.8 us (11%)
  matrix products  16.4 us (2%)
  other arithmetic  16.2 us (2%)
  between operations  14.3 us (2%)
    unnamed x1, blocking collectives  131 us
    all_to_all x1, blocking collectives, per_device(): lax.all_to_all(send_rows, 'expert', split_axis=0, concat_axis=0, tiled=True)  121 us
    ppermute x3, waiting for transfers between devices, swapped(): return lax.ppermute(block, axis, route)  82.4 us
    all_to_all x1, waiting for transfers between devices, per_device(): lax.all_to_all(recv_rows[None], 'dp', split_axis=4, concat_axis=0, tiled=...  60.8 us
    all_to_all x1, starting transfers between devices, per_device(): lax.all_to_all(recv_rows[None], 'dp', split_axis=4, concat_axis=0, tiled=...  54.9 us
    unnamed x17, local copies, waits for them, and re-layouts  48.6 us
    all_gather x1, blocking collectives, per_device(): gate_piece = lax.all_gather(recv_gates[None], 'dp', axis=0, tiled=True)  48.5 us
    broadcast_in_dim x1, local copies, waits for them, and re-layouts, per_device(): recv_rows[None]  29.1 us
  transfers between devices with their start and end apart: 6, of which 5 were waited for; matrix products, arithmetic and copies ran while one was open for 17% of the time, Pallas kernels for 0%

commit v1 on v0

v1 whole, which is shorter than its diff:
```python
import functools
import jax
import jax.numpy as jnp
from jax import lax
from jax.experimental import pallas as pl
from jax.experimental.pallas import tpu as pltpu
from jax.sharding import PartitionSpec as P

F32 = jnp.float32
BF16 = jnp.bfloat16
INSTANCES = 32
CAP = 4
TOP = 8
TOK = 128
SLOTS = INSTANCES * CAP
PIECE = 224
WIDE = 256


def route_masks(ids_ref, pick_ref, place_ref):
    rows = lax.broadcasted_iota(jnp.int32, (INSTANCES, TOK), 0)
    place = jnp.zeros((INSTANCES, TOK), jnp.int32)
    for i in range(INSTANCES):
        place = jnp.where(rows == i, place_ref[i], place)
    single = rows % 2 == 1
    first = rows < INSTANCES // 2
    masks = []
    for k in range(TOP):
        low = jnp.broadcast_to(pick_ref[k : k + 1, :], (INSTANCES, TOK)) == 0
        serves = jnp.logical_or(single, low == first)
        same = jnp.broadcast_to(ids_ref[k : k + 1, :], (INSTANCES, TOK)) == place
        masks.append(jnp.where(jnp.logical_and(same, serves), 1.0, 0.0).astype(F32))
    taken = functools.reduce(jnp.add, masks)
    before = (
        lax.broadcasted_iota(jnp.int32, (TOK, TOK), 0)
        < lax.broadcasted_iota(jnp.int32, (TOK, TOK), 1)
    ).astype(F32)
    rank = jnp.dot(taken.astype(BF16), before.astype(BF16), preferred_element_type=F32)
    return masks, taken, rank


def gather_kernel(place_ref, ids_ref, pick_ref, gate_ref, grad_ref, out_ref, select_ref):
    @pl.when(pl.program_id(0) == 0)
    def _():
        masks, taken, rank = route_masks(ids_ref, pick_ref, place_ref)
        gates = jnp.zeros((INSTANCES, TOK), F32)
        for k in range(TOP):
            low = gate_ref[k : k + 1, :].astype(BF16).astype(F32)
            gates = gates + masks[k] * jnp.broadcast_to(low, (INSTANCES, TOK))
        spread = (
            lax.broadcasted_iota(jnp.int32, (SLOTS, INSTANCES), 0) // CAP
            == lax.broadcasted_iota(jnp.int32, (SLOTS, INSTANCES), 1)
        ).astype(F32).astype(BF16)
        slot_rank = jnp.dot(spread, rank.astype(BF16), preferred_element_type=F32)
        slot_gate = jnp.dot(spread, gates.astype(BF16), preferred_element_type=F32)
        own = (lax.broadcasted_iota(jnp.int32, (SLOTS, TOK), 0) % CAP).astype(F32)
        select_ref[...] = jnp.where(slot_rank == own, slot_gate, 0.0).astype(BF16)

    rows = jnp.dot(select_ref[...], grad_ref[...], preferred_element_type=F32)
    blank = jnp.zeros((SLOTS, WIDE - PIECE), F32)
    for j in range(4):
        part = jnp.concatenate([rows[:, j * PIECE : (j + 1) * PIECE], blank], axis=1)
        out_ref[j] = part.astype(BF16)


def gather_rows(placement, ids, pick, gates, grad_out):
    width = grad_out.shape[1]
    steps = width // (4 * PIECE)
    whole = pl.BlockSpec((TOP, TOK), lambda s: (0, 0))
    return pl.pallas_call(
        gather_kernel,
        grid=(steps,),
        in_specs=[
            pl.BlockSpec(memory_space=pltpu.SMEM),
            whole,
            whole,
            whole,
            pl.BlockSpec((TOK, 4 * PIECE), lambda s: (0, s)),
        ],
        out_specs=pl.BlockSpec((4, SLOTS, WIDE), lambda s: (s, 0, 0)),
        out_shape=jax.ShapeDtypeStruct((steps * 4, SLOTS, WIDE), BF16),
        scratch_shapes=[pltpu.VMEM((SLOTS, TOK), BF16)],
        cost_estimate=pl.CostEstimate(
            flops=2 * SLOTS * TOK * width, bytes_accessed=4 * TOK * width, transcendentals=0
        ),
        name="gather_rows",
    )(placement, ids, pick, gates, grad_out)


def expert_kernel(rows_ref, hidden_ref, weight_ref, hot_ref, send_ref, cold_ref, gate_ref, acc_ref):
    step = pl.program_id(0)
    groups = hidden_ref.shape[0]
    count = rows_ref.shape[0] // 2
    both = rows_ref[...].astype(F32).reshape(count // 8, 2, 8, WIDE)
    even, odd = both[:, 0], both[:, 1]
    upper = lax.broadcasted_iota(jnp.int32, even.shape, 1) < CAP
    split = (
        jnp.where(upper, even, pltpu.roll(odd, 4, 1)),
        jnp.where(upper, pltpu.roll(even, 4, 1), odd),
    )
    ones = jnp.ones((8, PIECE), F32)
    for i in range(2):
        rows = split[i].reshape(count, WIDE)[:, :PIECE]
        hidden = hidden_ref[:, i].reshape(count, hidden_ref.shape[3])
        grad = lax.dot_general(
            rows.astype(BF16), hidden, (((0,), (0,)), ((), ())), preferred_element_type=F32
        )

        @pl.when(step == 0)
        def _():
            acc_ref[i] = grad

        @pl.when(step != 0)
        def _():
            acc_ref[i] += grad

        result = lax.dot_general(
            hidden, weight_ref[i], (((1,), (1,)), ((), ())), preferred_element_type=F32
        )
        dots = lax.dot_general(
            ones,
            result * rows,
            (((1,), (1,)), ((), ())),
            precision=lax.Precision.HIGHEST,
            preferred_element_type=F32,
        )
        span = count // groups
        for g in range(groups):
            gate_ref[g, i : i + 1, :] = dots[0:1, g * span : (g + 1) * span]

    @pl.when(step == pl.num_programs(0) - 1)
    def _():
        hot_ref[...] = acc_ref[0]
        send_ref[...] = acc_ref[0].astype(BF16)
        cold_ref[...] = acc_ref[1].astype(BF16)


def expert_grads(rows, hidden, weight):
    dp, _, span, ff = hidden.shape
    groups = 4
    steps = dp // groups
    fixed = lambda s: (0, 0)
    return pl.pallas_call(
        expert_kernel,
        grid=(steps,),
        in_specs=[
            pl.BlockSpec((groups * span * 2, WIDE), lambda s: (s, 0)),
            pl.BlockSpec((groups, 2, span, ff), lambda s: (s, 0, 0, 0)),
            pl.BlockSpec((2, PIECE, ff), lambda s: (0, 0, 0)),
        ],
        out_specs=[
            pl.BlockSpec((PIECE, ff), fixed),
            pl.BlockSpec((PIECE, ff), fixed),
            pl.BlockSpec((PIECE, ff), fixed),
            pl.BlockSpec((groups, 2, span), lambda s: (s, 0, 0)),
        ],
        out_shape=[
            jax.ShapeDtypeStruct((PIECE, ff), F32),
            jax.ShapeDtypeStruct((PIECE, ff), BF16),
            jax.ShapeDtypeStruct((PIECE, ff), BF16),
            jax.ShapeDtypeStruct((dp, 2, span), F32),
        ],
        scratch_shapes=[pltpu.VMEM((2, PIECE, ff), F32)],
        cost_estimate=pl.CostEstimate(
            flops=8 * dp * span * PIECE * ff,
            bytes_accessed=2 * hidden.size + 2 * rows.size + 2 * weight.size,
            transcendentals=0,
        ),
        name="expert_grads",
    )(rows, hidden, weight)


def pick_kernel(place_ref, ids_ref, pick_ref, gate_ref, back_ref, out_ref):
    masks, taken, rank = route_masks(ids_ref, pick_ref, place_ref)
    value = jnp.zeros((INSTANCES, TOK), F32)
    for c in range(CAP):
        column = jnp.broadcast_to(back_ref[:, c : c + 1], (INSTANCES, TOK))
        value = jnp.where(rank == c, column, value)
    for k in range(TOP):
        total = jnp.sum(masks[k] * value, axis=0, keepdims=True)
        low = gate_ref[k : k + 1, :].astype(BF16).astype(F32)
        out_ref[k : k + 1, :] = total / low


def pick_gates(placement, ids, pick, gates, back):
    vmem = pl.BlockSpec(memory_space=pltpu.VMEM)
    return pl.pallas_call(
        pick_kernel,
        in_specs=[pl.BlockSpec(memory_space=pltpu.SMEM)] + [vmem] * 4,
        out_specs=vmem,
        out_shape=jax.ShapeDtypeStruct((TOP, TOK), F32),
        name="pick_gates",
    )(placement, ids, pick, gates, back)


def per_device(grad_out, gate_weights, route_ids, replica_pick, placement, hidden_act, down_proj):
    dp, expert = lax.axis_size("dp"), lax.axis_size("expert")
    ff = hidden_act.shape[4]
    local = hidden_act[0].transpose(1, 0, 2, 3).reshape(1, 2, expert * CAP, ff)
    hidden = lax.all_gather(local, "dp", axis=0, tiled=True)
    ids, pick, gates = route_ids.T, replica_pick.T, gate_weights.T
    sent = gather_rows(placement, ids, pick, gates, grad_out)
    rows = lax.all_to_all(
        sent.reshape(dp * expert, 2 * CAP, WIDE),
        ("dp", "expert"),
        split_axis=0,
        concat_axis=0,
        tiled=True,
    )
    hot, hot_sent, cold, partial = expert_grads(
        rows.reshape(dp * expert * 2 * CAP, WIDE), hidden, down_proj
    )
    half = expert // 2
    other = lax.ppermute(hot_sent, "expert", [(e, (e + half) % expert) for e in range(expert)])
    spread = lax.all_to_all(partial, "dp", split_axis=0, concat_axis=0, tiled=True)
    own = jnp.sum(spread, axis=0).reshape(2, expert, CAP).transpose(1, 0, 2)
    back = lax.all_to_all(own, "expert", split_axis=0, concat_axis=0, tiled=True)
    grad_gate = pick_gates(placement, ids, pick, gates, back.reshape(INSTANCES, CAP)).T
    grad_w = jnp.stack([(hot + other.astype(F32)).astype(BF16), cold], axis=0)
    return grad_w, grad_gate


def solution(mesh):
    return jax.shard_map(
        per_device,
        mesh=mesh,
        in_specs=(
            P(("dp", "expert"), None),
            P(("dp", "expert"), None),
            P(("dp", "expert"), None),
            P(("dp", "expert"), None),
            P(),
            P("dp", None, "expert", None, None),
            P("expert", "dp", None),
        ),
        out_specs=(P("expert", "dp", None), P(("dp", "expert"), None)),
        check_vma=False,
    )
```

time: 715 us -> 283 us (0.40)
  waiting for transfers between devices: 157 us -> 10.4 us
  blocking collectives: 317 us -> 209 us
  local copies, waits for them, and re-layouts: 111 us -> 3.36 us
  starting transfers between devices: 79.8 us -> 11.4 us
  Pallas kernels: 0 us -> 30.7 us
  matrix products: 16.4 us -> 0 us
  other arithmetic: 16.2 us -> 3.03 us
    unnamed x1 -> x0, blocking collectives: 131 us -> none
    ppermute x3 -> x1, waiting for transfers between devices: 82.4 us -> 0.01 us  [per_device(): lax.ppermute(hot_sent, 'expert', [(e, (e + half) % expert) for e in range...]
    all_to_all x2 -> x0, waiting for transfers between devices: 74.2 us -> none  [the longest x1 60.8 us: per_device(): lax.all_to_all(recv_rows[None], 'dp', split_axis=4, concat_axis=0, tiled=...]
    all_to_all x2 -> x3, blocking collectives: 137 us -> 209 us  [the longest x1 148 us: per_device(): lax.all_to_all(sent.reshape(dp * expert, 2 * CAP, WIDE), ('dp', 'expert')...]
    all_to_all x2 -> x0, starting transfers between devices: 58.5 us -> none  [the longest x1 54.9 us: per_device(): lax.all_to_all(recv_rows[None], 'dp', split_axis=4, concat_axis=0, tiled=...]
    all_gather x1 -> x0, blocking collectives: 48.5 us -> none  [per_device(): gate_piece = lax.all_gather(recv_gates[None], 'dp', axis=0, tiled=True)]
    unnamed x17 -> x4, local copies, waits for them, and re-layouts: 48.6 us -> 0.94 us
    pallas_call x0 -> x3, Pallas kernels: none -> 30.7 us  [the longest x1 22.1 us: expert_grads(): pl.pallas_call(expert_kernel, grid=(steps,), in_specs=[pl.BlockSpec((grou...]
  transfers between devices with their start and end apart: 6 -> 2, of which waited for: 5 -> 1; matrix products, arithmetic and copies ran while one was open for 17% -> 1% of each run, Pallas kernels for 0% -> 3%
where the time goes in v1:
time: 283 us; the launch traced here: 282 us
  blocking collectives  209 us (74%)
  Pallas kernels  30.7 us (11%)
  between operations  14.1 us (5%)
  starting transfers between devices  11.4 us (4%)
  waiting for transfers between devices  10.4 us (4%)
  local copies, waits for them, and re-layouts  3.36 us (1%)
  other arithmetic  3.03 us (1%)
    all_to_all x1, blocking collectives, per_device(): lax.all_to_all(sent.reshape(dp * expert, 2 * CAP, WIDE), ('dp', 'expert')...  148 us
    all_to_all x1, blocking collectives, per_device(): lax.all_to_all(partial, 'dp', split_axis=0, concat_axis=0, tiled=True)  42.1 us
    pallas_call x1, Pallas kernels, expert_grads(): pl.pallas_call(expert_kernel, grid=(steps,), in_specs=[pl.BlockSpec((grou...  22.1 us
    all_to_all x1, blocking collectives, per_device(): lax.all_to_all(own, 'expert', split_axis=0, concat_axis=0, tiled=True)  19.3 us
    ppermute x1, starting transfers between devices, per_device(): lax.ppermute(hot_sent, 'expert', [(e, (e + half) % expert) for e in range...  11.3 us
    all_gather x1, waiting for transfers between devices, per_device(): hidden = lax.all_gather(local, 'dp', axis=0, tiled=True)  10.4 us
    pallas_call x1, Pallas kernels, gather_rows(): pl.pallas_call(gather_kernel, grid=(steps,), in_specs=[pl.BlockSpec(memor...  7.06 us
  transfers between devices with their start and end apart: 2, of which 1 were waited for; matrix products, arithmetic and copies ran while one was open for 1% of the time, Pallas kernels for 3%

profile of v1, /device:TPU:1, one launch (start us, length us, event | category | flops | bytes accessed | tf_op | source)
XLA Modules:
  0.0 282.1 jit_solution(13263016263374439901)
XLA Ops:
  7.2 0.0 all-gather.2.cloned.1.call-start
  7.2 1.0 copy.13
  8.3 0.8 reshape.21
  9.0 0.0 all-gather.2.cloned.1.call-update
  9.0 7.1 %gather_rows.1 = bf16[32,128,256]{2,1,0:T(8,128)(2,1)} custom-call(s32[32]{0:T(128)} %place_ref.3, s32[8,128]{1,0:T(8,128)} %bitcast.20, s32[8,128]{1,0:T(8,128)} %bitcast.22, f32[8,128]{1,0:T(8,128)} %bitcast.24, bf16[128,7168]{1,0:T(8,128)(2,1)} %grad_ref.1), custom_call_target="tpu_custom_call" | custom-call | flops 234881024 | bytes 3670016 | tf_op jit(solution)/shard_map/gather_rows/pallas_call | solution.py:70
  16.1 147.6 %all_to_all.15 = bf16[512,8,256]{2,1,0:T(8,128)(2,1)} all-to-all(bf16[512,8,256]{2,1,0:T(8,128)(2,1)} %bitcast.14), channel_id=1, replica_groups=mesh['dp'=32,'expert'=16] {'dp','expert'}, dimensions={0} | all-to-all | bytes 4194304 | tf_op jit(solution)/shard_map/all_to_all | solution.py:203
  163.7 10.4 %all-gather.2.cloned.1.call-done.hidden_ref = bf16[32,2,64,1024]{3,2,1,0:T(8,128)(2,1)} async-done(((bf16[1,2,64,1024]{3,2,1,0:T(8,128)(2,1)}), bf16[32,2,64,1024]{3,2,1,0:T(8,128)(2,1)}) %all-gather.2.cloned.1.call-update) | async-done | bytes 8388624 | tf_op jit(solution)/shard_map/all_gather | solution.py:200
  174.2 22.1 %expert_grads.1 = (f32[224,1024]{1,0:T(8,128)}, bf16[224,1024]{1,0:T(8,128)(2,1)}, bf16[224,1024]{1,0:T(8,128)(2,1)}, f32[32,2,64]{2,1,0:T(2,128)}) custom-call(bf16[4096,256]{1,0:T(8,128)(2,1)} %bitcast.15, bf16[32,2,64,1024]{3,2,1,0:T(8,128)(2,1)} %all-gather.2.cloned.1.call-done.hidden_ref, bf16[2,224,1024]{2,1,0:T(8,128)(2,1)} %weight_ref.1), custom_call_target="tpu_custom_call" | custom-call | flops 3758096384 | bytes 11403264 | tf_op jit(solution)/shard_map/expert_grads/pallas_call | solution.py:143
  196.3 0.0 copy-start
  196.3 11.3 %collective-permute-start = (bf16[224,1024]{1,0:T(8,128)(2,1)}, bf16[224,1024]{1,0:T(8,128)(2,1)S(1)}, u32[]{:S(2)}, u32[]{:S(2)}) collective-permute-start(bf16[224,1024]{1,0:T(8,128)(2,1)} %get-tuple-element.7), channel_id=1, source_target_pairs={{0,8},{1,9},{2,10},{3,11},{4,12},{5,13},{6,14},{7,15},{8,0},{9,1},... | collective-permute-start | bytes 1376264 | tf_op jit(solution)/shard_map/ppermute | solution.py:214
  207.6 0.9 reshape.24
  208.5 42.1 %all_to_all.16 = f32[32,1,128]{2,1,0:T(1,128)S(1)} all-to-all(f32[32,1,128]{2,1,0:T(1,128)S(1)} %reshape.24), channel_id=1, replica_groups=mesh['dp'=32,'expert'=16] {'dp'}, dimensions={0} | all-to-all | bytes 32768 | tf_op jit(solution)/shard_map/all_to_all | solution.py:215
  250.6 0.5 broadcast
  251.1 0.7 reduce
  251.8 0.1 reshape.25
  252.0 0.1 reshape.22
  252.1 19.3 %all_to_all.17 = f32[16,2,4]{2,1,0:T(2,128)} all-to-all(f32[16,2,4]{2,1,0:T(2,128)S(1)} %copy.14), channel_id=1, replica_groups=mesh['dp'=32,'expert'=16] {'expert'}, dimensions={0} | all-to-all | bytes 1024 | tf_op jit(solution)/shard_map/all_to_all | solution.py:217
  271.4 1.6 pick_gates.1
  273.0 0.0 collective-permute-done
  273.0 1.3 fusion
  274.3 0.0 copy-done
  274.3 1.0 pad_maximum_fusion
  (2 shorter events, 0.1 us)
Async XLA Ops:
  7.2 167.0 %all-gather.2.cloned.1.call-start = ((), (), s32[]{:S(2)}) async-start(), calls=%async_computation.3 | async-start | bytes 8650752 | tf_op jit(solution)/shard_map/all_gather | solution.py:200
  196.3 78.0 %copy-start = (bf16[224,1024]{1,0:T(8,128)(2,1)S(1)}, bf16[224,1024]{1,0:T(8,128)(2,1)}, u32[]{:S(2)}) copy-start(bf16[224,1024]{1,0:T(8,128)(2,1)} %get-tuple-element.8) | copy-start | bytes 1376260
  196.3 76.7 %collective-permute-start = (bf16[224,1024]{1,0:T(8,128)(2,1)}, bf16[224,1024]{1,0:T(8,128)(2,1)S(1)}, u32[]{:S(2)}, u32[]{:S(2)}) collective-permute-start(bf16[224,1024]{1,0:T(8,128)(2,1)} %get-tuple-element.7), channel_id=1, source_target_pairs={{0,8},{1,9},{2,10},{3,11},{4,12},{5,13},{6,14},{7,15},{8,0},{9,1},... | collective-permute-start | bytes 1376264 | tf_op jit(solution)/shard_map/ppermute | solution.py:214
Sparse Core Ops, SparseCore 0:
  10.7 163.4 all-gather.1

commit v2 on v1

v2 whole, which is shorter than its diff:
```python
import functools
import jax
import jax.numpy as jnp
from jax import lax
from jax.experimental import pallas as pl
from jax.experimental.pallas import tpu as pltpu
from jax.sharding import PartitionSpec as P


F32 = jnp.float32
BF16 = jnp.bfloat16
INSTANCES = 32
CAP = 4
TOP = 8
TOK = 128
SLOTS = INSTANCES * CAP
PIECE = 224
WIDE = 256


def route_masks(ids_ref, pick_ref, place_ref):
    rows = lax.broadcasted_iota(jnp.int32, (INSTANCES, TOK), 0)
    place = jnp.zeros((INSTANCES, TOK), jnp.int32)
    for i in range(INSTANCES):
        place = jnp.where(rows == i, place_ref[i], place)
    single = rows % 2 == 1
    first = rows < INSTANCES // 2
    masks = []
    for k in range(TOP):
        low = jnp.broadcast_to(pick_ref[k : k + 1, :], (INSTANCES, TOK)) == 0
        serves = jnp.logical_or(single, low == first)
        same = jnp.broadcast_to(ids_ref[k : k + 1, :], (INSTANCES, TOK)) == place
        masks.append(jnp.where(jnp.logical_and(same, serves), 1.0, 0.0).astype(F32))
    taken = functools.reduce(jnp.add, masks)
    before = (
        lax.broadcasted_iota(jnp.int32, (TOK, TOK), 0)
        < lax.broadcasted_iota(jnp.int32, (TOK, TOK), 1)
    ).astype(F32)
    rank = jnp.dot(taken.astype(BF16), before.astype(BF16), preferred_element_type=F32)
    return masks, taken, rank


def gather_kernel(place_ref, ids_ref, pick_ref, gate_ref, grad_ref, out_ref, select_ref):
    @pl.when(pl.program_id(0) == 0)
    def _():
        masks, _, rank = route_masks(ids_ref, pick_ref, place_ref)
        gates = jnp.zeros((INSTANCES, TOK), F32)
        for k in range(TOP):
            low = gate_ref[k : k + 1, :].astype(BF16).astype(F32)
            gates = gates + masks[k] * jnp.broadcast_to(low, (INSTANCES, TOK))
        spread = (
            lax.broadcasted_iota(jnp.int32, (SLOTS, INSTANCES), 0) // CAP
            == lax.broadcasted_iota(jnp.int32, (SLOTS, INSTANCES), 1)
        ).astype(F32).astype(BF16)
        slot_rank = jnp.dot(spread, rank.astype(BF16), preferred_element_type=F32)
        slot_gate = jnp.dot(spread, gates.astype(BF16), preferred_element_type=F32)
        own = (lax.broadcasted_iota(jnp.int32, (SLOTS, TOK), 0) % CAP).astype(F32)
        select_ref[...] = jnp.where(slot_rank == own, slot_gate, 0.0).astype(BF16)

    rows = jnp.dot(select_ref[...], grad_ref[...], preferred_element_type=F32)
    blank = jnp.zeros((SLOTS, WIDE - PIECE), F32)
    for j in range(4):
        part = jnp.concatenate([rows[:, j * PIECE : (j + 1) * PIECE], blank], axis=1)
        out_ref[j] = part.astype(BF16)


def gather_rows(placement, ids, pick, gates, grad_out):
    width = grad_out.shape[1]
    steps = width // (4 * PIECE)
    whole = pl.BlockSpec((TOP, TOK), lambda s: (0, 0))
    return pl.pallas_call(
        gather_kernel,
        grid=(steps,),
        in_specs=[
            pl.BlockSpec(memory_space=pltpu.SMEM),
            whole,
            whole,
            whole,
            pl.BlockSpec((TOK, 4 * PIECE), lambda s: (0, s)),
        ],
        out_specs=pl.BlockSpec((4, SLOTS, WIDE), lambda s: (s, 0, 0)),
        out_shape=jax.ShapeDtypeStruct((steps * 4, SLOTS, WIDE), BF16),
        scratch_shapes=[pltpu.VMEM((SLOTS, TOK), BF16)],
        cost_estimate=pl.CostEstimate(
            flops=2 * SLOTS * TOK * width, bytes_accessed=4 * TOK * width, transcendentals=0
        ),
        name="gather_rows",
    )(placement, ids, pick, gates, grad_out)


def swap_halves(first, second):
    count, lanes = first.shape
    first, second = first.reshape(count // 8, 8, lanes), second.reshape(count // 8, 8, lanes)
    upper = lax.broadcasted_iota(jnp.int32, first.shape, 1) < CAP
    return (
        jnp.where(upper, first, pltpu.roll(second, 4, 1)).reshape(count, lanes),
        jnp.where(upper, pltpu.roll(first, 4, 1), second).reshape(count, lanes),
    )


def instance_rows(rows_ref):
    count = rows_ref.shape[0] // 2
    both = rows_ref[...].astype(F32).reshape(count // 8, 2, 8, WIDE)
    return swap_halves(both[:, 0].reshape(count, WIDE), both[:, 1].reshape(count, WIDE))


def gate_kernel(place_ref, rows_ref, hidden_ref, weight_ref, gate_ref):
    split = instance_rows(rows_ref)
    count = rows_ref.shape[0] // 2
    folded = []
    for i in range(2):
        hidden = hidden_ref[:, 0, i].reshape(count, hidden_ref.shape[4])
        result = lax.dot_general(
            hidden, weight_ref[i], (((1,), (1,)), ((), ())), preferred_element_type=F32
        )
        product = result * split[i][:, :PIECE]
        blank = jnp.zeros((count, WIDE - PIECE), F32)
        tail = jnp.concatenate([product[:, 128:PIECE], blank], axis=1)
        folded.append(product[:, :128] + tail)
    even, odd = swap_halves(*folded)
    both = jnp.concatenate(
        [even.reshape(count // 8, 1, 8, 128), odd.reshape(count // 8, 1, 8, 128)], axis=1
    )
    both = both.reshape(count * 2 // 128, 128, 128)
    for g in range(count * 2 // 128):
        gate_ref[g] = jnp.sum(both[g].T, axis=0, keepdims=True)


def gate_parts(place, rows, hidden, weight):
    lines, steps, _, span, ff = hidden.shape
    dp = lines * steps
    return pl.pallas_call(
        gate_kernel,
        grid_spec=pltpu.PrefetchScalarGridSpec(
            num_scalar_prefetch=1,
            grid=(steps,),
            in_specs=[
                pl.BlockSpec((lines * span * 2, WIDE), lambda s, m: (s, 0)),
                pl.BlockSpec(
                    (lines, 1, 2, span, ff),
                    lambda s, m: (0, lax.rem(m[0] - s + steps, steps), 0, 0, 0),
                ),
                pl.BlockSpec((2, PIECE, ff), lambda s, m: (0, 0, 0)),
            ],
            out_specs=pl.BlockSpec((lines, 1, 2 * span), lambda s, m: (s, 0, 0)),
        ),
        out_shape=jax.ShapeDtypeStruct((dp, 1, 2 * span), F32),
        cost_estimate=pl.CostEstimate(
            flops=4 * dp * span * PIECE * ff,
            bytes_accessed=2 * hidden.size + 2 * rows.size + 2 * weight.size,
            transcendentals=0,
        ),
        name="gate_parts",
    )(place, rows, hidden, weight)


def grad_kernel(place_ref, rows_ref, hidden_ref, hot_ref, send_ref, out_ref, acc_ref):
    step = pl.program_id(0)
    split = instance_rows(rows_ref)
    count = rows_ref.shape[0] // 2
    for i in range(2):
        hidden = hidden_ref[:, 0, i].reshape(count, hidden_ref.shape[4])
        grad = lax.dot_general(
            split[i][:, :PIECE].astype(BF16),
            hidden,
            (((0,), (0,)), ((), ())),
            preferred_element_type=F32,
        )

        @pl.when(step == 0)
        def _():
            acc_ref[i] = grad

        @pl.when(step != 0)
        def _():
            acc_ref[i] += grad

    @pl.when(step == pl.num_programs(0) - 1)
    def _():
        hot_ref[...] = acc_ref[0]
        send_ref[...] = acc_ref[0].astype(BF16)
        out_ref[0] = acc_ref[1].astype(BF16)


def weight_parts(place, rows, hidden):
    lines, steps, _, span, ff = hidden.shape
    dp = lines * steps
    fixed = lambda s, m: (0, 0)
    return pl.pallas_call(
        grad_kernel,
        grid_spec=pltpu.PrefetchScalarGridSpec(
            num_scalar_prefetch=1,
            grid=(steps,),
            in_specs=[
                pl.BlockSpec((lines * span * 2, WIDE), lambda s, m: (s, 0)),
                pl.BlockSpec(
                    (lines, 1, 2, span, ff),
                    lambda s, m: (0, lax.rem(m[0] - s + steps, steps), 0, 0, 0),
                ),
            ],
            out_specs=[
                pl.BlockSpec((PIECE, ff), fixed),
                pl.BlockSpec((PIECE, ff), fixed),
                pl.BlockSpec((1, PIECE, ff), lambda s, m: (1, 0, 0)),
            ],
            scratch_shapes=[pltpu.VMEM((2, PIECE, ff), F32)],
        ),
        out_shape=[
            jax.ShapeDtypeStruct((PIECE, ff), F32),
            jax.ShapeDtypeStruct((PIECE, ff), BF16),
            jax.ShapeDtypeStruct((2, PIECE, ff), BF16),
        ],
        cost_estimate=pl.CostEstimate(
            flops=4 * dp * span * PIECE * ff,
            bytes_accessed=2 * hidden.size + 2 * rows.size,
            transcendentals=0,
        ),
        name="weight_parts",
    )(place, rows, hidden)


def pair_kernel(hot_ref, other_ref, grad_ref, out_ref):
    out_ref[0] = (hot_ref[...] + other_ref[...].astype(F32)).astype(BF16)


def pair_sum(hot, other, grad):
    ff = hot.shape[1]
    whole = pl.BlockSpec((PIECE, ff), lambda s: (0, 0))
    return pl.pallas_call(
        pair_kernel,
        grid=(1,),
        in_specs=[whole, whole, pl.BlockSpec(memory_space=pl.ANY)],
        out_specs=pl.BlockSpec((1, PIECE, ff), lambda s: (0, 0, 0)),
        out_shape=jax.ShapeDtypeStruct(grad.shape, BF16),
        input_output_aliases={2: 0},
        name="pair_sum",
    )(hot, other, grad)


def total_kernel(parts_ref, out_ref):
    total = jnp.sum(parts_ref[...], axis=0)
    for e in range(out_ref.shape[0]):
        out_ref[e] = total[:, e * 2 * CAP : (e + 1) * 2 * CAP]


def gate_totals(parts, expert):
    vmem = pl.BlockSpec(memory_space=pltpu.VMEM)
    return pl.pallas_call(
        total_kernel,
        in_specs=[vmem],
        out_specs=vmem,
        out_shape=jax.ShapeDtypeStruct((expert, 1, 2 * CAP), F32),
        name="gate_totals",
    )(parts)


def pick_kernel(place_ref, ids_ref, pick_ref, gate_ref, back_ref, out_ref):
    masks, _, rank = route_masks(ids_ref, pick_ref, place_ref)
    experts = back_ref.shape[0]
    spread = (
        lax.broadcasted_iota(jnp.int32, (INSTANCES, experts), 0) // 2
        == lax.broadcasted_iota(jnp.int32, (INSTANCES, experts), 1)
    ).astype(F32)
    back = jnp.dot(
        spread,
        back_ref[...].reshape(experts, 2 * CAP),
        precision=lax.Precision.HIGHEST,
        preferred_element_type=F32,
    )
    odd = lax.broadcasted_iota(jnp.int32, (INSTANCES, 1), 0) % 2 == 1
    value = jnp.zeros((INSTANCES, TOK), F32)
    for c in range(CAP):
        column = jnp.where(odd, back[:, CAP + c : CAP + c + 1], back[:, c : c + 1])
        value = jnp.where(rank == c, jnp.broadcast_to(column, (INSTANCES, TOK)), value)
    for k in range(TOP):
        total = jnp.sum(masks[k] * value, axis=0, keepdims=True)
        low = gate_ref[k : k + 1, :].astype(BF16).astype(F32)
        out_ref[k : k + 1, :] = total / low


def pick_gates(placement, ids, pick, gates, back):
    vmem = pl.BlockSpec(memory_space=pltpu.VMEM)
    return pl.pallas_call(
        pick_kernel,
        in_specs=[pl.BlockSpec(memory_space=pltpu.SMEM)] + [vmem] * 4,
        out_specs=vmem,
        out_shape=jax.ShapeDtypeStruct((TOP, TOK), F32),
        name="pick_gates",
    )(placement, ids, pick, gates, back)


LINES = ("y", "c")
EXPERT = ("zh", "x")
GROUPS = ("zl",) + LINES
EVERY = GROUPS + EXPERT


def layer(grad_out, gate_weights, route_ids, replica_pick, placement, hidden_act, down_proj):
    dp, expert = lax.axis_size(GROUPS), lax.axis_size(EXPERT)
    depth = lax.axis_size("zl")
    ff = hidden_act.shape[4]
    local = hidden_act[0].transpose(1, 0, 2, 3).reshape(1, 1, 2, expert * CAP, ff)
    column = [local] + [
        lax.ppermute(local, "zl", [(z, (z + d) % depth) for z in range(depth)])
        for d in range(1, depth)
    ]
    column = jnp.concatenate(column, axis=1)
    hidden = lax.all_gather(column, LINES, axis=0, tiled=True)
    place = lax.axis_index("zl").astype(jnp.int32).reshape(1)
    ids, pick, gates = route_ids.T, replica_pick.T, gate_weights.T
    sent = gather_rows(placement, ids, pick, gates, grad_out)
    sent = sent.reshape(dp * expert, 2 * CAP, WIDE)
    rows = lax.all_to_all(sent, EVERY, split_axis=0, concat_axis=0, tiled=True)
    rows = rows.reshape(dp * expert * 2 * CAP, WIDE)
    parts = gate_parts(place, rows, hidden, down_proj)
    parts = lax.all_to_all(parts, GROUPS, split_axis=0, concat_axis=0, tiled=True)
    hot, hot_sent, grad = weight_parts(place, rows, hidden)
    half = expert // 2
    other = lax.ppermute(hot_sent, EXPERT, [(e, (e + half) % expert) for e in range(expert)])
    own = gate_totals(parts, expert)
    back = lax.all_to_all(own, EXPERT, split_axis=0, concat_axis=0, tiled=True)
    grad_gate = pick_gates(placement, ids, pick, gates, back).T
    return pair_sum(hot, other, grad), grad_gate


def solution(mesh):
    fine = jax.sharding.Mesh(mesh.devices.reshape(4, 4, 2, 4, 4), EVERY)
    token = P(EVERY, None)
    return jax.shard_map(
        layer,
        mesh=fine,
        in_specs=(
            token,
            token,
            token,
            token,
            P(),
            P(GROUPS, None, EXPERT, None, None),
            P(EXPERT, GROUPS, None),
        ),
        out_specs=(P(EXPERT, GROUPS, None), token),
        check_vma=False,
    )
```

time: 283 us -> 266 us (0.940)
  blocking collectives: 209 us -> 60.7 us
  waiting for transfers between devices: 10.4 us -> 117 us
  starting transfers between devices: 11.4 us -> 40.4 us
  Pallas kernels: 30.7 us -> 27.7 us
    all_to_all x3 -> x2, blocking collectives: 209 us -> 60.7 us  [the longest x1 35.1 us: layer(): lax.all_to_all(parts, GROUPS, split_axis=0, concat_axis=0, tiled=True)]
    all_to_all x0 -> x1, waiting for transfers between devices: none -> 100 us  [layer(): rows = lax.all_to_all(sent, EVERY, split_axis=0, concat_axis=0, tiled=True)]
    all_to_all x0 -> x1, starting transfers between devices: none -> 23.4 us  [layer(): rows = lax.all_to_all(sent, EVERY, split_axis=0, concat_axis=0, tiled=True)]
    ppermute x1 -> x4, waiting for transfers between devices: 0.01 us -> 17 us  [the longest x3 17 us: layer(): lax.ppermute(local, 'zl', [(z, (z + d) % depth) for z in range(depth)])]
    all_gather x1, waiting for transfers between devices: 10.4 us -> 0.01 us  [layer(): hidden = lax.all_gather(column, LINES, axis=0, tiled=True)]
    ppermute x1 -> x4, starting transfers between devices: 11.3 us -> 17 us  [the longest x3 11.2 us: layer(): lax.ppermute(local, 'zl', [(z, (z + d) % depth) for z in range(depth)])]
    pallas_call x1 -> x4, Pallas kernels: 22.1 us -> 18.9 us  [the longest x1 8.2 us: weight_parts(): pl.pallas_call(grad_kernel, grid_spec=pltpu.PrefetchScalarGridSpec(num_sc...]
  transfers between devices with their start and end apart: 2 -> 6, of which waited for: 1 -> 3; matrix products, arithmetic and copies ran while one was open for 1% -> 0% of each run, Pallas kernels for 3% -> 7%
where the time goes in v2:
time: 266 us; the launch traced here: 265 us
  waiting for transfers between devices  117 us (44%)
  blocking collectives  60.7 us (23%)
  starting transfers between devices  40.4 us (15%)
  Pallas kernels  27.7 us (10%)
  between operations  14.1 us (5%)
  local copies, waits for them, and re-layouts  3.25 us (1%)
    all_to_all x1, waiting for transfers between devices, layer(): rows = lax.all_to_all(sent, EVERY, split_axis=0, concat_axis=0, tiled=True)  100 us
    all_to_all x1, blocking collectives, layer(): lax.all_to_all(parts, GROUPS, split_axis=0, concat_axis=0, tiled=True)  35.1 us
    all_to_all x1, blocking collectives, layer(): back = lax.all_to_all(own, EXPERT, split_axis=0, concat_axis=0, tiled=True)  25.6 us
    all_to_all x1, starting transfers between devices, layer(): rows = lax.all_to_all(sent, EVERY, split_axis=0, concat_axis=0, tiled=True)  23.4 us
    ppermute x3, waiting for transfers between devices, layer(): lax.ppermute(local, 'zl', [(z, (z + d) % depth) for z in range(depth)])  17 us
    ppermute x3, starting transfers between devices, layer(): lax.ppermute(local, 'zl', [(z, (z + d) % depth) for z in range(depth)])  11.2 us
    pallas_call x1, Pallas kernels, weight_parts(): pl.pallas_call(grad_kernel, grid_spec=pltpu.PrefetchScalarGridSpec(num_sc...  8.2 us
    pallas_call x1, Pallas kernels, gate_parts(): pl.pallas_call(gate_kernel, grid_spec=pltpu.PrefetchScalarGridSpec(num_sc...  7.17 us
  transfers between devices with their start and end apart: 6, of which 3 were waited for; matrix products, arithmetic and copies ran while one was open for 0% of the time, Pallas kernels for 7%

profile of v2, /device:TPU:1, one launch (start us, length us, event | category | flops | bytes accessed | tf_op | source)
XLA Modules:
  0.0 264.7 jit_solution(13827578535017529156)
XLA Ops:
  7.2 0.0 all-gather.2.cloned.1.call-start
  7.2 1.0 copy.11
  8.3 0.1 reshape.19
  8.3 7.1 %collective-permute-start.2 = (bf16[1,1,2,64,1024]{4,3,2,1,0:T(8,128)(2,1)S(1)}, bf16[1,1,2,64,1024]{4,3,2,1,0:T(8,128)(2,1)S(1)}, u32[]{:S(2)}, u32[]{:S(2)}) collective-permute-start(bf16[1,1,2,64,1024]{4,3,2,1,0:T(8,128)(2,1)S(1)} %reshape.19), channel_id=1, source_target_pairs={{0,384},{128,0},{256,128},{384,256},{1,385},{129,1},{257,129},{385... | collective-permute-start | bytes 786440 | tf_op jit(solution)/shard_map/ppermute | solution.py:304
  15.4 1.9 collective-permute-start.1
  17.3 2.2 collective-permute-start
  19.5 0.1 collective-permute-done.2
  19.7 16.8 %collective-permute-done.1 = bf16[1,1,2,64,1024]{4,3,2,1,0:T(8,128)(2,1)S(1)} collective-permute-done((bf16[1,1,2,64,1024]{4,3,2,1,0:T(8,128)(2,1)S(1)}, bf16[1,1,2,64,1024]{4,3,2,1,0:T(8,128)(2,1)S(1)}, u32[]{:S(2)}, u32[]{:S(2)}) %collective-permute-start.1) | collective-permute-done | bytes 262176 | tf_op jit(solution)/shard_map/ppermute | solution.py:304
  36.5 0.0 collective-permute-done
  36.5 1.1 pad_maximum_fusion
  37.6 0.0 all-gather.2.cloned.1.call-update
  37.6 7.0 %gather_rows.1 = bf16[32,128,256]{2,1,0:T(8,128)(2,1)} custom-call(s32[32]{0:T(128)} %place_ref.3, s32[8,128]{1,0:T(8,128)} %bitcast.14, s32[8,128]{1,0:T(8,128)} %bitcast.16, f32[8,128]{1,0:T(8,128)} %bitcast.18, bf16[128,7168]{1,0:T(8,128)(2,1)} %grad_ref.1), custom_call_target="tpu_custom_call" | custom-call | flops 234881024 | bytes 3670016 | tf_op jit(solution)/shard_map/gather_rows/pallas_call | solution.py:71
  44.7 23.4 %all-to-all-start = ((bf16[512,8,256]{2,1,0:T(8,128)(2,1)}), bf16[512,8,256]{2,1,0:T(8,128)(2,1)S(1)}, u32[]{:S(2)}, u32[]{:S(2)}) async-start(bf16[512,8,256]{2,1,0:T(8,128)(2,1)} %bitcast.12), calls=%async_computation | async-start | bytes 4194304 | tf_op jit(solution)/shard_map/all_to_all | solution.py:313
  68.1 100.5 %all-to-all-done = bf16[512,8,256]{2,1,0:T(8,128)(2,1)S(1)} async-done(((bf16[512,8,256]{2,1,0:T(8,128)(2,1)}), bf16[512,8,256]{2,1,0:T(8,128)(2,1)S(1)}, u32[]{:S(2)}, u32[]{:S(2)}) %all-to-all-start) | async-done | bytes 2097184 | tf_op jit(solution)/shard_map/all_to_all | solution.py:313
  168.5 1.4 copy-done
  169.9 8.2 %weight_parts.1 = (f32[224,1024]{1,0:T(8,128)}, bf16[224,1024]{1,0:T(8,128)(2,1)}, bf16[2,224,1024]{2,1,0:T(8,128)(2,1)}) custom-call(s32[1]{0:T(128)} %bitcast.place_ref, bf16[4096,256]{1,0:T(8,128)(2,1)} %bitcast.10, bf16[8,4,2,64,1024]{4,3,2,1,0:T(8,128)(2,1)} %all-gather.2.cloned.1.call-done.hidden_ref), custom_call_target="tpu_custom_call" | custom-call | flops 1879048192 | bytes 10485760 | tf_op jit(solution)/shard_map/weight_parts/pallas_call | solution.py:189
  178.1 5.8 %collective-permute-start.3 = (bf16[224,1024]{1,0:T(8,128)(2,1)}, bf16[224,1024]{1,0:T(8,128)(2,1)S(1)}, u32[]{:S(2)}, u32[]{:S(2)}) collective-permute-start(bf16[224,1024]{1,0:T(8,128)(2,1)} %get-tuple-element.6), channel_id=1, source_target_pairs={{0,8},{1,9},{2,10},{3,11},{4,12},{5,13},{6,14},{7,15},{8,0},{9,1},... | collective-permute-start | bytes 1376264 | tf_op jit(solution)/shard_map/ppermute | solution.py:319
  183.9 7.2 %gate_parts.1 = f32[32,1,128]{2,1,0:T(1,128)} custom-call(s32[1]{0:T(128)} %bitcast.place_ref, bf16[4096,256]{1,0:T(8,128)(2,1)} %bitcast.11, bf16[8,4,2,64,1024]{4,3,2,1,0:T(8,128)(2,1)} %all-gather.2.cloned.1.call-done.hidden_ref, bf16[2,224,1024]{2,1,0:T(8,128)(2,1)} %weight_ref.1), custom_call_target="tpu_custom_call" | custom-call | flops 1879048192 | bytes 11403264 | tf_op jit(solution)/shard_map/gate_parts/pallas_call | solution.py:132
  191.1 35.1 %all_to_all.15.parts_ref = f32[32,1,128]{2,1,0:T(1,128)} all-to-all(f32[32,1,128]{2,1,0:T(1,128)} %gate_parts.1), channel_id=1, replica_groups=mesh['zl'=4,'y'=4,'c'=2,'zh'=4,'x'=4] {'zl','y','c'}, dimensions={0} | all-to-all | bytes 32768 | tf_op jit(solution)/shard_map/all_to_all | solution.py:316
  226.2 1.4 gate_totals.1
  227.7 25.6 %all_to_all.16.back_ref = f32[16,1,8]{2,1,0:T(1,128)} all-to-all(f32[16,1,8]{2,1,0:T(1,128)} %gate_totals.1), channel_id=1, replica_groups=mesh['zl'=4,'y'=4,'c'=2,'zh'=4,'x'=4] {'zh','x'}, dimensions={0} | all-to-all | bytes 1024 | tf_op jit(solution)/shard_map/all_to_all | solution.py:321
  253.2 1.8 pick_gates.1
  255.0 0.8 copy-done.1
  255.7 2.1 pair_sum.1
  (4 shorter events, 0.0 us)
Async XLA Ops:
  7.2 161.4 %all-gather.2.cloned.1.call-start = ((), (), s32[]{:S(2)}) async-start(), calls=%async_computation.3 | async-start | bytes 9437184 | tf_op jit(solution)/shard_map/all_gather | solution.py:308
  8.3 11.4 %collective-permute-start.2 = (bf16[1,1,2,64,1024]{4,3,2,1,0:T(8,128)(2,1)S(1)}, bf16[1,1,2,64,1024]{4,3,2,1,0:T(8,128)(2,1)S(1)}, u32[]{:S(2)}, u32[]{:S(2)}) collective-permute-start(bf16[1,1,2,64,1024]{4,3,2,1,0:T(8,128)(2,1)S(1)} %reshape.19), channel_id=1, source_target_pairs={{0,384},{128,0},{256,128},{384,256},{1,385},{129,1},{257,129},{385... | collective-permute-start | bytes 786440 | tf_op jit(solution)/shard_map/ppermute | solution.py:304
  15.4 21.1 %collective-permute-start.1 = (bf16[1,1,2,64,1024]{4,3,2,1,0:T(8,128)(2,1)S(1)}, bf16[1,1,2,64,1024]{4,3,2,1,0:T(8,128)(2,1)S(1)}, u32[]{:S(2)}, u32[]{:S(2)}) collective-permute-start(bf16[1,1,2,64,1024]{4,3,2,1,0:T(8,128)(2,1)S(1)} %reshape.19), channel_id=1, source_target_pairs={{0,256},{128,384},{256,0},{384,128},{1,257},{129,385},{257,1},{385... | collective-permute-start | bytes 786440 | tf_op jit(solution)/shard_map/ppermute | solution.py:304
  17.3 19.2 %collective-permute-start = (bf16[1,1,2,64,1024]{4,3,2,1,0:T(8,128)(2,1)S(1)}, bf16[1,1,2,64,1024]{4,3,2,1,0:T(8,128)(2,1)S(1)}, u32[]{:S(2)}, u32[]{:S(2)}) collective-permute-start(bf16[1,1,2,64,1024]{4,3,2,1,0:T(8,128)(2,1)S(1)} %reshape.19), channel_id=1, source_target_pairs={{0,128},{128,256},{256,384},{384,0},{1,129},{129,257},{257,385},{3... | collective-permute-start | bytes 786440 | tf_op jit(solution)/shard_map/ppermute | solution.py:304
  44.7 123.9 %all-to-all-start = ((bf16[512,8,256]{2,1,0:T(8,128)(2,1)}), bf16[512,8,256]{2,1,0:T(8,128)(2,1)S(1)}, u32[]{:S(2)}, u32[]{:S(2)}) async-start(bf16[512,8,256]{2,1,0:T(8,128)(2,1)} %bitcast.12), calls=%async_computation | async-start | bytes 4194304 | tf_op jit(solution)/shard_map/all_to_all | solution.py:313
  168.5 1.4 copy-start
  178.1 76.9 %collective-permute-start.3 = (bf16[224,1024]{1,0:T(8,128)(2,1)}, bf16[224,1024]{1,0:T(8,128)(2,1)S(1)}, u32[]{:S(2)}, u32[]{:S(2)}) collective-permute-start(bf16[224,1024]{1,0:T(8,128)(2,1)} %get-tuple-element.6), channel_id=1, source_target_pairs={{0,8},{1,9},{2,10},{3,11},{4,12},{5,13},{6,14},{7,15},{8,0},{9,1},... | collective-permute-start | bytes 1376264 | tf_op jit(solution)/shard_map/ppermute | solution.py:319
  255.0 0.8 copy-start.1
Sparse Core Ops, SparseCore 0:
  37.7 71.1 all-gather.1

commit v3 on v2

--- a/solution.py
+++ b/solution.py
@@ -104,7 +104,7 @@
     return swap_halves(both[:, 0].reshape(count, WIDE), both[:, 1].reshape(count, WIDE))
 
 
-def gate_kernel(place_ref, rows_ref, hidden_ref, weight_ref, gate_ref):
+def gate_kernel(rows_ref, hidden_ref, weight_ref, gate_ref):
     split = instance_rows(rows_ref)
     count = rows_ref.shape[0] // 2
     folded = []
@@ -126,24 +126,18 @@
         gate_ref[g] = jnp.sum(both[g].T, axis=0, keepdims=True)
 
 
-def gate_parts(place, rows, hidden, weight):
+def gate_parts(rows, hidden, weight):
     lines, steps, _, span, ff = hidden.shape
     dp = lines * steps
     return pl.pallas_call(
         gate_kernel,
-        grid_spec=pltpu.PrefetchScalarGridSpec(
-            num_scalar_prefetch=1,
-            grid=(steps,),
-            in_specs=[
-                pl.BlockSpec((lines * span * 2, WIDE), lambda s, m: (s, 0)),
-                pl.BlockSpec(
-                    (lines, 1, 2, span, ff),
-                    lambda s, m: (0, lax.rem(m[0] - s + steps, steps), 0, 0, 0),
-                ),
-                pl.BlockSpec((2, PIECE, ff), lambda s, m: (0, 0, 0)),
-            ],
-            out_specs=pl.BlockSpec((lines, 1, 2 * span), lambda s, m: (s, 0, 0)),
-        ),
+        grid=(steps,),
+        in_specs=[
+            pl.BlockSpec((lines * span * 2, WIDE), lambda s: (s, 0)),
+            pl.BlockSpec((lines, 1, 2, span, ff), lambda s: (0, s, 0, 0, 0)),
+            pl.BlockSpec((2, PIECE, ff), lambda s: (0, 0, 0)),
+        ],
+        out_specs=pl.BlockSpec((lines, 1, 2 * span), lambda s: (s, 0, 0)),
         out_shape=jax.ShapeDtypeStruct((dp, 1, 2 * span), F32),
         cost_estimate=pl.CostEstimate(
             flops=4 * dp * span * PIECE * ff,
@@ -151,72 +145,84 @@
             transcendentals=0,
         ),
         name="gate_parts",
-    )(place, rows, hidden, weight)
-
-
-def grad_kernel(place_ref, rows_ref, hidden_ref, hot_ref, send_ref, out_ref, acc_ref):
-    step = pl.program_id(0)
-    split = instance_rows(rows_ref)
-    count = rows_ref.shape[0] // 2
-    for i in range(2):
-        hidden = hidden_ref[:, 0, i].reshape(count, hidden_ref.shape[4])
-        grad = lax.dot_general(
-            split[i][:, :PIECE].astype(BF16),
-            hidden,
-            (((0,), (0,)), ((), ())),
-            preferred_element_type=F32,
-        )
-
-        @pl.when(step == 0)
-        def _():
-            acc_ref[i] = grad
-
-        @pl.when(step != 0)
-        def _():
-            acc_ref[i] += grad
-
-    @pl.when(step == pl.num_programs(0) - 1)
-    def _():
-        hot_ref[...] = acc_ref[0]
-        send_ref[...] = acc_ref[0].astype(BF16)
-        out_ref[0] = acc_ref[1].astype(BF16)
-
-
-def weight_parts(place, rows, hidden):
+    )(rows, hidden, weight)
+
+
+def add_grad(which, rows_ref, hidden_ref, acc_ref):
+    lines, span, ff = hidden_ref.shape
+    grad = lax.dot_general(
+        instance_rows(rows_ref)[which][:, :PIECE].astype(BF16),
+        hidden_ref[...].reshape(lines * span, ff),
+        (((0,), (0,)), ((), ())),
+        preferred_element_type=F32,
+    )
+
+    @pl.when(pl.program_id(0) == 0)
+    def _():
+        acc_ref[...] = grad
+
+    @pl.when(pl.program_id(0) != 0)
+    def _():
+        acc_ref[...] += grad
+
+
+def hot_kernel(rows_ref, hidden_ref, hot_ref, send_ref, acc_ref):
+    add_grad(0, rows_ref, hidden_ref, acc_ref)
+
+    @pl.when(pl.program_id(0) == pl.num_programs(0) - 1)
+    def _():
+        hot_ref[...] = acc_ref[...]
+        send_ref[...] = acc_ref[...].astype(BF16)
+
+
+def cold_kernel(rows_ref, hidden_ref, out_ref, acc_ref):
+    add_grad(1, rows_ref, hidden_ref, acc_ref)
+
+    @pl.when(pl.program_id(0) == pl.num_programs(0) - 1)
+    def _():
+        out_ref[0] = acc_ref[...].astype(BF16)
+
+
+def weight_parts(which, rows, hidden):
     lines, steps, _, span, ff = hidden.shape
     dp = lines * steps
-    fixed = lambda s, m: (0, 0)
-    return pl.pallas_call(
-        grad_kernel,
-        grid_spec=pltpu.PrefetchScalarGridSpec(
-            num_scalar_prefetch=1,
-            grid=(steps,),
-            in_specs=[
-                pl.BlockSpec((lines * span * 2, WIDE), lambda s, m: (s, 0)),
-                pl.BlockSpec(
-                    (lines, 1, 2, span, ff),
-                    lambda s, m: (0, lax.rem(m[0] - s + steps, steps), 0, 0, 0),
-                ),
-            ],
-            out_specs=[
-                pl.BlockSpec((PIECE, ff), fixed),
-                pl.BlockSpec((PIECE, ff), fixed),
-                pl.BlockSpec((1, PIECE, ff), lambda s, m: (1, 0, 0)),
-            ],
-            scratch_shapes=[pltpu.VMEM((2, PIECE, ff), F32)],
-        ),
-        out_shape=[
-            jax.ShapeDtypeStruct((PIECE, ff), F32),
-            jax.ShapeDtypeStruct((PIECE, ff), BF16),
-            jax.ShapeDtypeStruct((2, PIECE, ff), BF16),
+    whole = pl.BlockSpec((PIECE, ff), lambda s: (0, 0))
+    hot = which == 0
+    return pl.pallas_call(
+        hot_kernel if hot else cold_kernel,
+        grid=(steps,),
+        in_specs=[
+            pl.BlockSpec((lines * span * 2, WIDE), lambda s: (s, 0)),
+            pl.BlockSpec((lines, None, None, span, ff), lambda s: (0, s, which, 0, 0)),
         ],
+        out_specs=[whole, whole] if hot else pl.BlockSpec((1, PIECE, ff), lambda s: (1, 0, 0)),
+        out_shape=[jax.ShapeDtypeStruct((PIECE, ff), t) for t in (F32, BF16)]
+        if hot
+        else jax.ShapeDtypeStruct((2, PIECE, ff), BF16),
+        scratch_shapes=[pltpu.VMEM((PIECE, ff), F32)],
         cost_estimate=pl.CostEstimate(
-            flops=4 * dp * span * PIECE * ff,
-            bytes_accessed=2 * hidden.size + 2 * rows.size,
+            flops=2 * dp * span * PIECE * ff,
+            bytes_accessed=hidden.size + 2 * rows.size,
             transcendentals=0,
         ),
-        name="weight_parts",
-    )(place, rows, hidden)
+        name="hot_parts" if hot else "cold_parts",
+    )(rows, hidden)
+
+
+def copy_kernel(in_ref, out_ref):
+    out_ref[...] = in_ref[...]
+
+
+def copied(x):
+    block = pl.BlockSpec((1,) + x.shape[1:], lambda s: (s, 0, 0, 0))
+    return pl.pallas_call(
+        copy_kernel,
+        grid=x.shape[:1],
+        in_specs=[block],
+        out_specs=block,
+        out_shape=jax.ShapeDtypeStruct(x.shape, x.dtype),
+        name="copied",
+    )(x)
 
 
 def pair_kernel(hot_ref, other_ref, grad_ref, out_ref):
@@ -297,26 +303,22 @@
 
 def layer(grad_out, gate_weights, route_ids, replica_pick, placement, hidden_act, down_proj):
     dp, expert = lax.axis_size(GROUPS), lax.axis_size(EXPERT)
-    depth = lax.axis_size("zl")
     ff = hidden_act.shape[4]
-    local = hidden_act[0].transpose(1, 0, 2, 3).reshape(1, 1, 2, expert * CAP, ff)
-    column = [local] + [
-        lax.ppermute(local, "zl", [(z, (z + d) % depth) for z in range(depth)])
-        for d in range(1, depth)
-    ]
-    column = jnp.concatenate(column, axis=1)
-    hidden = lax.all_gather(column, LINES, axis=0, tiled=True)
-    place = lax.axis_index("zl").astype(jnp.int32).reshape(1)
+    local = hidden_act[0].transpose(1, 0, 2, 3).reshape(1, 2, expert * CAP, ff)
+    column = lax.all_gather(local, "zl", axis=0, tiled=True)
+    column = copied(column)
+    hidden = lax.all_gather(column[None], LINES, axis=0, tiled=True)
     ids, pick, gates = route_ids.T, replica_pick.T, gate_weights.T
     sent = gather_rows(placement, ids, pick, gates, grad_out)
     sent = sent.reshape(dp * expert, 2 * CAP, WIDE)
     rows = lax.all_to_all(sent, EVERY, split_axis=0, concat_axis=0, tiled=True)
     rows = rows.reshape(dp * expert * 2 * CAP, WIDE)
-    parts = gate_parts(place, rows, hidden, down_proj)
+    parts = gate_parts(rows, hidden, down_proj)
     parts = lax.all_to_all(parts, GROUPS, split_axis=0, concat_axis=0, tiled=True)
-    hot, hot_sent, grad = weight_parts(place, rows, hidden)
+    hot, hot_sent = weight_parts(0, rows, hidden)
     half = expert // 2
     other = lax.ppermute(hot_sent, EXPERT, [(e, (e + half) % expert) for e in range(expert)])
+    grad = weight_parts(1, rows, hidden)
     own = gate_totals(parts, expert)
     back = lax.all_to_all(own, EXPERT, split_axis=0, concat_axis=0, tiled=True)
     grad_gate = pick_gates(placement, ids, pick, gates, back).T

time: 266 us -> 278 us (1.045)
  blocking collectives: 60.7 us -> 154 us
  waiting for transfers between devices: 117 us -> 53.2 us
  starting transfers between devices: 40.4 us -> 17.8 us
  Pallas kernels: 27.7 us -> 33.7 us
    all_to_all x1, blocking collectives: 25.6 us -> 119 us  [layer(): rows = lax.all_to_all(sent, EVERY, split_axis=0, concat_axis=0, tiled=True)]
    all_to_all x1, waiting for transfers between devices: 100 us -> 8.37 us  [layer(): back = lax.all_to_all(own, EXPERT, split_axis=0, concat_axis=0, tiled=True)]
    all_gather x1 -> x2, waiting for transfers between devices: 0.01 us -> 44.8 us  [the longest x1 44.8 us: layer(): column = lax.all_gather(local, 'zl', axis=0, tiled=True)]
    ppermute x3 -> x0, waiting for transfers between devices: 17 us -> none  [layer(): lax.ppermute(local, 'zl', [(z, (z + d) % depth) for z in range(depth)])]
    all_to_all x1, starting transfers between devices: 23.4 us -> 11.9 us  [layer(): back = lax.all_to_all(own, EXPERT, split_axis=0, concat_axis=0, tiled=True)]
    ppermute x3 -> x0, starting transfers between devices: 11.2 us -> none  [layer(): lax.ppermute(local, 'zl', [(z, (z + d) % depth) for z in range(depth)])]
    pallas_call x2 -> x4, Pallas kernels: 15.4 us -> 21.4 us  [the longest x2 10.9 us: weight_parts(): pl.pallas_call(hot_kernel if hot else cold_kernel, grid=(steps,), in_spec...]
  transfers between devices with their start and end apart: 6 -> 4, of which waited for: 3 -> 2; matrix products, arithmetic and copies ran while one was open for 0% -> 0% of each run, Pallas kernels for 7% -> 8%
where the time goes in v3:
time: 278 us; the launch traced here: 276 us
  blocking collectives  154 us (55%)
  waiting for transfers between devices  53.2 us (19%)
  Pallas kernels  33.7 us (12%)
  starting transfers between devices  17.8 us (6%)
  between operations  14.1 us (5%)
  local copies, waits for them, and re-layouts  3.17 us (1%)
    all_to_all x1, blocking collectives, layer(): rows = lax.all_to_all(sent, EVERY, split_axis=0, concat_axis=0, tiled=True)  119 us
    all_gather x1, waiting for transfers between devices, layer(): column = lax.all_gather(local, 'zl', axis=0, tiled=True)  44.8 us
    all_to_all x1, blocking collectives, layer(): lax.all_to_all(parts, GROUPS, split_axis=0, concat_axis=0, tiled=True)  35.1 us
    all_to_all x1, starting transfers between devices, layer(): back = lax.all_to_all(own, EXPERT, split_axis=0, concat_axis=0, tiled=True)  11.9 us
    pallas_call x2, Pallas kernels, weight_parts(): pl.pallas_call(hot_kernel if hot else cold_kernel, grid=(steps,), in_spec...  10.9 us
    all_to_all x1, waiting for transfers between devices, layer(): back = lax.all_to_all(own, EXPERT, split_axis=0, concat_axis=0, tiled=True)  8.37 us
    pallas_call x1, Pallas kernels, gate_parts(): pl.pallas_call(gate_kernel, grid=(steps,), in_specs=[pl.BlockSpec((lines...  7.12 us
    pallas_call x1, Pallas kernels, gather_rows(): pl.pallas_call(gather_kernel, grid=(steps,), in_specs=[pl.BlockSpec(memor...  7.03 us
  transfers between devices with their start and end apart: 4, of which 2 were waited for; matrix products, arithmetic and copies ran while one was open for 0% of the time, Pallas kernels for 8%

profile of v3, /device:TPU:1, one launch (start us, length us, event | category | flops | bytes accessed | tf_op | source)
XLA Modules:
  0.0 276.4 jit_solution(9728556411189212025)
XLA Ops:
  7.2 0.0 all-gather.4.cloned.1.call-start
  7.2 1.0 copy.11
  8.3 0.8 reshape.15
  9.0 0.0 all-gather.4.cloned.1.call-update
  9.0 0.0 all-gather.6.cloned.1.call-start
  9.1 44.8 %all-gather.4.cloned.1.call-done.in_ref = bf16[4,2,64,1024]{3,2,1,0:T(8,128)(2,1)} async-done(((bf16[1,2,64,1024]{3,2,1,0:T(8,128)(2,1)}), bf16[4,2,64,1024]{3,2,1,0:T(8,128)(2,1)}) %all-gather.4.cloned.1.call-update) | async-done | bytes 1048592 | tf_op jit(solution)/shard_map/all_gather | solution.py:308
  53.9 3.4 %copied.1 = bf16[4,2,64,1024]{3,2,1,0:T(8,128)(2,1)} custom-call(bf16[4,2,64,1024]{3,2,1,0:T(8,128)(2,1)} %all-gather.4.cloned.1.call-done.in_ref), custom_call_target="tpu_custom_call" | custom-call | tf_op jit(solution)/shard_map/copied/pallas_call | solution.py:218
  57.2 0.0 all-gather.6.cloned.1.call-update
  57.2 7.0 %gather_rows.1 = bf16[32,128,256]{2,1,0:T(8,128)(2,1)} custom-call(s32[32]{0:T(128)} %place_ref.3, s32[8,128]{1,0:T(8,128)} %bitcast.18, s32[8,128]{1,0:T(8,128)} %bitcast.20, f32[8,128]{1,0:T(8,128)} %bitcast.22, bf16[128,7168]{1,0:T(8,128)(2,1)} %grad_ref.1), custom_call_target="tpu_custom_call" | custom-call | flops 234881024 | bytes 3670016 | tf_op jit(solution)/shard_map/gather_rows/pallas_call | solution.py:71
  64.3 119.3 %all_to_all.15 = bf16[512,8,256]{2,1,0:T(8,128)(2,1)} all-to-all(bf16[512,8,256]{2,1,0:T(8,128)(2,1)} %bitcast.16), channel_id=1, replica_groups=mesh['zl'=4,'y'=4,'c'=2,'zh'=4,'x'=4] {'zl','y','c','zh','x'}, dimensions={0} | all-to-all | bytes 4194304 | tf_op jit(solution)/shard_map/all_to_all | solution.py:314
  183.6 0.0 all-gather.6.cloned.1.call-done
  183.6 5.6 %hot_parts.1 = (f32[224,1024]{1,0:T(8,128)}, bf16[224,1024]{1,0:T(8,128)(2,1)}) custom-call(bf16[4096,256]{1,0:T(8,128)(2,1)} %bitcast.13, bf16[8,4,2,64,1024]{4,3,2,1,0:T(8,128)(2,1)} %bitcast.10), custom_call_target="tpu_custom_call" | custom-call | flops 939524096 | bytes 6291456 | tf_op jit(solution)/shard_map/hot_parts/pallas_call | solution.py:191
  189.2 5.8 %collective-permute-start = (bf16[224,1024]{1,0:T(8,128)(2,1)}, bf16[224,1024]{1,0:T(8,128)(2,1)S(1)}, u32[]{:S(2)}, u32[]{:S(2)}) collective-permute-start(bf16[224,1024]{1,0:T(8,128)(2,1)} %get-tuple-element.5), channel_id=1, source_target_pairs={{0,8},{1,9},{2,10},{3,11},{4,12},{5,13},{6,14},{7,15},{8,0},{9,1},... | collective-permute-start | bytes 1376264 | tf_op jit(solution)/shard_map/ppermute | solution.py:320
  195.1 7.1 %gate_parts.1 = f32[32,1,128]{2,1,0:T(1,128)} custom-call(bf16[4096,256]{1,0:T(8,128)(2,1)} %bitcast.14, bf16[8,4,2,64,1024]{4,3,2,1,0:T(8,128)(2,1)} %bitcast.11, bf16[2,224,1024]{2,1,0:T(8,128)(2,1)} %weight_ref.1), custom_call_target="tpu_custom_call" | custom-call | flops 1879048192 | bytes 11403264 | tf_op jit(solution)/shard_map/gate_parts/pallas_call | solution.py:132
  202.2 35.1 %all_to_all.16.parts_ref = f32[32,1,128]{2,1,0:T(1,128)} all-to-all(f32[32,1,128]{2,1,0:T(1,128)} %gate_parts.1), channel_id=1, replica_groups=mesh['zl'=4,'y'=4,'c'=2,'zh'=4,'x'=4] {'zl','y','c'}, dimensions={0} | all-to-all | bytes 32768 | tf_op jit(solution)/shard_map/all_to_all | solution.py:317
  237.3 1.4 gate_totals.1
  238.7 11.9 %all-to-all-start.2 = ((f32[16,1,8]{2,1,0:T(1,128)}), f32[16,1,8]{2,1,0:T(1,128)S(1)}, u32[]{:S(2)}, u32[]{:S(2)}) async-start(f32[16,1,8]{2,1,0:T(1,128)} %gate_totals.1), calls=%async_computation.2 | async-start | bytes 16384 | tf_op jit(solution)/shard_map/all_to_all | solution.py:323
  250.6 5.3 %cold_parts.1.grad_ref = bf16[2,224,1024]{2,1,0:T(8,128)(2,1)} custom-call(bf16[4096,256]{1,0:T(8,128)(2,1)} %bitcast.15, bf16[8,4,2,64,1024]{4,3,2,1,0:T(8,128)(2,1)} %bitcast.12), custom_call_target="tpu_custom_call" | custom-call | flops 939524096 | bytes 6291456 | tf_op jit(solution)/shard_map/cold_parts/pallas_call | solution.py:191
  255.9 8.4 %all-to-all-done.2.back_ref = f32[16,1,8]{2,1,0:T(1,128)S(1)} async-done(((f32[16,1,8]{2,1,0:T(1,128)}), f32[16,1,8]{2,1,0:T(1,128)S(1)}, u32[]{:S(2)}, u32[]{:S(2)}) %all-to-all-start.2) | async-done | bytes 544 | tf_op jit(solution)/shard_map/all_to_all | solution.py:323
  264.3 0.6 copy-done.1
  264.9 1.7 pick_gates.1
  266.6 0.0 collective-permute-done.other_ref
  266.6 0.8 copy-done
  267.4 2.1 pair_sum.1
  (2 shorter events, 0.0 us)
Async XLA Ops:
  7.2 46.7 %all-gather.4.cloned.1.call-start = ((), (), s32[]{:S(2)}) async-start(), calls=%async_computation.3 | async-start | bytes 1310720 | tf_op jit(solution)/shard_map/all_gather | solution.py:308
  9.0 174.6 %all-gather.6.cloned.1.call-start = ((), (), s32[]{:S(2)}) async-start(), calls=%async_computation.4 | async-start | bytes 9437184 | tf_op jit(solution)/shard_map/all_gather | solution.py:310
  189.2 77.4 %collective-permute-start = (bf16[224,1024]{1,0:T(8,128)(2,1)}, bf16[224,1024]{1,0:T(8,128)(2,1)S(1)}, u32[]{:S(2)}, u32[]{:S(2)}) collective-permute-start(bf16[224,1024]{1,0:T(8,128)(2,1)} %get-tuple-element.5), channel_id=1, source_target_pairs={{0,8},{1,9},{2,10},{3,11},{4,12},{5,13},{6,14},{7,15},{8,0},{9,1},... | collective-permute-start | bytes 1376264 | tf_op jit(solution)/shard_map/ppermute | solution.py:320
  238.7 25.6 %all-to-all-start.2 = ((f32[16,1,8]{2,1,0:T(1,128)}), f32[16,1,8]{2,1,0:T(1,128)S(1)}, u32[]{:S(2)}, u32[]{:S(2)}) async-start(f32[16,1,8]{2,1,0:T(1,128)} %gate_totals.1), calls=%async_computation.2 | async-start | bytes 16384 | tf_op jit(solution)/shard_map/all_to_all | solution.py:323
  264.3 0.6 copy-start.1
  266.6 0.8 copy-start
Sparse Core Ops, SparseCore 0:
  10.6 43.1 all-gather.3
  57.4 66.5 all-gather.5

commit v4 on v2

--- a/solution.py
+++ b/solution.py
@@ -104,20 +104,34 @@
     return swap_halves(both[:, 0].reshape(count, WIDE), both[:, 1].reshape(count, WIDE))
 
 
-def gate_kernel(place_ref, rows_ref, hidden_ref, weight_ref, gate_ref):
+def folded_dots(rows, hidden, weight):
+    result = lax.dot_general(hidden, weight, (((1,), (1,)), ((), ())), preferred_element_type=F32)
+    product = result * rows[:, :PIECE]
+    blank = jnp.zeros((rows.shape[0], WIDE - PIECE), F32)
+    return product[:, :128] + jnp.concatenate([product[:, 128:PIECE], blank], axis=1)
+
+
+def add_grad(acc_ref, rows, hidden):
+    grad = lax.dot_general(
+        rows[:, :PIECE].astype(BF16), hidden, (((0,), (0,)), ((), ())), preferred_element_type=F32
+    )
+
+    @pl.when(pl.program_id(0) == 0)
+    def _():
+        acc_ref[...] = grad
+
+    @pl.when(pl.program_id(0) != 0)
+    def _():
+        acc_ref[...] += grad
+
+
+def first_kernel(place_ref, rows_ref, hidden_ref, weight_ref, gate_ref, hot_ref, send_ref, acc_ref):
+    lines, _, span, ff = hidden_ref.shape
+    count = lines * span
     split = instance_rows(rows_ref)
-    count = rows_ref.shape[0] // 2
-    folded = []
-    for i in range(2):
-        hidden = hidden_ref[:, 0, i].reshape(count, hidden_ref.shape[4])
-        result = lax.dot_general(
-            hidden, weight_ref[i], (((1,), (1,)), ((), ())), preferred_element_type=F32
-        )
-        product = result * split[i][:, :PIECE]
-        blank = jnp.zeros((count, WIDE - PIECE), F32)
-        tail = jnp.concatenate([product[:, 128:PIECE], blank], axis=1)
-        folded.append(product[:, :128] + tail)
-    even, odd = swap_halves(*folded)
+    hidden = [hidden_ref[:, i].reshape(count, ff) for i in range(2)]
+    add_grad(acc_ref, split[0], hidden[0])
+    even, odd = swap_halves(*(folded_dots(split[i], hidden[i], weight_ref[i]) for i in range(2)))
     both = jnp.concatenate(
         [even.reshape(count // 8, 1, 8, 128), odd.reshape(count // 8, 1, 8, 128)], axis=1
     )
@@ -125,97 +139,83 @@
     for g in range(count * 2 // 128):
         gate_ref[g] = jnp.sum(both[g].T, axis=0, keepdims=True)
 
-
-def gate_parts(place, rows, hidden, weight):
+    @pl.when(pl.program_id(0) == pl.num_programs(0) - 1)
+    def _():
+        hot_ref[...] = acc_ref[...]
+        send_ref[...] = acc_ref[...].astype(BF16)
+
+
+def first_parts(place, rows, hidden, weight):
     lines, steps, _, span, ff = hidden.shape
     dp = lines * steps
-    return pl.pallas_call(
-        gate_kernel,
+    whole = pl.BlockSpec((PIECE, ff), lambda s, m: (0, 0))
+    return pl.pallas_call(
+        first_kernel,
         grid_spec=pltpu.PrefetchScalarGridSpec(
             num_scalar_prefetch=1,
             grid=(steps,),
             in_specs=[
                 pl.BlockSpec((lines * span * 2, WIDE), lambda s, m: (s, 0)),
                 pl.BlockSpec(
-                    (lines, 1, 2, span, ff),
+                    (lines, None, 2, span, ff),
                     lambda s, m: (0, lax.rem(m[0] - s + steps, steps), 0, 0, 0),
                 ),
                 pl.BlockSpec((2, PIECE, ff), lambda s, m: (0, 0, 0)),
             ],
-            out_specs=pl.BlockSpec((lines, 1, 2 * span), lambda s, m: (s, 0, 0)),
-        ),
-        out_shape=jax.ShapeDtypeStruct((dp, 1, 2 * span), F32),
+            out_specs=[
+                pl.BlockSpec((lines, 1, 2 * span), lambda s, m: (s, 0, 0)),
+                whole,
+                whole,
+            ],
+            scratch_shapes=[pltpu.VMEM((PIECE, ff), F32)],
+        ),
+        out_shape=[
+            jax.ShapeDtypeStruct((dp, 1, 2 * span), F32),
+            jax.ShapeDtypeStruct((PIECE, ff), F32),
+            jax.ShapeDtypeStruct((PIECE, ff), BF16),
+        ],
         cost_estimate=pl.CostEstimate(
-            flops=4 * dp * span * PIECE * ff,
+            flops=6 * dp * span * PIECE * ff,
             bytes_accessed=2 * hidden.size + 2 * rows.size + 2 * weight.size,
             transcendentals=0,
         ),
-        name="gate_parts",
+        name="first_parts",
     )(place, rows, hidden, weight)
 
 
-def grad_kernel(place_ref, rows_ref, hidden_ref, hot_ref, send_ref, out_ref, acc_ref):
-    step = pl.program_id(0)
-    split = instance_rows(rows_ref)
-    count = rows_ref.shape[0] // 2
-    for i in range(2):
-        hidden = hidden_ref[:, 0, i].reshape(count, hidden_ref.shape[4])
-        grad = lax.dot_general(
-            split[i][:, :PIECE].astype(BF16),
-            hidden,
-            (((0,), (0,)), ((), ())),
-            preferred_element_type=F32,
-        )
-
-        @pl.when(step == 0)
-        def _():
-            acc_ref[i] = grad
-
-        @pl.when(step != 0)
-        def _():
-            acc_ref[i] += grad
-
-    @pl.when(step == pl.num_programs(0) - 1)
-    def _():
-        hot_ref[...] = acc_ref[0]
-        send_ref[...] = acc_ref[0].astype(BF16)
-        out_ref[0] = acc_ref[1].astype(BF16)
-
-
-def weight_parts(place, rows, hidden):
+def cold_kernel(place_ref, rows_ref, hidden_ref, out_ref, acc_ref):
+    lines, span, ff = hidden_ref.shape
+    add_grad(acc_ref, instance_rows(rows_ref)[1], hidden_ref[...].reshape(lines * span, ff))
+
+    @pl.when(pl.program_id(0) == pl.num_programs(0) - 1)
+    def _():
+        out_ref[0] = acc_ref[...].astype(BF16)
+
+
+def cold_parts(place, rows, hidden):
     lines, steps, _, span, ff = hidden.shape
-    dp = lines * steps
-    fixed = lambda s, m: (0, 0)
-    return pl.pallas_call(
-        grad_kernel,
+    return pl.pallas_call(
+        cold_kernel,
         grid_spec=pltpu.PrefetchScalarGridSpec(
             num_scalar_prefetch=1,
             grid=(steps,),
             in_specs=[
                 pl.BlockSpec((lines * span * 2, WIDE), lambda s, m: (s, 0)),
                 pl.BlockSpec(
-                    (lines, 1, 2, span, ff),
-                    lambda s, m: (0, lax.rem(m[0] - s + steps, steps), 0, 0, 0),
+                    (lines, None, None, span, ff),
+                    lambda s, m: (0, lax.rem(m[0] - s + steps, steps), 1, 0, 0),
                 ),
             ],
-            out_specs=[
-                pl.BlockSpec((PIECE, ff), fixed),
-                pl.BlockSpec((PIECE, ff), fixed),
-                pl.BlockSpec((1, PIECE, ff), lambda s, m: (1, 0, 0)),
-            ],
-            scratch_shapes=[pltpu.VMEM((2, PIECE, ff), F32)],
-        ),
-        out_shape=[
-            jax.ShapeDtypeStruct((PIECE, ff), F32),
-            jax.ShapeDtypeStruct((PIECE, ff), BF16),
-            jax.ShapeDtypeStruct((2, PIECE, ff), BF16),
-        ],
+            out_specs=pl.BlockSpec((1, PIECE, ff), lambda s, m: (1, 0, 0)),
+            scratch_shapes=[pltpu.VMEM((PIECE, ff), F32)],
+        ),
+        out_shape=jax.ShapeDtypeStruct((2, PIECE, ff), BF16),
         cost_estimate=pl.CostEstimate(
-            flops=4 * dp * span * PIECE * ff,
-            bytes_accessed=2 * hidden.size + 2 * rows.size,
+            flops=2 * lines * steps * span * PIECE * ff,
+            bytes_accessed=hidden.size + 2 * rows.size,
             transcendentals=0,
         ),
-        name="weight_parts",
+        name="cold_parts",
     )(place, rows, hidden)
 
 
@@ -312,11 +312,11 @@
     sent = sent.reshape(dp * expert, 2 * CAP, WIDE)
     rows = lax.all_to_all(sent, EVERY, split_axis=0, concat_axis=0, tiled=True)
     rows = rows.reshape(dp * expert * 2 * CAP, WIDE)
-    parts = gate_parts(place, rows, hidden, down_proj)
+    parts, hot, hot_sent = first_parts(place, rows, hidden, down_proj)
     parts = lax.all_to_all(parts, GROUPS, split_axis=0, concat_axis=0, tiled=True)
-    hot, hot_sent, grad = weight_parts(place, rows, hidden)
     half = expert // 2
     other = lax.ppermute(hot_sent, EXPERT, [(e, (e + half) % expert) for e in range(expert)])
+    grad = cold_parts(place, rows, hidden)
     own = gate_totals(parts, expert)
     back = lax.all_to_all(own, EXPERT, split_axis=0, concat_axis=0, tiled=True)
     grad_gate = pick_gates(placement, ids, pick, gates, back).T

time: 266 us -> 266 us (level)
  blocking collectives: 60.7 us -> 42.2 us
  starting transfers between devices: 40.4 us -> 50.9 us
  waiting for transfers between devices: 117 us -> 126 us
    all_to_all x1 -> x0, blocking collectives: 25.6 us -> none  [layer(): back = lax.all_to_all(own, EXPERT, split_axis=0, concat_axis=0, tiled=True)]
    all_to_all x0 -> x1, starting transfers between devices: none -> 10.4 us  [layer(): back = lax.all_to_all(own, EXPERT, split_axis=0, concat_axis=0, tiled=True)]
    all_to_all x0 -> x1, waiting for transfers between devices: none -> 8.35 us  [layer(): back = lax.all_to_all(own, EXPERT, split_axis=0, concat_axis=0, tiled=True)]
    all_to_all x1, blocking collectives: 35.1 us -> 42.2 us  [layer(): lax.all_to_all(parts, GROUPS, split_axis=0, concat_axis=0, tiled=True)]
  transfers between devices with their start and end apart: 6 -> 7, of which waited for: 3 -> 4; matrix products, arithmetic and copies ran while one was open for 0% -> 0% of each run, Pallas kernels for 7% -> 6%
where the time goes in v4:
time: 266 us; the launch traced here: 265 us
  waiting for transfers between devices  126 us (47%)
  starting transfers between devices  50.9 us (19%)
  blocking collectives  42.2 us (16%)
  Pallas kernels  27 us (10%)
  between operations  14.1 us (5%)
  local copies, waits for them, and re-layouts  3.84 us (1%)
    all_to_all x1, waiting for transfers between devices, layer(): rows = lax.all_to_all(sent, EVERY, split_axis=0, concat_axis=0, tiled=True)  100 us
    all_to_all x1, blocking collectives, layer(): lax.all_to_all(parts, GROUPS, split_axis=0, concat_axis=0, tiled=True)  42.2 us
    all_to_all x1, starting transfers between devices, layer(): rows = lax.all_to_all(sent, EVERY, split_axis=0, concat_axis=0, tiled=True)  23.4 us
    ppermute x3, waiting for transfers between devices, layer(): lax.ppermute(local, 'zl', [(z, (z + d) % depth) for z in range(depth)])  17 us
    ppermute x3, starting transfers between devices, layer(): lax.ppermute(local, 'zl', [(z, (z + d) % depth) for z in range(depth)])  11.2 us
    all_to_all x1, starting transfers between devices, layer(): back = lax.all_to_all(own, EXPERT, split_axis=0, concat_axis=0, tiled=True)  10.4 us
    pallas_call x1, Pallas kernels, first_parts(): pl.pallas_call(first_kernel, grid_spec=pltpu.PrefetchScalarGridSpec(num_s...  9.33 us
    all_to_all x1, waiting for transfers between devices, layer(): back = lax.all_to_all(own, EXPERT, split_axis=0, concat_axis=0, tiled=True)  8.35 us
  transfers between devices with their start and end apart: 7, of which 4 were waited for; matrix products, arithmetic and copies ran while one was open for 0% of the time, Pallas kernels for 6%

profile of v4, /device:TPU:1, one launch (start us, length us, event | category | flops | bytes accessed | tf_op | source)
XLA Modules:
  0.0 264.9 jit_solution(15281196494055291429)
XLA Ops:
  7.2 0.0 all-gather.2.cloned.1.call-start
  7.2 1.0 copy.11
  8.3 0.1 reshape.19
  8.3 7.1 %collective-permute-start.2 = (bf16[1,1,2,64,1024]{4,3,2,1,0:T(8,128)(2,1)S(1)}, bf16[1,1,2,64,1024]{4,3,2,1,0:T(8,128)(2,1)S(1)}, u32[]{:S(2)}, u32[]{:S(2)}) collective-permute-start(bf16[1,1,2,64,1024]{4,3,2,1,0:T(8,128)(2,1)S(1)} %reshape.19), channel_id=1, source_target_pairs={{0,384},{128,0},{256,128},{384,256},{1,385},{129,1},{257,129},{385... | collective-permute-start | bytes 786440 | tf_op jit(solution)/shard_map/ppermute | solution.py:304
  15.4 1.9 collective-permute-start.1
  17.3 2.2 collective-permute-start
  19.5 0.1 collective-permute-done.2
  19.7 16.8 %collective-permute-done.1 = bf16[1,1,2,64,1024]{4,3,2,1,0:T(8,128)(2,1)S(1)} collective-permute-done((bf16[1,1,2,64,1024]{4,3,2,1,0:T(8,128)(2,1)S(1)}, bf16[1,1,2,64,1024]{4,3,2,1,0:T(8,128)(2,1)S(1)}, u32[]{:S(2)}, u32[]{:S(2)}) %collective-permute-start.1) | collective-permute-done | bytes 262176 | tf_op jit(solution)/shard_map/ppermute | solution.py:304
  36.5 1.1 pad_maximum_fusion
  37.6 7.0 %gather_rows.1 = bf16[32,128,256]{2,1,0:T(8,128)(2,1)} custom-call(s32[32]{0:T(128)} %place_ref.3, s32[8,128]{1,0:T(8,128)} %bitcast.14, s32[8,128]{1,0:T(8,128)} %bitcast.16, f32[8,128]{1,0:T(8,128)} %bitcast.18, bf16[128,7168]{1,0:T(8,128)(2,1)} %grad_ref.1), custom_call_target="tpu_custom_call" | custom-call | flops 234881024 | bytes 3670016 | tf_op jit(solution)/shard_map/gather_rows/pallas_call | solution.py:71
  44.7 23.4 %all-to-all-start = ((bf16[512,8,256]{2,1,0:T(8,128)(2,1)}), bf16[512,8,256]{2,1,0:T(8,128)(2,1)S(1)}, u32[]{:S(2)}, u32[]{:S(2)}) async-start(bf16[512,8,256]{2,1,0:T(8,128)(2,1)} %bitcast.12), calls=%async_computation | async-start | bytes 4194304 | tf_op jit(solution)/shard_map/all_to_all | solution.py:313
  68.1 100.5 %all-to-all-done = bf16[512,8,256]{2,1,0:T(8,128)(2,1)S(1)} async-done(((bf16[512,8,256]{2,1,0:T(8,128)(2,1)}), bf16[512,8,256]{2,1,0:T(8,128)(2,1)S(1)}, u32[]{:S(2)}, u32[]{:S(2)}) %all-to-all-start) | async-done | bytes 2097184 | tf_op jit(solution)/shard_map/all_to_all | solution.py:313
  168.5 1.4 copy-done
  169.9 9.3 %first_parts.1 = (f32[32,1,128]{2,1,0:T(1,128)}, f32[224,1024]{1,0:T(8,128)}, bf16[224,1024]{1,0:T(8,128)(2,1)}) custom-call(s32[1]{0:T(128)} %bitcast.place_ref, bf16[4096,256]{1,0:T(8,128)(2,1)} %bitcast.10, bf16[8,4,2,64,1024]{4,3,2,1,0:T(8,128)(2,1)} %all-gather.2.cloned.1.call-done.hidden_ref, bf16[2,224,1024]{2,1,0:T(8,128)(2,1)} %weight_ref.1), custom_call_target="tpu_custom_call" | custom-call | flops 2818572288 | bytes 11403264 | tf_op jit(solution)/shard_map/first_parts/pallas_call | solution.py:152
  179.2 5.8 %collective-permute-start.3 = (bf16[224,1024]{1,0:T(8,128)(2,1)}, bf16[224,1024]{1,0:T(8,128)(2,1)S(1)}, u32[]{:S(2)}, u32[]{:S(2)}) collective-permute-start(bf16[224,1024]{1,0:T(8,128)(2,1)} %get-tuple-element.6), channel_id=1, source_target_pairs={{0,8},{1,9},{2,10},{3,11},{4,12},{5,13},{6,14},{7,15},{8,0},{9,1},... | collective-permute-start | bytes 1376264 | tf_op jit(solution)/shard_map/ppermute | solution.py:318
  185.1 42.2 %all_to_all.15.parts_ref = f32[32,1,128]{2,1,0:T(1,128)} all-to-all(f32[32,1,128]{2,1,0:T(1,128)} %get-tuple-element.7), channel_id=1, replica_groups=mesh['zl'=4,'y'=4,'c'=2,'zh'=4,'x'=4] {'zl','y','c'}, dimensions={0} | all-to-all | bytes 32768 | tf_op jit(solution)/shard_map/all_to_all | solution.py:316
  227.3 1.4 gate_totals.1
  228.7 10.4 %all-to-all-start.2 = ((f32[16,1,8]{2,1,0:T(1,128)}), f32[16,1,8]{2,1,0:T(1,128)S(1)}, u32[]{:S(2)}, u32[]{:S(2)}) async-start(f32[16,1,8]{2,1,0:T(1,128)} %gate_totals.1), calls=%async_computation.2 | async-start | bytes 16384 | tf_op jit(solution)/shard_map/all_to_all | solution.py:321
  239.1 5.3 %cold_parts.1.grad_ref = bf16[2,224,1024]{2,1,0:T(8,128)(2,1)} custom-call(s32[1]{0:T(128)} %bitcast.place_ref, bf16[4096,256]{1,0:T(8,128)(2,1)} %bitcast.11, bf16[8,4,2,64,1024]{4,3,2,1,0:T(8,128)(2,1)} %all-gather.2.cloned.1.call-done.hidden_ref), custom_call_target="tpu_custom_call" | custom-call | flops 939524096 | bytes 6291456 | tf_op jit(solution)/shard_map/cold_parts/pallas_call | solution.py:197
  244.4 8.3 %all-to-all-done.2.back_ref = f32[16,1,8]{2,1,0:T(1,128)S(1)} async-done(((f32[16,1,8]{2,1,0:T(1,128)}), f32[16,1,8]{2,1,0:T(1,128)S(1)}, u32[]{:S(2)}, u32[]{:S(2)}) %all-to-all-start.2) | async-done | bytes 544 | tf_op jit(solution)/shard_map/all_to_all | solution.py:321
  252.8 0.6 copy-done.2
  253.4 1.7 pick_gates.1
  255.1 0.8 copy-done.1
  255.9 2.1 pair_sum.1
  (7 shorter events, 0.0 us)
Async XLA Ops:
  7.2 161.4 %all-gather.2.cloned.1.call-start = ((), (), s32[]{:S(2)}) async-start(), calls=%async_computation.3 | async-start | bytes 9437184 | tf_op jit(solution)/shard_map/all_gather | solution.py:308
  8.3 11.4 %collective-permute-start.2 = (bf16[1,1,2,64,1024]{4,3,2,1,0:T(8,128)(2,1)S(1)}, bf16[1,1,2,64,1024]{4,3,2,1,0:T(8,128)(2,1)S(1)}, u32[]{:S(2)}, u32[]{:S(2)}) collective-permute-start(bf16[1,1,2,64,1024]{4,3,2,1,0:T(8,128)(2,1)S(1)} %reshape.19), channel_id=1, source_target_pairs={{0,384},{128,0},{256,128},{384,256},{1,385},{129,1},{257,129},{385... | collective-permute-start | bytes 786440 | tf_op jit(solution)/shard_map/ppermute | solution.py:304
  15.4 21.1 %collective-permute-start.1 = (bf16[1,1,2,64,1024]{4,3,2,1,0:T(8,128)(2,1)S(1)}, bf16[1,1,2,64,1024]{4,3,2,1,0:T(8,128)(2,1)S(1)}, u32[]{:S(2)}, u32[]{:S(2)}) collective-permute-start(bf16[1,1,2,64,1024]{4,3,2,1,0:T(8,128)(2,1)S(1)} %reshape.19), channel_id=1, source_target_pairs={{0,256},{128,384},{256,0},{384,128},{1,257},{129,385},{257,1},{385... | collective-permute-start | bytes 786440 | tf_op jit(solution)/shard_map/ppermute | solution.py:304
  17.3 19.2 %collective-permute-start = (bf16[1,1,2,64,1024]{4,3,2,1,0:T(8,128)(2,1)S(1)}, bf16[1,1,2,64,1024]{4,3,2,1,0:T(8,128)(2,1)S(1)}, u32[]{:S(2)}, u32[]{:S(2)}) collective-permute-start(bf16[1,1,2,64,1024]{4,3,2,1,0:T(8,128)(2,1)S(1)} %reshape.19), channel_id=1, source_target_pairs={{0,128},{128,256},{256,384},{384,0},{1,129},{129,257},{257,385},{3... | collective-permute-start | bytes 786440 | tf_op jit(solution)/shard_map/ppermute | solution.py:304
  44.7 123.9 %all-to-all-start = ((bf16[512,8,256]{2,1,0:T(8,128)(2,1)}), bf16[512,8,256]{2,1,0:T(8,128)(2,1)S(1)}, u32[]{:S(2)}, u32[]{:S(2)}) async-start(bf16[512,8,256]{2,1,0:T(8,128)(2,1)} %bitcast.12), calls=%async_computation | async-start | bytes 4194304 | tf_op jit(solution)/shard_map/all_to_all | solution.py:313
  168.5 1.4 copy-start
  179.2 75.9 %collective-permute-start.3 = (bf16[224,1024]{1,0:T(8,128)(2,1)}, bf16[224,1024]{1,0:T(8,128)(2,1)S(1)}, u32[]{:S(2)}, u32[]{:S(2)}) collective-permute-start(bf16[224,1024]{1,0:T(8,128)(2,1)} %get-tuple-element.6), channel_id=1, source_target_pairs={{0,8},{1,9},{2,10},{3,11},{4,12},{5,13},{6,14},{7,15},{8,0},{9,1},... | collective-permute-start | bytes 1376264 | tf_op jit(solution)/shard_map/ppermute | solution.py:318
  228.7 24.1 %all-to-all-start.2 = ((f32[16,1,8]{2,1,0:T(1,128)}), f32[16,1,8]{2,1,0:T(1,128)S(1)}, u32[]{:S(2)}, u32[]{:S(2)}) async-start(f32[16,1,8]{2,1,0:T(1,128)} %gate_totals.1), calls=%async_computation.2 | async-start | bytes 16384 | tf_op jit(solution)/shard_map/all_to_all | solution.py:321
  252.8 0.6 copy-start.2
  255.1 0.8 copy-start.1
Sparse Core Ops, SparseCore 0:
  37.8 71.1 all-gather.1

commit v5 on v4

--- a/solution.py
+++ b/solution.py
@@ -98,9 +98,21 @@
     )
 
 
-def instance_rows(rows_ref):
+def piece_lines(place_ref):
+    lines = []
+    for other in range(2):
+        for d in range(4):
+            y = lax.rem(place_ref[1] - d + 4, 4)
+            core = place_ref[2] if other == 0 else 1 - place_ref[2]
+            lines.append(y * 2 + core)
+    return lines
+
+
+def instance_rows(rows_ref, lines):
+    span = rows_ref.shape[0] // len(lines)
+    rows = [rows_ref[pl.ds(pl.multiple_of(n * span, span), span), :].astype(F32) for n in lines]
     count = rows_ref.shape[0] // 2
-    both = rows_ref[...].astype(F32).reshape(count // 8, 2, 8, WIDE)
+    both = jnp.concatenate(rows, axis=0).reshape(count // 8, 2, 8, WIDE)
     return swap_halves(both[:, 0].reshape(count, WIDE), both[:, 1].reshape(count, WIDE))
 
 
@@ -125,19 +137,20 @@
         acc_ref[...] += grad
 
 
-def first_kernel(place_ref, rows_ref, hidden_ref, weight_ref, gate_ref, hot_ref, send_ref, acc_ref):
-    lines, _, span, ff = hidden_ref.shape
-    count = lines * span
-    split = instance_rows(rows_ref)
-    hidden = [hidden_ref[:, i].reshape(count, ff) for i in range(2)]
+def first_kernel(place_ref, rows_ref, weight_ref, *refs):
+    pieces, (gate_ref, hot_ref, send_ref, acc_ref) = refs[:-4], refs[-4:]
+    lines = piece_lines(place_ref)
+    split = instance_rows(rows_ref, lines)
+    count = rows_ref.shape[0] // 2
+    hidden = [jnp.concatenate([piece[i] for piece in pieces], axis=0) for i in range(2)]
     add_grad(acc_ref, split[0], hidden[0])
     even, odd = swap_halves(*(folded_dots(split[i], hidden[i], weight_ref[i]) for i in range(2)))
     both = jnp.concatenate(
         [even.reshape(count // 8, 1, 8, 128), odd.reshape(count // 8, 1, 8, 128)], axis=1
     )
     both = both.reshape(count * 2 // 128, 128, 128)
-    for g in range(count * 2 // 128):
-        gate_ref[g] = jnp.sum(both[g].T, axis=0, keepdims=True)
+    for g, line in enumerate(lines):
+        gate_ref[line] = jnp.sum(both[g].T, axis=0, keepdims=True)
 
     @pl.when(pl.program_id(0) == pl.num_programs(0) - 1)
     def _():
@@ -145,8 +158,13 @@
         send_ref[...] = acc_ref[...].astype(BF16)
 
 
-def first_parts(place, rows, hidden, weight):
-    lines, steps, _, span, ff = hidden.shape
+def piece_index(s, m, instance):
+    return (lax.rem(m[0] - s + 4, 4), instance, 0, 0)
+
+
+def first_parts(place, rows, pieces, weight):
+    steps, _, span, ff = pieces[0].shape
+    lines = len(pieces)
     dp = lines * steps
     whole = pl.BlockSpec((PIECE, ff), lambda s, m: (0, 0))
     return pl.pallas_call(
@@ -156,12 +174,9 @@
             grid=(steps,),
             in_specs=[
                 pl.BlockSpec((lines * span * 2, WIDE), lambda s, m: (s, 0)),
-                pl.BlockSpec(
-                    (lines, None, 2, span, ff),
-                    lambda s, m: (0, lax.rem(m[0] - s + steps, steps), 0, 0, 0),
-                ),
                 pl.BlockSpec((2, PIECE, ff), lambda s, m: (0, 0, 0)),
-            ],
+            ]
+            + [pl.BlockSpec((None, 2, span, ff), lambda s, m: piece_index(s, m, 0))] * lines,
             out_specs=[
                 pl.BlockSpec((lines, 1, 2 * span), lambda s, m: (s, 0, 0)),
                 whole,
@@ -176,47 +191,44 @@
         ],
         cost_estimate=pl.CostEstimate(
             flops=6 * dp * span * PIECE * ff,
-            bytes_accessed=2 * hidden.size + 2 * rows.size + 2 * weight.size,
+            bytes_accessed=4 * dp * span * ff + 2 * rows.size + 2 * weight.size,
             transcendentals=0,
         ),
         name="first_parts",
-    )(place, rows, hidden, weight)
-
-
-def cold_kernel(place_ref, rows_ref, hidden_ref, out_ref, acc_ref):
-    lines, span, ff = hidden_ref.shape
-    add_grad(acc_ref, instance_rows(rows_ref)[1], hidden_ref[...].reshape(lines * span, ff))
+    )(place, rows, weight, *pieces)
+
+
+def cold_kernel(place_ref, rows_ref, *refs):
+    pieces, (out_ref, acc_ref) = refs[:-2], refs[-2:]
+    hidden = jnp.concatenate([piece[...] for piece in pieces], axis=0)
+    add_grad(acc_ref, instance_rows(rows_ref, piece_lines(place_ref))[1], hidden)
 
     @pl.when(pl.program_id(0) == pl.num_programs(0) - 1)
     def _():
         out_ref[0] = acc_ref[...].astype(BF16)
 
 
-def cold_parts(place, rows, hidden):
-    lines, steps, _, span, ff = hidden.shape
+def cold_parts(place, rows, pieces):
+    steps, _, span, ff = pieces[0].shape
+    lines = len(pieces)
     return pl.pallas_call(
         cold_kernel,
         grid_spec=pltpu.PrefetchScalarGridSpec(
             num_scalar_prefetch=1,
             grid=(steps,),
-            in_specs=[
-                pl.BlockSpec((lines * span * 2, WIDE), lambda s, m: (s, 0)),
-                pl.BlockSpec(
-                    (lines, None, None, span, ff),
-                    lambda s, m: (0, lax.rem(m[0] - s + steps, steps), 1, 0, 0),
-                ),
-            ],
+            in_specs=[pl.BlockSpec((lines * span * 2, WIDE), lambda s, m: (s, 0))]
+            + [pl.BlockSpec((None, None, span, ff), lambda s, m: piece_index(s, m, 1))] * lines,
             out_specs=pl.BlockSpec((1, PIECE, ff), lambda s, m: (1, 0, 0)),
             scratch_shapes=[pltpu.VMEM((PIECE, ff), F32)],
         ),
         out_shape=jax.ShapeDtypeStruct((2, PIECE, ff), BF16),
         cost_estimate=pl.CostEstimate(
             flops=2 * lines * steps * span * PIECE * ff,
-            bytes_accessed=hidden.size + 2 * rows.size,
+            bytes_accessed=2 * lines * steps * span * ff + 2 * rows.size,
             transcendentals=0,
         ),
         name="cold_parts",
-    )(place, rows, hidden)
+    )(place, rows, *pieces)
 
 
 def pair_kernel(hot_ref, other_ref, grad_ref, out_ref):
@@ -299,24 +311,27 @@
     dp, expert = lax.axis_size(GROUPS), lax.axis_size(EXPERT)
     depth = lax.axis_size("zl")
     ff = hidden_act.shape[4]
-    local = hidden_act[0].transpose(1, 0, 2, 3).reshape(1, 1, 2, expert * CAP, ff)
+    local = hidden_act[0].transpose(1, 0, 2, 3).reshape(1, 2, expert * CAP, ff)
     column = [local] + [
         lax.ppermute(local, "zl", [(z, (z + d) % depth) for z in range(depth)])
         for d in range(1, depth)
     ]
-    column = jnp.concatenate(column, axis=1)
-    hidden = lax.all_gather(column, LINES, axis=0, tiled=True)
-    place = lax.axis_index("zl").astype(jnp.int32).reshape(1)
+    column = jnp.concatenate(column, axis=0)
+    pieces = [column]
+    for d in range(1, lax.axis_size("y")):
+        pieces.append(lax.ppermute(column, "y", [(y, (y + d) % 4) for y in range(4)]))
+    pieces = pieces + [lax.ppermute(piece, "c", [(0, 1), (1, 0)]) for piece in pieces]
+    place = jnp.stack([lax.axis_index(axis) for axis in GROUPS]).astype(jnp.int32)
     ids, pick, gates = route_ids.T, replica_pick.T, gate_weights.T
     sent = gather_rows(placement, ids, pick, gates, grad_out)
     sent = sent.reshape(dp * expert, 2 * CAP, WIDE)
     rows = lax.all_to_all(sent, EVERY, split_axis=0, concat_axis=0, tiled=True)
     rows = rows.reshape(dp * expert * 2 * CAP, WIDE)
-    parts, hot, hot_sent = first_parts(place, rows, hidden, down_proj)
+    parts, hot, hot_sent = first_parts(place, rows, pieces, down_proj)
     parts = lax.all_to_all(parts, GROUPS, split_axis=0, concat_axis=0, tiled=True)
     half = expert // 2
     other = lax.ppermute(hot_sent, EXPERT, [(e, (e + half) % expert) for e in range(expert)])
-    grad = cold_parts(place, rows, hidden)
+    grad = cold_parts(place, rows, pieces)
     own = gate_totals(parts, expert)
     back = lax.all_to_all(own, EXPERT, split_axis=0, concat_axis=0, tiled=True)
     grad_gate = pick_gates(placement, ids, pick, gates, back).T

time: 266 us -> 298 us (1.12)
  starting transfers between devices: 50.9 us -> 96.2 us
  between operations: 14.1 us -> 0.82 us
  waiting for transfers between devices: 126 us -> 119 us
  blocking collectives: 42.2 us -> 48.5 us
    all_to_all x1, waiting for transfers between devices: 100 us -> 0.01 us  [layer(): rows = lax.all_to_all(sent, EVERY, split_axis=0, concat_axis=0, tiled=True)]
    ppermute x3, waiting for transfers between devices: 17 us -> 95.4 us  [layer(): lax.ppermute(local, 'zl', [(z, (z + d) % depth) for z in range(depth)])]
    ppermute x0 -> x7, starting transfers between devices: none -> 43.8 us  [the longest x4 34.4 us: layer(): lax.ppermute(piece, 'c', [(0, 1), (1, 0)])]
    ppermute x0 -> x7, waiting for transfers between devices: none -> 16 us  [the longest x3 14.1 us: layer(): lax.ppermute(column, 'y', [(y, (y + d) % 4) for y in range(4)])]
    all_to_all x1, blocking collectives: 42.2 us -> 48.5 us  [layer(): lax.all_to_all(parts, GROUPS, split_axis=0, concat_axis=0, tiled=True)]
    ppermute x1, starting transfers between devices: 5.83 us -> 12 us  [layer(): lax.ppermute(hot_sent, EXPERT, [(e, (e + half) % expert) for e in range(e...]
    all_to_all x1, starting transfers between devices: 10.4 us -> 5.34 us  [layer(): back = lax.all_to_all(own, EXPERT, split_axis=0, concat_axis=0, tiled=True)]
  transfers between devices with their start and end apart: 7 -> 13, of which waited for: 4 -> 6; matrix products, arithmetic and copies ran while one was open for 0% -> 0% of each run, Pallas kernels for 6% -> 3%
where the time goes in v5:
time: 298 us; the launch traced here: 297 us
  waiting for transfers between devices  119 us (40%)
  starting transfers between devices  96.2 us (32%)
  blocking collectives  48.5 us (16%)
  Pallas kernels  28.7 us (10%)
    ppermute x3, waiting for transfers between devices, layer(): lax.ppermute(local, 'zl', [(z, (z + d) % depth) for z in range(depth)])  95.4 us
    all_to_all x1, blocking collectives, layer(): lax.all_to_all(parts, GROUPS, split_axis=0, concat_axis=0, tiled=True)  48.5 us
    ppermute x4, starting transfers between devices, layer(): lax.ppermute(piece, 'c', [(0, 1), (1, 0)])  34.4 us
    all_to_all x1, starting transfers between devices, layer(): rows = lax.all_to_all(sent, EVERY, split_axis=0, concat_axis=0, tiled=True)  24.3 us
    ppermute x3, waiting for transfers between devices, layer(): lax.ppermute(column, 'y', [(y, (y + d) % 4) for y in range(4)])  14.1 us
    ppermute x1, starting transfers between devices, layer(): lax.ppermute(hot_sent, EXPERT, [(e, (e + half) % expert) for e in range(e...  12 us
    ppermute x3, starting transfers between devices, layer(): lax.ppermute(local, 'zl', [(z, (z + d) % depth) for z in range(depth)])  10.7 us
    pallas_call x1, Pallas kernels, first_parts(): pl.pallas_call(first_kernel, grid_spec=pltpu.PrefetchScalarGridSpec(num_s...  10.1 us
  transfers between devices with their start and end apart: 13, of which 6 were waited for; matrix products, arithmetic and copies ran while one was open for 0% of the time, Pallas kernels for 3%

profile of v5, /device:TPU:1, one launch (start us, length us, event | category | flops | bytes accessed | tf_op | source)
XLA Modules:
  0.0 296.6 jit_solution(16372287115274230544)
XLA Ops:
  0.6 7.0 %gather_rows.1 = bf16[32,128,256]{2,1,0:T(8,128)(2,1)} custom-call(s32[32]{0:T(128)} %place_ref.3, s32[8,128]{1,0:T(8,128)} %bitcast.16, s32[8,128]{1,0:T(8,128)} %bitcast.18, f32[8,128]{1,0:T(8,128)} %bitcast.20, bf16[128,7168]{1,0:T(8,128)(2,1)} %grad_ref.1), custom_call_target="tpu_custom_call" | custom-call | flops 234881024 | bytes 3670016 | tf_op jit(solution)/shard_map/gather_rows/pallas_call | solution.py:71
  7.6 24.3 %all-to-all-start = ((bf16[512,8,256]{2,1,0:T(8,128)(2,1)}), bf16[512,8,256]{2,1,0:T(8,128)(2,1)S(1)}, u32[]{:S(2)}, u32[]{:S(2)}) async-start(bf16[512,8,256]{2,1,0:T(8,128)(2,1)} %bitcast.14), calls=%async_computation | async-start | bytes 4194304 | tf_op jit(solution)/shard_map/all_to_all | solution.py:328
  32.1 3.4 %collective-permute-start = (bf16[1,2,64,1024]{3,2,1,0:T(8,128)(2,1)S(1)}, bf16[1,2,64,1024]{3,2,1,0:T(8,128)(2,1)S(1)}, u32[]{:S(2)}, u32[]{:S(2)}) collective-permute-start(bf16[1,2,64,1024]{3,2,1,0:T(8,128)(2,1)S(1)} %reshape.15), channel_id=1, source_target_pairs={{0,128},{128,256},{256,384},{384,0},{1,129},{129,257},{257,385},{3... | collective-permute-start | bytes 786440 | tf_op jit(solution)/shard_map/ppermute | solution.py:316
  35.5 4.5 %collective-permute-start.1 = (bf16[1,2,64,1024]{3,2,1,0:T(8,128)(2,1)S(1)}, bf16[1,2,64,1024]{3,2,1,0:T(8,128)(2,1)S(1)}, u32[]{:S(2)}, u32[]{:S(2)}) collective-permute-start(bf16[1,2,64,1024]{3,2,1,0:T(8,128)(2,1)S(1)} %reshape.15), channel_id=1, source_target_pairs={{0,256},{128,384},{256,0},{384,128},{1,257},{129,385},{257,1},{385... | collective-permute-start | bytes 786440 | tf_op jit(solution)/shard_map/ppermute | solution.py:316
  40.1 2.8 collective-permute-start.2
  42.9 84.9 %collective-permute-done = bf16[1,2,64,1024]{3,2,1,0:T(8,128)(2,1)S(1)} collective-permute-done((bf16[1,2,64,1024]{3,2,1,0:T(8,128)(2,1)S(1)}, bf16[1,2,64,1024]{3,2,1,0:T(8,128)(2,1)S(1)}, u32[]{:S(2)}, u32[]{:S(2)}) %collective-permute-start) | collective-permute-done | bytes 262176 | tf_op jit(solution)/shard_map/ppermute | solution.py:316
  127.8 10.5 %collective-permute-done.1 = bf16[1,2,64,1024]{3,2,1,0:T(8,128)(2,1)S(1)} collective-permute-done((bf16[1,2,64,1024]{3,2,1,0:T(8,128)(2,1)S(1)}, bf16[1,2,64,1024]{3,2,1,0:T(8,128)(2,1)S(1)}, u32[]{:S(2)}, u32[]{:S(2)}) %collective-permute-start.1) | collective-permute-done | bytes 262176 | tf_op jit(solution)/shard_map/ppermute | solution.py:316
  138.4 4.5 %collective-permute-start.5 = (bf16[4,2,64,1024]{3,2,1,0:T(8,128)(2,1)S(1)}, bf16[4,2,64,1024]{3,2,1,0:T(8,128)(2,1)}, u32[]{:S(2)}, u32[]{:S(2)}) collective-permute-start(bf16[4,2,64,1024]{3,2,1,0:T(8,128)(2,1)S(1)} %constant_dynamic-update-slice_fusion.refs_0_), channel_id=1, source_target_pairs={{0,96},{32,0},{64,32},{96,64},{1,97},{33,1},{65,33},{97,65},{2,98}... | collective-permute-start | bytes 3145736 | tf_op jit(solution)/shard_map/ppermute | solution.py:322
  142.9 2.4 collective-permute-start.4
  145.2 2.6 collective-permute-start.3
  147.8 4.3 %collective-permute-start.6 = (bf16[4,2,64,1024]{3,2,1,0:T(8,128)(2,1)S(1)}, bf16[4,2,64,1024]{3,2,1,0:T(8,128)(2,1)}, u32[]{:S(2)}, u32[]{:S(2)}) collective-permute-start(bf16[4,2,64,1024]{3,2,1,0:T(8,128)(2,1)S(1)} %constant_dynamic-update-slice_fusion.refs_0_), channel_id=1, source_target_pairs={{0,16},{16,0},{1,17},{17,1},{2,18},{18,2},{3,19},{19,3},{4,20},{20... | collective-permute-start | bytes 3145736 | tf_op jit(solution)/shard_map/ppermute | solution.py:323
  152.1 12.7 %collective-permute-done.5.refs_3_ = bf16[4,2,64,1024]{3,2,1,0:T(8,128)(2,1)} collective-permute-done((bf16[4,2,64,1024]{3,2,1,0:T(8,128)(2,1)S(1)}, bf16[4,2,64,1024]{3,2,1,0:T(8,128)(2,1)}, u32[]{:S(2)}, u32[]{:S(2)}) %collective-permute-start.5) | collective-permute-done | bytes 1048608 | tf_op jit(solution)/shard_map/ppermute | solution.py:322
  164.8 25.8 %collective-permute-start.9 = (bf16[4,2,64,1024]{3,2,1,0:T(8,128)(2,1)}, bf16[4,2,64,1024]{3,2,1,0:T(8,128)(2,1)}, u32[]{:S(2)}, u32[]{:S(2)}) collective-permute-start(bf16[4,2,64,1024]{3,2,1,0:T(8,128)(2,1)} %collective-permute-done.5.refs_3_), channel_id=1, source_target_pairs={{0,16},{16,0},{1,17},{17,1},{2,18},{18,2},{3,19},{19,3},{4,20},{20... | collective-permute-start | bytes 3145736 | tf_op jit(solution)/shard_map/ppermute | solution.py:323
  190.6 1.9 collective-permute-start.8
  193.9 2.4 collective-permute-start.7
  197.0 1.9 collective-permute-done.7.refs_5_
  200.3 10.1 %first_parts.1 = (f32[32,1,128]{2,1,0:T(1,128)}, f32[224,1024]{1,0:T(8,128)}, bf16[224,1024]{1,0:T(8,128)(2,1)}) custom-call(s32[3]{0:T(128)} %pad_add_fusion.place_ref, bf16[4096,256]{1,0:T(8,128)(2,1)} %bitcast.12, bf16[2,224,1024]{2,1,0:T(8,128)(2,1)} %weight_ref.1, bf16[4,2,64,1024]{3,2,1,0:T(8,128)(2,1)} %copy-done.1, ...), custom_call_target="tpu_custom_call" | custom-call | flops 2818572288 | bytes 11403264 | tf_op jit(solution)/shard_map/first_parts/pallas_call | solution.py:170
  210.4 12.0 %collective-permute-start.10 = (bf16[224,1024]{1,0:T(8,128)(2,1)}, bf16[224,1024]{1,0:T(8,128)(2,1)S(1)}, u32[]{:S(2)}, u32[]{:S(2)}) collective-permute-start(bf16[224,1024]{1,0:T(8,128)(2,1)} %get-tuple-element.6), channel_id=1, source_target_pairs={{0,8},{1,9},{2,10},{3,11},{4,12},{5,13},{6,14},{7,15},{8,0},{9,1},... | collective-permute-start | bytes 1376264 | tf_op jit(solution)/shard_map/ppermute | solution.py:333
  222.4 48.5 %all_to_all.15.parts_ref = f32[32,1,128]{2,1,0:T(1,128)} all-to-all(f32[32,1,128]{2,1,0:T(1,128)} %get-tuple-element.7), channel_id=1, replica_groups=mesh['zl'=4,'y'=4,'c'=2,'zh'=4,'x'=4] {'zl','y','c'}, dimensions={0} | all-to-all | bytes 32768 | tf_op jit(solution)/shard_map/all_to_all | solution.py:331
  272.3 5.3 %all-to-all-start.2 = ((f32[16,1,8]{2,1,0:T(1,128)}), f32[16,1,8]{2,1,0:T(1,128)S(1)}, u32[]{:S(2)}, u32[]{:S(2)}) async-start(f32[16,1,8]{2,1,0:T(1,128)} %gate_totals.1), calls=%async_computation.2 | async-start | bytes 16384 | tf_op jit(solution)/shard_map/all_to_all | solution.py:336
  277.6 6.2 %cold_parts.1.grad_ref = bf16[2,224,1024]{2,1,0:T(8,128)(2,1)} custom-call(s32[3]{0:T(128)} %pad_add_fusion.place_ref, bf16[4096,256]{1,0:T(8,128)(2,1)} %bitcast.13, bf16[4,2,64,1024]{3,2,1,0:T(8,128)(2,1)} %copy-done.1, bf16[4,2,64,1024]{3,2,1,0:T(8,128)(2,1)} %collective-permute-done.3.refs_1_, bf16[4,2,64,1024]{3,2,1,0:T(8,128)(2,1)} %collective-permute-done.4.refs_2_, ...), custom_call_target="tpu_custom_call" | custom-call | flops 939524096 | bytes 6291456 | tf_op jit(solution)/shard_map/cold_parts/pallas_call | solution.py:214
  283.9 7.4 %all-to-all-done.2.back_ref = f32[16,1,8]{2,1,0:T(1,128)S(1)} async-done(((f32[16,1,8]{2,1,0:T(1,128)}), f32[16,1,8]{2,1,0:T(1,128)S(1)}, u32[]{:S(2)}, u32[]{:S(2)}) %all-to-all-start.2) | async-done | bytes 544 | tf_op jit(solution)/shard_map/all_to_all | solution.py:336
  291.9 1.7 pick_gates.1
  294.4 2.1 pair_sum.1
  (26 shorter events, 6.4 us)
Async XLA Ops:
  7.6 24.3 %copy-start.3 = (bf16[1,16,2,4,1024]{4,3,2,1,0:T(4,128)(2,1)S(1)}, bf16[1,16,2,4,1024]{4,3,2,1,0:T(4,128)(2,1)}, u32[]{:S(2)}) copy-start(bf16[1,16,2,4,1024]{4,3,2,1,0:T(4,128)(2,1)} %param.12) | copy-start | bytes 786436
  7.6 191.3 %all-to-all-start = ((bf16[512,8,256]{2,1,0:T(8,128)(2,1)}), bf16[512,8,256]{2,1,0:T(8,128)(2,1)S(1)}, u32[]{:S(2)}, u32[]{:S(2)}) async-start(bf16[512,8,256]{2,1,0:T(8,128)(2,1)} %bitcast.14), calls=%async_computation | async-start | bytes 4194304 | tf_op jit(solution)/shard_map/all_to_all | solution.py:328
  32.1 95.7 %collective-permute-start = (bf16[1,2,64,1024]{3,2,1,0:T(8,128)(2,1)S(1)}, bf16[1,2,64,1024]{3,2,1,0:T(8,128)(2,1)S(1)}, u32[]{:S(2)}, u32[]{:S(2)}) collective-permute-start(bf16[1,2,64,1024]{3,2,1,0:T(8,128)(2,1)S(1)} %reshape.15), channel_id=1, source_target_pairs={{0,128},{128,256},{256,384},{384,0},{1,129},{129,257},{257,385},{3... | collective-permute-start | bytes 786440 | tf_op jit(solution)/shard_map/ppermute | solution.py:316
  35.5 102.8 %collective-permute-start.1 = (bf16[1,2,64,1024]{3,2,1,0:T(8,128)(2,1)S(1)}, bf16[1,2,64,1024]{3,2,1,0:T(8,128)(2,1)S(1)}, u32[]{:S(2)}, u32[]{:S(2)}) collective-permute-start(bf16[1,2,64,1024]{3,2,1,0:T(8,128)(2,1)S(1)} %reshape.15), channel_id=1, source_target_pairs={{0,256},{128,384},{256,0},{384,128},{1,257},{129,385},{257,1},{385... | collective-permute-start | bytes 786440 | tf_op jit(solution)/shard_map/ppermute | solution.py:316
  40.1 98.3 %collective-permute-start.2 = (bf16[1,2,64,1024]{3,2,1,0:T(8,128)(2,1)S(1)}, bf16[1,2,64,1024]{3,2,1,0:T(8,128)(2,1)S(1)}, u32[]{:S(2)}, u32[]{:S(2)}) collective-permute-start(bf16[1,2,64,1024]{3,2,1,0:T(8,128)(2,1)S(1)} %reshape.15), channel_id=1, source_target_pairs={{0,384},{128,0},{256,128},{384,256},{1,385},{129,1},{257,129},{385... | collective-permute-start | bytes 786440 | tf_op jit(solution)/shard_map/ppermute | solution.py:316
  138.4 60.6 %copy-start.1 = (bf16[4,2,64,1024]{3,2,1,0:T(8,128)(2,1)}, bf16[4,2,64,1024]{3,2,1,0:T(8,128)(2,1)S(1)}, u32[]{:S(2)}) copy-start(bf16[4,2,64,1024]{3,2,1,0:T(8,128)(2,1)S(1)} %constant_dynamic-update-slice_fusion.refs_0_) | copy-start | bytes 3145732
  138.4 26.4 %collective-permute-start.5 = (bf16[4,2,64,1024]{3,2,1,0:T(8,128)(2,1)S(1)}, bf16[4,2,64,1024]{3,2,1,0:T(8,128)(2,1)}, u32[]{:S(2)}, u32[]{:S(2)}) collective-permute-start(bf16[4,2,64,1024]{3,2,1,0:T(8,128)(2,1)S(1)} %constant_dynamic-update-slice_fusion.refs_0_), channel_id=1, source_target_pairs={{0,96},{32,0},{64,32},{96,64},{1,97},{33,1},{65,33},{97,65},{2,98}... | collective-permute-start | bytes 3145736 | tf_op jit(solution)/shard_map/ppermute | solution.py:322
  142.9 47.7 %collective-permute-start.4 = (bf16[4,2,64,1024]{3,2,1,0:T(8,128)(2,1)S(1)}, bf16[4,2,64,1024]{3,2,1,0:T(8,128)(2,1)}, u32[]{:S(2)}, u32[]{:S(2)}) collective-permute-start(bf16[4,2,64,1024]{3,2,1,0:T(8,128)(2,1)S(1)} %constant_dynamic-update-slice_fusion.refs_0_), channel_id=1, source_target_pairs={{0,64},{32,96},{64,0},{96,32},{1,65},{33,97},{65,1},{97,33},{2,66}... | collective-permute-start | bytes 3145736 | tf_op jit(solution)/shard_map/ppermute | solution.py:322
  145.2 48.7 %collective-permute-start.3 = (bf16[4,2,64,1024]{3,2,1,0:T(8,128)(2,1)S(1)}, bf16[4,2,64,1024]{3,2,1,0:T(8,128)(2,1)}, u32[]{:S(2)}, u32[]{:S(2)}) collective-permute-start(bf16[4,2,64,1024]{3,2,1,0:T(8,128)(2,1)S(1)} %constant_dynamic-update-slice_fusion.refs_0_), channel_id=1, source_target_pairs={{0,32},{32,64},{64,96},{96,0},{1,33},{33,65},{65,97},{97,1},{2,34}... | collective-permute-start | bytes 3145736 | tf_op jit(solution)/shard_map/ppermute | solution.py:322
  147.8 49.2 %collective-permute-start.6 = (bf16[4,2,64,1024]{3,2,1,0:T(8,128)(2,1)S(1)}, bf16[4,2,64,1024]{3,2,1,0:T(8,128)(2,1)}, u32[]{:S(2)}, u32[]{:S(2)}) collective-permute-start(bf16[4,2,64,1024]{3,2,1,0:T(8,128)(2,1)S(1)} %constant_dynamic-update-slice_fusion.refs_0_), channel_id=1, source_target_pairs={{0,16},{16,0},{1,17},{17,1},{2,18},{18,2},{3,19},{19,3},{4,20},{20... | collective-permute-start | bytes 3145736 | tf_op jit(solution)/shard_map/ppermute | solution.py:323
  164.8 32.3 %collective-permute-start.9 = (bf16[4,2,64,1024]{3,2,1,0:T(8,128)(2,1)}, bf16[4,2,64,1024]{3,2,1,0:T(8,128)(2,1)}, u32[]{:S(2)}, u32[]{:S(2)}) collective-permute-start(bf16[4,2,64,1024]{3,2,1,0:T(8,128)(2,1)} %collective-permute-done.5.refs_3_), channel_id=1, source_target_pairs={{0,16},{16,0},{1,17},{17,1},{2,18},{18,2},{3,19},{19,3},{4,20},{20... | collective-permute-start | bytes 3145736 | tf_op jit(solution)/shard_map/ppermute | solution.py:323
  190.6 6.4 %collective-permute-start.8 = (bf16[4,2,64,1024]{3,2,1,0:T(8,128)(2,1)}, bf16[4,2,64,1024]{3,2,1,0:T(8,128)(2,1)}, u32[]{:S(2)}, u32[]{:S(2)}) collective-permute-start(bf16[4,2,64,1024]{3,2,1,0:T(8,128)(2,1)} %collective-permute-done.4.refs_2_), channel_id=1, source_target_pairs={{0,16},{16,0},{1,17},{17,1},{2,18},{18,2},{3,19},{19,3},{4,20},{20... | collective-permute-start | bytes 3145736 | tf_op jit(solution)/shard_map/ppermute | solution.py:323
  193.9 5.0 %collective-permute-start.7 = (bf16[4,2,64,1024]{3,2,1,0:T(8,128)(2,1)}, bf16[4,2,64,1024]{3,2,1,0:T(8,128)(2,1)}, u32[]{:S(2)}, u32[]{:S(2)}) collective-permute-start(bf16[4,2,64,1024]{3,2,1,0:T(8,128)(2,1)} %collective-permute-done.3.refs_1_), channel_id=1, source_target_pairs={{0,16},{16,0},{1,17},{17,1},{2,18},{18,2},{3,19},{19,3},{4,20},{20... | collective-permute-start | bytes 3145736 | tf_op jit(solution)/shard_map/ppermute | solution.py:323
  199.0 1.3 copy-start
  210.4 83.2 %collective-permute-start.10 = (bf16[224,1024]{1,0:T(8,128)(2,1)}, bf16[224,1024]{1,0:T(8,128)(2,1)S(1)}, u32[]{:S(2)}, u32[]{:S(2)}) collective-permute-start(bf16[224,1024]{1,0:T(8,128)(2,1)} %get-tuple-element.6), channel_id=1, source_target_pairs={{0,8},{1,9},{2,10},{3,11},{4,12},{5,13},{6,14},{7,15},{8,0},{9,1},... | collective-permute-start | bytes 1376264 | tf_op jit(solution)/shard_map/ppermute | solution.py:333
  272.3 19.0 %all-to-all-start.2 = ((f32[16,1,8]{2,1,0:T(1,128)}), f32[16,1,8]{2,1,0:T(1,128)S(1)}, u32[]{:S(2)}, u32[]{:S(2)}) async-start(f32[16,1,8]{2,1,0:T(1,128)} %gate_totals.1), calls=%async_computation.2 | async-start | bytes 16384 | tf_op jit(solution)/shard_map/all_to_all | solution.py:336
  291.3 0.6 copy-start.4
  293.6 0.8 copy-start.2

commit v6 on v5

--- a/solution.py
+++ b/solution.py
@@ -137,20 +137,25 @@
         acc_ref[...] += grad
 
 
-def first_kernel(place_ref, rows_ref, weight_ref, *refs):
-    pieces, (gate_ref, hot_ref, send_ref, acc_ref) = refs[:-4], refs[-4:]
+def gate_kernel(place_ref, rows_ref, weight_ref, *refs):
+    pieces, gate_ref = refs[:-1], refs[-1]
     lines = piece_lines(place_ref)
     split = instance_rows(rows_ref, lines)
     count = rows_ref.shape[0] // 2
     hidden = [jnp.concatenate([piece[i] for piece in pieces], axis=0) for i in range(2)]
-    add_grad(acc_ref, split[0], hidden[0])
     even, odd = swap_halves(*(folded_dots(split[i], hidden[i], weight_ref[i]) for i in range(2)))
     both = jnp.concatenate(
         [even.reshape(count // 8, 1, 8, 128), odd.reshape(count // 8, 1, 8, 128)], axis=1
     )
     both = both.reshape(count * 2 // 128, 128, 128)
     for g, line in enumerate(lines):
-        gate_ref[line] = jnp.sum(both[g].T, axis=0, keepdims=True)
+        gate_ref[line, 0] = jnp.sum(both[g].T, axis=0, keepdims=True)
+
+
+def hot_kernel(place_ref, rows_ref, *refs):
+    pieces, (hot_ref, send_ref, acc_ref) = refs[:-3], refs[-3:]
+    hidden = jnp.concatenate([piece[...] for piece in pieces], axis=0)
+    add_grad(acc_ref, instance_rows(rows_ref, piece_lines(place_ref))[0], hidden)
 
     @pl.when(pl.program_id(0) == pl.num_programs(0) - 1)
     def _():
@@ -158,17 +163,25 @@
         send_ref[...] = acc_ref[...].astype(BF16)
 
 
+def cold_kernel(place_ref, rows_ref, *refs):
+    pieces, (out_ref, acc_ref) = refs[:-2], refs[-2:]
+    hidden = jnp.concatenate([piece[...] for piece in pieces], axis=0)
+    add_grad(acc_ref, instance_rows(rows_ref, piece_lines(place_ref))[1], hidden)
+
+    @pl.when(pl.program_id(0) == pl.num_programs(0) - 1)
+    def _():
+        out_ref[0] = acc_ref[...].astype(BF16)
+
+
 def piece_index(s, m, instance):
     return (lax.rem(m[0] - s + 4, 4), instance, 0, 0)
 
 
-def first_parts(place, rows, pieces, weight):
+def gate_parts(place, rows, pieces, weight):
     steps, _, span, ff = pieces[0].shape
     lines = len(pieces)
-    dp = lines * steps
-    whole = pl.BlockSpec((PIECE, ff), lambda s, m: (0, 0))
-    return pl.pallas_call(
-        first_kernel,
+    return pl.pallas_call(
+        gate_kernel,
         grid_spec=pltpu.PrefetchScalarGridSpec(
             num_scalar_prefetch=1,
             grid=(steps,),
@@ -177,57 +190,43 @@
                 pl.BlockSpec((2, PIECE, ff), lambda s, m: (0, 0, 0)),
             ]
             + [pl.BlockSpec((None, 2, span, ff), lambda s, m: piece_index(s, m, 0))] * lines,
-            out_specs=[
-                pl.BlockSpec((lines, 1, 2 * span), lambda s, m: (s, 0, 0)),
-                whole,
-                whole,
-            ],
-            scratch_shapes=[pltpu.VMEM((PIECE, ff), F32)],
-        ),
-        out_shape=[
-            jax.ShapeDtypeStruct((dp, 1, 2 * span), F32),
-            jax.ShapeDtypeStruct((PIECE, ff), F32),
-            jax.ShapeDtypeStruct((PIECE, ff), BF16),
-        ],
+            out_specs=pl.BlockSpec((lines, 1, 1, 2 * span), lambda s, m: (0, s, 0, 0)),
+        ),
+        out_shape=jax.ShapeDtypeStruct((lines, steps, 1, 2 * span), F32),
         cost_estimate=pl.CostEstimate(
-            flops=6 * dp * span * PIECE * ff,
-            bytes_accessed=4 * dp * span * ff + 2 * rows.size + 2 * weight.size,
+            flops=4 * lines * steps * span * PIECE * ff,
+            bytes_accessed=4 * lines * steps * span * ff + 2 * rows.size + 2 * weight.size,
             transcendentals=0,
         ),
-        name="first_parts",
+        name="gate_parts",
     )(place, rows, weight, *pieces)
 
 
-def cold_kernel(place_ref, rows_ref, *refs):
-    pieces, (out_ref, acc_ref) = refs[:-2], refs[-2:]
-    hidden = jnp.concatenate([piece[...] for piece in pieces], axis=0)
-    add_grad(acc_ref, instance_rows(rows_ref, piece_lines(place_ref))[1], hidden)
-
-    @pl.when(pl.program_id(0) == pl.num_programs(0) - 1)
-    def _():
-        out_ref[0] = acc_ref[...].astype(BF16)
-
-
-def cold_parts(place, rows, pieces):
+def weight_parts(which, place, rows, pieces):
     steps, _, span, ff = pieces[0].shape
     lines = len(pieces)
-    return pl.pallas_call(
-        cold_kernel,
+    hot = which == 0
+    whole = pl.BlockSpec((PIECE, ff), lambda s, m: (0, 0))
+    half = pl.BlockSpec((1, PIECE, ff), lambda s, m: (1, 0, 0))
+    return pl.pallas_call(
+        hot_kernel if hot else cold_kernel,
         grid_spec=pltpu.PrefetchScalarGridSpec(
             num_scalar_prefetch=1,
             grid=(steps,),
             in_specs=[pl.BlockSpec((lines * span * 2, WIDE), lambda s, m: (s, 0))]
-            + [pl.BlockSpec((None, None, span, ff), lambda s, m: piece_index(s, m, 1))] * lines,
-            out_specs=pl.BlockSpec((1, PIECE, ff), lambda s, m: (1, 0, 0)),
+            + [pl.BlockSpec((None, None, span, ff), lambda s, m: piece_index(s, m, which))] * lines,
+            out_specs=[whole, whole] if hot else half,
             scratch_shapes=[pltpu.VMEM((PIECE, ff), F32)],
         ),
-        out_shape=jax.ShapeDtypeStruct((2, PIECE, ff), BF16),
+        out_shape=[jax.ShapeDtypeStruct((PIECE, ff), t) for t in (F32, BF16)]
+        if hot
+        else jax.ShapeDtypeStruct((2, PIECE, ff), BF16),
         cost_estimate=pl.CostEstimate(
             flops=2 * lines * steps * span * PIECE * ff,
             bytes_accessed=2 * lines * steps * span * ff + 2 * rows.size,
             transcendentals=0,
         ),
-        name="cold_parts",
+        name="hot_parts" if hot else "cold_parts",
     )(place, rows, *pieces)
 
 
@@ -250,9 +249,12 @@
 
 
 def total_kernel(parts_ref, out_ref):
+    steps = parts_ref.shape[1]
+    experts = out_ref.shape[0] // steps
     total = jnp.sum(parts_ref[...], axis=0)
-    for e in range(out_ref.shape[0]):
-        out_ref[e] = total[:, e * 2 * CAP : (e + 1) * 2 * CAP]
+    for z in range(steps):
+        for e in range(experts):
+            out_ref[z * experts + e] = total[z, :, e * 2 * CAP : (e + 1) * 2 * CAP]
 
 
 def gate_totals(parts, expert):
@@ -261,21 +263,21 @@
         total_kernel,
         in_specs=[vmem],
         out_specs=vmem,
-        out_shape=jax.ShapeDtypeStruct((expert, 1, 2 * CAP), F32),
+        out_shape=jax.ShapeDtypeStruct((parts.shape[1] * expert, 1, 2 * CAP), F32),
         name="gate_totals",
     )(parts)
 
 
 def pick_kernel(place_ref, ids_ref, pick_ref, gate_ref, back_ref, out_ref):
     masks, _, rank = route_masks(ids_ref, pick_ref, place_ref)
-    experts = back_ref.shape[0]
+    parts = back_ref.shape[0]
     spread = (
-        lax.broadcasted_iota(jnp.int32, (INSTANCES, experts), 0) // 2
-        == lax.broadcasted_iota(jnp.int32, (INSTANCES, experts), 1)
+        lax.broadcasted_iota(jnp.int32, (INSTANCES, parts), 0) // 2
+        == lax.broadcasted_iota(jnp.int32, (INSTANCES, parts), 1) % (INSTANCES // 2)
     ).astype(F32)
     back = jnp.dot(
         spread,
-        back_ref[...].reshape(experts, 2 * CAP),
+        back_ref[...].reshape(parts, 2 * CAP),
         precision=lax.Precision.HIGHEST,
         preferred_element_type=F32,
     )
@@ -327,13 +329,14 @@
     sent = sent.reshape(dp * expert, 2 * CAP, WIDE)
     rows = lax.all_to_all(sent, EVERY, split_axis=0, concat_axis=0, tiled=True)
     rows = rows.reshape(dp * expert * 2 * CAP, WIDE)
-    parts, hot, hot_sent = first_parts(place, rows, pieces, down_proj)
-    parts = lax.all_to_all(parts, GROUPS, split_axis=0, concat_axis=0, tiled=True)
+    hot, hot_sent = weight_parts(0, place, rows, pieces)
     half = expert // 2
     other = lax.ppermute(hot_sent, EXPERT, [(e, (e + half) % expert) for e in range(expert)])
-    grad = cold_parts(place, rows, pieces)
+    parts = gate_parts(place, rows, pieces, down_proj)
+    parts = lax.all_to_all(parts, LINES, split_axis=0, concat_axis=0, tiled=True)
+    grad = weight_parts(1, place, rows, pieces)
     own = gate_totals(parts, expert)
-    back = lax.all_to_all(own, EXPERT, split_axis=0, concat_axis=0, tiled=True)
+    back = lax.all_to_all(own, ("zl",) + EXPERT, split_axis=0, concat_axis=0, tiled=True)
     grad_gate = pick_gates(placement, ids, pick, gates, back).T
     return pair_sum(hot, other, grad), grad_gate
 

time: 298 us -> 276 us (0.926)
  blocking collectives: 48.5 us -> 9.43 us
  starting transfers between devices: 96.2 us -> 104 us
  Pallas kernels: 28.7 us -> 33.2 us
  waiting for transfers between devices: 119 us -> 123 us
    all_to_all x1, blocking collectives: 48.5 us -> 9.43 us  [layer(): lax.all_to_all(parts, LINES, split_axis=0, concat_axis=0, tiled=True)]
    all_to_all x1, starting transfers between devices: 5.34 us -> 13.4 us  [layer(): lax.all_to_all(own, ('zl',) + EXPERT, split_axis=0, concat_axis=0, tiled=...]
    pallas_call x2 -> x3, Pallas kernels: 16.3 us -> 20.8 us  [the longest x2 12.8 us: weight_parts(): pl.pallas_call(hot_kernel if hot else cold_kernel, grid_spec=pltpu.Prefet...]
    all_to_all x1, waiting for transfers between devices: 7.41 us -> 11.5 us  [layer(): lax.all_to_all(own, ('zl',) + EXPERT, split_axis=0, concat_axis=0, tiled=...]
  transfers between devices with their start and end apart: 13 -> 13, of which waited for: 6 -> 6; matrix products, arithmetic and copies ran while one was open for 0% -> 0% of each run, Pallas kernels for 3% -> 6%
where the time goes in v6:
time: 276 us; the launch traced here: 274 us
  waiting for transfers between devices  123 us (45%)
  starting transfers between devices  104 us (38%)
  Pallas kernels  33.2 us (12%)
  blocking collectives  9.43 us (3%)
  local copies, waits for them, and re-layouts  2.95 us (1%)
    ppermute x3, waiting for transfers between devices, layer(): lax.ppermute(local, 'zl', [(z, (z + d) % depth) for z in range(depth)])  95.4 us
    ppermute x4, starting transfers between devices, layer(): lax.ppermute(piece, 'c', [(0, 1), (1, 0)])  34.4 us
    all_to_all x1, starting transfers between devices, layer(): rows = lax.all_to_all(sent, EVERY, split_axis=0, concat_axis=0, tiled=True)  24.3 us
    ppermute x3, waiting for transfers between devices, layer(): lax.ppermute(column, 'y', [(y, (y + d) % 4) for y in range(4)])  14.1 us
    all_to_all x1, starting transfers between devices, layer(): lax.all_to_all(own, ('zl',) + EXPERT, split_axis=0, concat_axis=0, tiled=...  13.4 us
    pallas_call x2, Pallas kernels, weight_parts(): pl.pallas_call(hot_kernel if hot else cold_kernel, grid_spec=pltpu.Prefet...  12.8 us
    ppermute x1, starting transfers between devices, layer(): lax.ppermute(hot_sent, EXPERT, [(e, (e + half) % expert) for e in range(e...  11.9 us
    all_to_all x1, waiting for transfers between devices, layer(): lax.all_to_all(own, ('zl',) + EXPERT, split_axis=0, concat_axis=0, tiled=...  11.5 us
  transfers between devices with their start and end apart: 13, of which 6 were waited for; matrix products, arithmetic and copies ran while one was open for 0% of the time, Pallas kernels for 6%

profile of v6, /device:TPU:1, one launch (start us, length us, event | category | flops | bytes accessed | tf_op | source)
XLA Modules:
  0.0 274.1 jit_solution(589882687195242205)
XLA Ops:
  0.6 7.0 %gather_rows.1 = bf16[32,128,256]{2,1,0:T(8,128)(2,1)} custom-call(s32[32]{0:T(128)} %place_ref.3, s32[8,128]{1,0:T(8,128)} %bitcast.17, s32[8,128]{1,0:T(8,128)} %bitcast.19, f32[8,128]{1,0:T(8,128)} %bitcast.21, bf16[128,7168]{1,0:T(8,128)(2,1)} %grad_ref.1), custom_call_target="tpu_custom_call" | custom-call | flops 234881024 | bytes 3670016 | tf_op jit(solution)/shard_map/gather_rows/pallas_call | solution.py:71
  7.6 24.3 %all-to-all-start = ((bf16[512,8,256]{2,1,0:T(8,128)(2,1)}), bf16[512,8,256]{2,1,0:T(8,128)(2,1)S(1)}, u32[]{:S(2)}, u32[]{:S(2)}) async-start(bf16[512,8,256]{2,1,0:T(8,128)(2,1)} %bitcast.15), calls=%async_computation | async-start | bytes 4194304 | tf_op jit(solution)/shard_map/all_to_all | solution.py:330
  32.1 3.4 %collective-permute-start = (bf16[1,2,64,1024]{3,2,1,0:T(8,128)(2,1)S(1)}, bf16[1,2,64,1024]{3,2,1,0:T(8,128)(2,1)S(1)}, u32[]{:S(2)}, u32[]{:S(2)}) collective-permute-start(bf16[1,2,64,1024]{3,2,1,0:T(8,128)(2,1)S(1)} %reshape.15), channel_id=1, source_target_pairs={{0,128},{128,256},{256,384},{384,0},{1,129},{129,257},{257,385},{3... | collective-permute-start | bytes 786440 | tf_op jit(solution)/shard_map/ppermute | solution.py:318
  35.5 4.5 %collective-permute-start.1 = (bf16[1,2,64,1024]{3,2,1,0:T(8,128)(2,1)S(1)}, bf16[1,2,64,1024]{3,2,1,0:T(8,128)(2,1)S(1)}, u32[]{:S(2)}, u32[]{:S(2)}) collective-permute-start(bf16[1,2,64,1024]{3,2,1,0:T(8,128)(2,1)S(1)} %reshape.15), channel_id=1, source_target_pairs={{0,256},{128,384},{256,0},{384,128},{1,257},{129,385},{257,1},{385... | collective-permute-start | bytes 786440 | tf_op jit(solution)/shard_map/ppermute | solution.py:318
  40.1 2.8 %collective-permute-start.2 = (bf16[1,2,64,1024]{3,2,1,0:T(8,128)(2,1)S(1)}, bf16[1,2,64,1024]{3,2,1,0:T(8,128)(2,1)S(1)}, u32[]{:S(2)}, u32[]{:S(2)}) collective-permute-start(bf16[1,2,64,1024]{3,2,1,0:T(8,128)(2,1)S(1)} %reshape.15), channel_id=1, source_target_pairs={{0,384},{128,0},{256,128},{384,256},{1,385},{129,1},{257,129},{385... | collective-permute-start | bytes 786440 | tf_op jit(solution)/shard_map/ppermute | solution.py:318
  42.9 84.9 %collective-permute-done = bf16[1,2,64,1024]{3,2,1,0:T(8,128)(2,1)S(1)} collective-permute-done((bf16[1,2,64,1024]{3,2,1,0:T(8,128)(2,1)S(1)}, bf16[1,2,64,1024]{3,2,1,0:T(8,128)(2,1)S(1)}, u32[]{:S(2)}, u32[]{:S(2)}) %collective-permute-start) | collective-permute-done | bytes 262176 | tf_op jit(solution)/shard_map/ppermute | solution.py:318
  127.8 10.5 %collective-permute-done.1 = bf16[1,2,64,1024]{3,2,1,0:T(8,128)(2,1)S(1)} collective-permute-done((bf16[1,2,64,1024]{3,2,1,0:T(8,128)(2,1)S(1)}, bf16[1,2,64,1024]{3,2,1,0:T(8,128)(2,1)S(1)}, u32[]{:S(2)}, u32[]{:S(2)}) %collective-permute-start.1) | collective-permute-done | bytes 262176 | tf_op jit(solution)/shard_map/ppermute | solution.py:318
  138.4 4.5 %collective-permute-start.5 = (bf16[4,2,64,1024]{3,2,1,0:T(8,128)(2,1)S(1)}, bf16[4,2,64,1024]{3,2,1,0:T(8,128)(2,1)}, u32[]{:S(2)}, u32[]{:S(2)}) collective-permute-start(bf16[4,2,64,1024]{3,2,1,0:T(8,128)(2,1)S(1)} %constant_dynamic-update-slice_fusion.refs_0_), channel_id=1, source_target_pairs={{0,96},{32,0},{64,32},{96,64},{1,97},{33,1},{65,33},{97,65},{2,98}... | collective-permute-start | bytes 3145736 | tf_op jit(solution)/shard_map/ppermute | solution.py:324
  142.9 2.4 collective-permute-start.4
  145.2 2.6 collective-permute-start.3
  147.8 4.3 %collective-permute-start.6 = (bf16[4,2,64,1024]{3,2,1,0:T(8,128)(2,1)S(1)}, bf16[4,2,64,1024]{3,2,1,0:T(8,128)(2,1)}, u32[]{:S(2)}, u32[]{:S(2)}) collective-permute-start(bf16[4,2,64,1024]{3,2,1,0:T(8,128)(2,1)S(1)} %constant_dynamic-update-slice_fusion.refs_0_), channel_id=1, source_target_pairs={{0,16},{16,0},{1,17},{17,1},{2,18},{18,2},{3,19},{19,3},{4,20},{20... | collective-permute-start | bytes 3145736 | tf_op jit(solution)/shard_map/ppermute | solution.py:325
  152.1 12.7 %collective-permute-done.5.refs_3_ = bf16[4,2,64,1024]{3,2,1,0:T(8,128)(2,1)} collective-permute-done((bf16[4,2,64,1024]{3,2,1,0:T(8,128)(2,1)S(1)}, bf16[4,2,64,1024]{3,2,1,0:T(8,128)(2,1)}, u32[]{:S(2)}, u32[]{:S(2)}) %collective-permute-start.5) | collective-permute-done | bytes 1048608 | tf_op jit(solution)/shard_map/ppermute | solution.py:324
  164.8 25.8 %collective-permute-start.9 = (bf16[4,2,64,1024]{3,2,1,0:T(8,128)(2,1)}, bf16[4,2,64,1024]{3,2,1,0:T(8,128)(2,1)}, u32[]{:S(2)}, u32[]{:S(2)}) collective-permute-start(bf16[4,2,64,1024]{3,2,1,0:T(8,128)(2,1)} %collective-permute-done.5.refs_3_), channel_id=1, source_target_pairs={{0,16},{16,0},{1,17},{17,1},{2,18},{18,2},{3,19},{19,3},{4,20},{20... | collective-permute-start | bytes 3145736 | tf_op jit(solution)/shard_map/ppermute | solution.py:325
  190.6 1.9 collective-permute-start.8
  193.9 2.4 collective-permute-start.7
  197.0 1.9 collective-permute-done.7.refs_5_
  200.3 6.6 %hot_parts.1 = (f32[224,1024]{1,0:T(8,128)}, bf16[224,1024]{1,0:T(8,128)(2,1)}) custom-call(s32[3]{0:T(128)} %pad_add_fusion.place_ref, bf16[4096,256]{1,0:T(8,128)(2,1)} %bitcast.12, bf16[4,2,64,1024]{3,2,1,0:T(8,128)(2,1)} %copy-done.1, bf16[4,2,64,1024]{3,2,1,0:T(8,128)(2,1)} %collective-permute-done.3.refs_1_, ...), custom_call_target="tpu_custom_call" | custom-call | flops 939524096 | bytes 6291456 | tf_op jit(solution)/shard_map/hot_parts/pallas_call | solution.py:211
  206.9 11.9 %collective-permute-start.10 = (bf16[224,1024]{1,0:T(8,128)(2,1)}, bf16[224,1024]{1,0:T(8,128)(2,1)S(1)}, u32[]{:S(2)}, u32[]{:S(2)}) collective-permute-start(bf16[224,1024]{1,0:T(8,128)(2,1)} %get-tuple-element.5), channel_id=1, source_target_pairs={{0,8},{1,9},{2,10},{3,11},{4,12},{5,13},{6,14},{7,15},{8,0},{9,1},... | collective-permute-start | bytes 1376264 | tf_op jit(solution)/shard_map/ppermute | solution.py:334
  218.8 7.9 %gate_parts.1 = f32[8,4,1,128]{3,2,1,0:T(1,128)} custom-call(s32[3]{0:T(128)} %pad_add_fusion.place_ref, bf16[4096,256]{1,0:T(8,128)(2,1)} %bitcast.13, bf16[2,224,1024]{2,1,0:T(8,128)(2,1)} %weight_ref.1, bf16[4,2,64,1024]{3,2,1,0:T(8,128)(2,1)} %copy-done.1, bf16[4,2,64,1024]{3,2,1,0:T(8,128)(2,1)} %collective-permute-done.3.refs_1_, ...), custom_call_target="tpu_custom_call" | custom-call | flops 1879048192 | bytes 11403264 | tf_op jit(solution)/shard_map/gate_parts/pallas_call | solution.py:183
  226.8 9.4 %all_to_all.15.parts_ref = f32[8,4,1,128]{3,2,1,0:T(1,128)} all-to-all(f32[8,4,1,128]{3,2,1,0:T(1,128)} %gate_parts.1), channel_id=1, replica_groups=mesh['zl'=4,'y'=4,'c'=2,'zh'=4,'x'=4] {'y','c'}, dimensions={0} | all-to-all | bytes 32768 | tf_op jit(solution)/shard_map/all_to_all | solution.py:336
  237.7 13.4 %all-to-all-start.2 = ((f32[64,1,8]{2,1,0:T(1,128)}), f32[64,1,8]{2,1,0:T(1,128)S(1)}, u32[]{:S(2)}, u32[]{:S(2)}) async-start(f32[64,1,8]{2,1,0:T(1,128)} %gate_totals.1), calls=%async_computation.2 | async-start | bytes 65536 | tf_op jit(solution)/shard_map/all_to_all | solution.py:339
  251.1 6.2 %cold_parts.1.grad_ref = bf16[2,224,1024]{2,1,0:T(8,128)(2,1)} custom-call(s32[3]{0:T(128)} %pad_add_fusion.place_ref, bf16[4096,256]{1,0:T(8,128)(2,1)} %bitcast.14, bf16[4,2,64,1024]{3,2,1,0:T(8,128)(2,1)} %copy-done.1, bf16[4,2,64,1024]{3,2,1,0:T(8,128)(2,1)} %collective-permute-done.3.refs_1_, bf16[4,2,64,1024]{3,2,1,0:T(8,128)(2,1)} %collective-permute-done.4.refs_2_, ...), custom_call_target="tpu_custom_call" | custom-call | flops 939524096 | bytes 6291456 | tf_op jit(solution)/shard_map/cold_parts/pallas_call | solution.py:211
  257.3 11.5 %all-to-all-done.2.back_ref = f32[64,1,8]{2,1,0:T(1,128)S(1)} async-done(((f32[64,1,8]{2,1,0:T(1,128)}), f32[64,1,8]{2,1,0:T(1,128)S(1)}, u32[]{:S(2)}, u32[]{:S(2)}) %all-to-all-start.2) | async-done | bytes 2080 | tf_op jit(solution)/shard_map/all_to_all | solution.py:339
  272.0 2.1 pair_sum.1
  (27 shorter events, 8.3 us)
Async XLA Ops:
  7.6 24.3 %copy-start.3 = (bf16[1,16,2,4,1024]{4,3,2,1,0:T(4,128)(2,1)S(1)}, bf16[1,16,2,4,1024]{4,3,2,1,0:T(4,128)(2,1)}, u32[]{:S(2)}) copy-start(bf16[1,16,2,4,1024]{4,3,2,1,0:T(4,128)(2,1)} %param.12) | copy-start | bytes 786436
  7.6 191.3 %all-to-all-start = ((bf16[512,8,256]{2,1,0:T(8,128)(2,1)}), bf16[512,8,256]{2,1,0:T(8,128)(2,1)S(1)}, u32[]{:S(2)}, u32[]{:S(2)}) async-start(bf16[512,8,256]{2,1,0:T(8,128)(2,1)} %bitcast.15), calls=%async_computation | async-start | bytes 4194304 | tf_op jit(solution)/shard_map/all_to_all | solution.py:330
  32.1 95.7 %collective-permute-start = (bf16[1,2,64,1024]{3,2,1,0:T(8,128)(2,1)S(1)}, bf16[1,2,64,1024]{3,2,1,0:T(8,128)(2,1)S(1)}, u32[]{:S(2)}, u32[]{:S(2)}) collective-permute-start(bf16[1,2,64,1024]{3,2,1,0:T(8,128)(2,1)S(1)} %reshape.15), channel_id=1, source_target_pairs={{0,128},{128,256},{256,384},{384,0},{1,129},{129,257},{257,385},{3... | collective-permute-start | bytes 786440 | tf_op jit(solution)/shard_map/ppermute | solution.py:318
  35.5 102.8 %collective-permute-start.1 = (bf16[1,2,64,1024]{3,2,1,0:T(8,128)(2,1)S(1)}, bf16[1,2,64,1024]{3,2,1,0:T(8,128)(2,1)S(1)}, u32[]{:S(2)}, u32[]{:S(2)}) collective-permute-start(bf16[1,2,64,1024]{3,2,1,0:T(8,128)(2,1)S(1)} %reshape.15), channel_id=1, source_target_pairs={{0,256},{128,384},{256,0},{384,128},{1,257},{129,385},{257,1},{385... | collective-permute-start | bytes 786440 | tf_op jit(solution)/shard_map/ppermute | solution.py:318
  40.1 98.3 %collective-permute-start.2 = (bf16[1,2,64,1024]{3,2,1,0:T(8,128)(2,1)S(1)}, bf16[1,2,64,1024]{3,2,1,0:T(8,128)(2,1)S(1)}, u32[]{:S(2)}, u32[]{:S(2)}) collective-permute-start(bf16[1,2,64,1024]{3,2,1,0:T(8,128)(2,1)S(1)} %reshape.15), channel_id=1, source_target_pairs={{0,384},{128,0},{256,128},{384,256},{1,385},{129,1},{257,129},{385... | collective-permute-start | bytes 786440 | tf_op jit(solution)/shard_map/ppermute | solution.py:318
  138.4 60.6 %copy-start.1 = (bf16[4,2,64,1024]{3,2,1,0:T(8,128)(2,1)}, bf16[4,2,64,1024]{3,2,1,0:T(8,128)(2,1)S(1)}, u32[]{:S(2)}) copy-start(bf16[4,2,64,1024]{3,2,1,0:T(8,128)(2,1)S(1)} %constant_dynamic-update-slice_fusion.refs_0_) | copy-start | bytes 3145732
  138.4 26.4 %collective-permute-start.5 = (bf16[4,2,64,1024]{3,2,1,0:T(8,128)(2,1)S(1)}, bf16[4,2,64,1024]{3,2,1,0:T(8,128)(2,1)}, u32[]{:S(2)}, u32[]{:S(2)}) collective-permute-start(bf16[4,2,64,1024]{3,2,1,0:T(8,128)(2,1)S(1)} %constant_dynamic-update-slice_fusion.refs_0_), channel_id=1, source_target_pairs={{0,96},{32,0},{64,32},{96,64},{1,97},{33,1},{65,33},{97,65},{2,98}... | collective-permute-start | bytes 3145736 | tf_op jit(solution)/shard_map/ppermute | solution.py:324
  142.9 47.7 %collective-permute-start.4 = (bf16[4,2,64,1024]{3,2,1,0:T(8,128)(2,1)S(1)}, bf16[4,2,64,1024]{3,2,1,0:T(8,128)(2,1)}, u32[]{:S(2)}, u32[]{:S(2)}) collective-permute-start(bf16[4,2,64,1024]{3,2,1,0:T(8,128)(2,1)S(1)} %constant_dynamic-update-slice_fusion.refs_0_), channel_id=1, source_target_pairs={{0,64},{32,96},{64,0},{96,32},{1,65},{33,97},{65,1},{97,33},{2,66}... | collective-permute-start | bytes 3145736 | tf_op jit(solution)/shard_map/ppermute | solution.py:324
  145.2 48.7 %collective-permute-start.3 = (bf16[4,2,64,1024]{3,2,1,0:T(8,128)(2,1)S(1)}, bf16[4,2,64,1024]{3,2,1,0:T(8,128)(2,1)}, u32[]{:S(2)}, u32[]{:S(2)}) collective-permute-start(bf16[4,2,64,1024]{3,2,1,0:T(8,128)(2,1)S(1)} %constant_dynamic-update-slice_fusion.refs_0_), channel_id=1, source_target_pairs={{0,32},{32,64},{64,96},{96,0},{1,33},{33,65},{65,97},{97,1},{2,34}... | collective-permute-start | bytes 3145736 | tf_op jit(solution)/shard_map/ppermute | solution.py:324
  147.8 49.2 %collective-permute-start.6 = (bf16[4,2,64,1024]{3,2,1,0:T(8,128)(2,1)S(1)}, bf16[4,2,64,1024]{3,2,1,0:T(8,128)(2,1)}, u32[]{:S(2)}, u32[]{:S(2)}) collective-permute-start(bf16[4,2,64,1024]{3,2,1,0:T(8,128)(2,1)S(1)} %constant_dynamic-update-slice_fusion.refs_0_), channel_id=1, source_target_pairs={{0,16},{16,0},{1,17},{17,1},{2,18},{18,2},{3,19},{19,3},{4,20},{20... | collective-permute-start | bytes 3145736 | tf_op jit(solution)/shard_map/ppermute | solution.py:325
  164.8 32.2 %collective-permute-start.9 = (bf16[4,2,64,1024]{3,2,1,0:T(8,128)(2,1)}, bf16[4,2,64,1024]{3,2,1,0:T(8,128)(2,1)}, u32[]{:S(2)}, u32[]{:S(2)}) collective-permute-start(bf16[4,2,64,1024]{3,2,1,0:T(8,128)(2,1)} %collective-permute-done.5.refs_3_), channel_id=1, source_target_pairs={{0,16},{16,0},{1,17},{17,1},{2,18},{18,2},{3,19},{19,3},{4,20},{20... | collective-permute-start | bytes 3145736 | tf_op jit(solution)/shard_map/ppermute | solution.py:325
  190.6 6.4 %collective-permute-start.8 = (bf16[4,2,64,1024]{3,2,1,0:T(8,128)(2,1)}, bf16[4,2,64,1024]{3,2,1,0:T(8,128)(2,1)}, u32[]{:S(2)}, u32[]{:S(2)}) collective-permute-start(bf16[4,2,64,1024]{3,2,1,0:T(8,128)(2,1)} %collective-permute-done.4.refs_2_), channel_id=1, source_target_pairs={{0,16},{16,0},{1,17},{17,1},{2,18},{18,2},{3,19},{19,3},{4,20},{20... | collective-permute-start | bytes 3145736 | tf_op jit(solution)/shard_map/ppermute | solution.py:325
  193.9 5.0 %collective-permute-start.7 = (bf16[4,2,64,1024]{3,2,1,0:T(8,128)(2,1)}, bf16[4,2,64,1024]{3,2,1,0:T(8,128)(2,1)}, u32[]{:S(2)}, u32[]{:S(2)}) collective-permute-start(bf16[4,2,64,1024]{3,2,1,0:T(8,128)(2,1)} %collective-permute-done.3.refs_1_), channel_id=1, source_target_pairs={{0,16},{16,0},{1,17},{17,1},{2,18},{18,2},{3,19},{19,3},{4,20},{20... | collective-permute-start | bytes 3145736 | tf_op jit(solution)/shard_map/ppermute | solution.py:325
  199.0 1.3 copy-start
  206.9 64.3 %collective-permute-start.10 = (bf16[224,1024]{1,0:T(8,128)(2,1)}, bf16[224,1024]{1,0:T(8,128)(2,1)S(1)}, u32[]{:S(2)}, u32[]{:S(2)}) collective-permute-start(bf16[224,1024]{1,0:T(8,128)(2,1)} %get-tuple-element.5), channel_id=1, source_target_pairs={{0,8},{1,9},{2,10},{3,11},{4,12},{5,13},{6,14},{7,15},{8,0},{9,1},... | collective-permute-start | bytes 1376264 | tf_op jit(solution)/shard_map/ppermute | solution.py:334
  237.7 31.1 %all-to-all-start.2 = ((f32[64,1,8]{2,1,0:T(1,128)}), f32[64,1,8]{2,1,0:T(1,128)S(1)}, u32[]{:S(2)}, u32[]{:S(2)}) async-start(f32[64,1,8]{2,1,0:T(1,128)} %gate_totals.1), calls=%async_computation.2 | async-start | bytes 65536 | tf_op jit(solution)/shard_map/all_to_all | solution.py:339
  268.8 0.6 copy-start.4
  271.2 0.8 copy-start.2

commit v7 on v6

--- a/solution.py
+++ b/solution.py
@@ -59,14 +59,15 @@
 
     rows = jnp.dot(select_ref[...], grad_ref[...], preferred_element_type=F32)
     blank = jnp.zeros((SLOTS, WIDE - PIECE), F32)
-    for j in range(4):
+    for j in range(out_ref.shape[0]):
         part = jnp.concatenate([rows[:, j * PIECE : (j + 1) * PIECE], blank], axis=1)
         out_ref[j] = part.astype(BF16)
 
 
 def gather_rows(placement, ids, pick, gates, grad_out):
     width = grad_out.shape[1]
-    steps = width // (4 * PIECE)
+    per = 8
+    steps = width // (per * PIECE)
     whole = pl.BlockSpec((TOP, TOK), lambda s: (0, 0))
     return pl.pallas_call(
         gather_kernel,
@@ -76,10 +77,10 @@
             whole,
             whole,
             whole,
-            pl.BlockSpec((TOK, 4 * PIECE), lambda s: (0, s)),
+            pl.BlockSpec((TOK, per * PIECE), lambda s: (0, s)),
         ],
-        out_specs=pl.BlockSpec((4, SLOTS, WIDE), lambda s: (s, 0, 0)),
-        out_shape=jax.ShapeDtypeStruct((steps * 4, SLOTS, WIDE), BF16),
+        out_specs=pl.BlockSpec((per, SLOTS, WIDE), lambda s: (s, 0, 0)),
+        out_shape=jax.ShapeDtypeStruct((steps * per, SLOTS, WIDE), BF16),
         scratch_shapes=[pltpu.VMEM((SLOTS, TOK), BF16)],
         cost_estimate=pl.CostEstimate(
             flops=2 * SLOTS * TOK * width, bytes_accessed=4 * TOK * width, transcendentals=0
@@ -228,24 +229,6 @@
         ),
         name="hot_parts" if hot else "cold_parts",
     )(place, rows, *pieces)
-
-
-def pair_kernel(hot_ref, other_ref, grad_ref, out_ref):
-    out_ref[0] = (hot_ref[...] + other_ref[...].astype(F32)).astype(BF16)
-
-
-def pair_sum(hot, other, grad):
-    ff = hot.shape[1]
-    whole = pl.BlockSpec((PIECE, ff), lambda s: (0, 0))
-    return pl.pallas_call(
-        pair_kernel,
-        grid=(1,),
-        in_specs=[whole, whole, pl.BlockSpec(memory_space=pl.ANY)],
-        out_specs=pl.BlockSpec((1, PIECE, ff), lambda s: (0, 0, 0)),
-        out_shape=jax.ShapeDtypeStruct(grad.shape, BF16),
-        input_output_aliases={2: 0},
-        name="pair_sum",
-    )(hot, other, grad)
 
 
 def total_kernel(parts_ref, out_ref):
@@ -338,7 +321,8 @@
     own = gate_totals(parts, expert)
     back = lax.all_to_all(own, ("zl",) + EXPERT, split_axis=0, concat_axis=0, tiled=True)
     grad_gate = pick_gates(placement, ids, pick, gates, back).T
-    return pair_sum(hot, other, grad), grad_gate
+    pair = (hot + other.astype(F32)).astype(BF16)
+    return lax.dynamic_update_slice(grad, pair[None], (0, 0, 0)), grad_gate
 
 
 def solution(mesh):

time: 276 us -> 271 us (0.982)
  starting transfers between devices: 104 us -> 86.7 us
  waiting for transfers between devices: 123 us -> 139 us
  Pallas kernels: 33.2 us -> 28.9 us
    ppermute x4, starting transfers between devices: 34.4 us -> 15.7 us  [layer(): lax.ppermute(piece, 'c', [(0, 1), (1, 0)])]
    ppermute x3, waiting for transfers between devices: 14.1 us -> 29.9 us  [layer(): lax.ppermute(column, 'y', [(y, (y + d) % 4) for y in range(4)])]
  transfers between devices with their start and end apart: 13 -> 13, of which waited for: 6 -> 6; matrix products, arithmetic and copies ran while one was open for 0% -> 0% of each run, Pallas kernels for 6% -> 7%
where the time goes in v7:
time: 271 us; the launch traced here: 268 us
  waiting for transfers between devices  139 us (51%)
  starting transfers between devices  86.7 us (32%)
  Pallas kernels  28.9 us (11%)
  blocking collectives  9.18 us (3%)
    ppermute x3, waiting for transfers between devices, layer(): lax.ppermute(local, 'zl', [(z, (z + d) % depth) for z in range(depth)])  95.4 us
    ppermute x3, waiting for transfers between devices, layer(): lax.ppermute(column, 'y', [(y, (y + d) % 4) for y in range(4)])  29.9 us
    all_to_all x1, starting transfers between devices, layer(): rows = lax.all_to_all(sent, EVERY, split_axis=0, concat_axis=0, tiled=True)  24.3 us
    ppermute x4, starting transfers between devices, layer(): lax.ppermute(piece, 'c', [(0, 1), (1, 0)])  15.7 us
    all_to_all x1, starting transfers between devices, layer(): lax.all_to_all(own, ('zl',) + EXPERT, split_axis=0, concat_axis=0, tiled=...  13.4 us
    pallas_call x2, Pallas kernels, weight_parts(): pl.pallas_call(hot_kernel if hot else cold_kernel, grid_spec=pltpu.Prefet...  13 us
    ppermute x1, starting transfers between devices, layer(): lax.ppermute(hot_sent, EXPERT, [(e, (e + half) % expert) for e in range(e...  12 us
    all_to_all x1, waiting for transfers between devices, layer(): lax.all_to_all(own, ('zl',) + EXPERT, split_axis=0, concat_axis=0, tiled=...  11.6 us
  transfers between devices with their start and end apart: 13, of which 6 were waited for; matrix products, arithmetic and copies ran while one was open for 0% of the time, Pallas kernels for 7%

profile of v7, /device:TPU:1, one launch (start us, length us, event | category | flops | bytes accessed | tf_op | source)
XLA Modules:
  0.0 268.5 jit_solution(2124896106667636924)
XLA Ops:
  0.6 4.8 %gather_rows.1 = bf16[32,128,256]{2,1,0:T(8,128)(2,1)} custom-call(s32[32]{0:T(128)} %place_ref.3, s32[8,128]{1,0:T(8,128)} %bitcast.21, s32[8,128]{1,0:T(8,128)} %bitcast.23, f32[8,128]{1,0:T(8,128)} %bitcast.25, bf16[128,7168]{1,0:T(8,128)(2,1)} %grad_ref.1), custom_call_target="tpu_custom_call" | custom-call | flops 234881024 | bytes 3670016 | tf_op jit(solution)/shard_map/gather_rows/pallas_call | solution.py:72
  5.4 24.3 %all-to-all-start = ((bf16[512,8,256]{2,1,0:T(8,128)(2,1)}), bf16[512,8,256]{2,1,0:T(8,128)(2,1)S(1)}, u32[]{:S(2)}, u32[]{:S(2)}) async-start(bf16[512,8,256]{2,1,0:T(8,128)(2,1)} %bitcast.19), calls=%async_computation | async-start | bytes 4194304 | tf_op jit(solution)/shard_map/all_to_all | solution.py:313
  29.9 3.4 %collective-permute-start = (bf16[1,2,64,1024]{3,2,1,0:T(8,128)(2,1)S(1)}, bf16[1,2,64,1024]{3,2,1,0:T(8,128)(2,1)S(1)}, u32[]{:S(2)}, u32[]{:S(2)}) collective-permute-start(bf16[1,2,64,1024]{3,2,1,0:T(8,128)(2,1)S(1)} %reshape.15), channel_id=1, source_target_pairs={{0,128},{128,256},{256,384},{384,0},{1,129},{129,257},{257,385},{3... | collective-permute-start | bytes 786440 | tf_op jit(solution)/shard_map/ppermute | solution.py:301
  33.3 4.5 %collective-permute-start.1 = (bf16[1,2,64,1024]{3,2,1,0:T(8,128)(2,1)S(1)}, bf16[1,2,64,1024]{3,2,1,0:T(8,128)(2,1)S(1)}, u32[]{:S(2)}, u32[]{:S(2)}) collective-permute-start(bf16[1,2,64,1024]{3,2,1,0:T(8,128)(2,1)S(1)} %reshape.15), channel_id=1, source_target_pairs={{0,256},{128,384},{256,0},{384,128},{1,257},{129,385},{257,1},{385... | collective-permute-start | bytes 786440 | tf_op jit(solution)/shard_map/ppermute | solution.py:301
  37.9 2.8 %collective-permute-start.2 = (bf16[1,2,64,1024]{3,2,1,0:T(8,128)(2,1)S(1)}, bf16[1,2,64,1024]{3,2,1,0:T(8,128)(2,1)S(1)}, u32[]{:S(2)}, u32[]{:S(2)}) collective-permute-start(bf16[1,2,64,1024]{3,2,1,0:T(8,128)(2,1)S(1)} %reshape.15), channel_id=1, source_target_pairs={{0,384},{128,0},{256,128},{384,256},{1,385},{129,1},{257,129},{385... | collective-permute-start | bytes 786440 | tf_op jit(solution)/shard_map/ppermute | solution.py:301
  40.7 84.9 %collective-permute-done = bf16[1,2,64,1024]{3,2,1,0:T(8,128)(2,1)S(1)} collective-permute-done((bf16[1,2,64,1024]{3,2,1,0:T(8,128)(2,1)S(1)}, bf16[1,2,64,1024]{3,2,1,0:T(8,128)(2,1)S(1)}, u32[]{:S(2)}, u32[]{:S(2)}) %collective-permute-start) | collective-permute-done | bytes 262176 | tf_op jit(solution)/shard_map/ppermute | solution.py:301
  125.6 10.5 %collective-permute-done.1 = bf16[1,2,64,1024]{3,2,1,0:T(8,128)(2,1)S(1)} collective-permute-done((bf16[1,2,64,1024]{3,2,1,0:T(8,128)(2,1)S(1)}, bf16[1,2,64,1024]{3,2,1,0:T(8,128)(2,1)S(1)}, u32[]{:S(2)}, u32[]{:S(2)}) %collective-permute-start.1) | collective-permute-done | bytes 262176 | tf_op jit(solution)/shard_map/ppermute | solution.py:301
  136.2 3.2 %collective-permute-start.3 = (bf16[4,2,64,1024]{3,2,1,0:T(8,128)(2,1)S(1)}, bf16[4,2,64,1024]{3,2,1,0:T(8,128)(2,1)}, u32[]{:S(2)}, u32[]{:S(2)}) collective-permute-start(bf16[4,2,64,1024]{3,2,1,0:T(8,128)(2,1)S(1)} %constant_dynamic-update-slice_fusion.refs_0_), channel_id=1, source_target_pairs={{0,32},{32,64},{64,96},{96,0},{1,33},{33,65},{65,97},{97,1},{2,34}... | collective-permute-start | bytes 3145736 | tf_op jit(solution)/shard_map/ppermute | solution.py:307
  139.3 4.4 %collective-permute-start.4 = (bf16[4,2,64,1024]{3,2,1,0:T(8,128)(2,1)S(1)}, bf16[4,2,64,1024]{3,2,1,0:T(8,128)(2,1)}, u32[]{:S(2)}, u32[]{:S(2)}) collective-permute-start(bf16[4,2,64,1024]{3,2,1,0:T(8,128)(2,1)S(1)} %constant_dynamic-update-slice_fusion.refs_0_), channel_id=1, source_target_pairs={{0,64},{32,96},{64,0},{96,32},{1,65},{33,97},{65,1},{97,33},{2,66}... | collective-permute-start | bytes 3145736 | tf_op jit(solution)/shard_map/ppermute | solution.py:307
  143.8 3.0 %collective-permute-start.5 = (bf16[4,2,64,1024]{3,2,1,0:T(8,128)(2,1)S(1)}, bf16[4,2,64,1024]{3,2,1,0:T(8,128)(2,1)}, u32[]{:S(2)}, u32[]{:S(2)}) collective-permute-start(bf16[4,2,64,1024]{3,2,1,0:T(8,128)(2,1)S(1)} %constant_dynamic-update-slice_fusion.refs_0_), channel_id=1, source_target_pairs={{0,96},{32,0},{64,32},{96,64},{1,97},{33,1},{65,33},{97,65},{2,98}... | collective-permute-start | bytes 3145736 | tf_op jit(solution)/shard_map/ppermute | solution.py:307
  146.8 4.3 %collective-permute-start.6 = (bf16[4,2,64,1024]{3,2,1,0:T(8,128)(2,1)S(1)}, bf16[4,2,64,1024]{3,2,1,0:T(8,128)(2,1)}, u32[]{:S(2)}, u32[]{:S(2)}) collective-permute-start(bf16[4,2,64,1024]{3,2,1,0:T(8,128)(2,1)S(1)} %constant_dynamic-update-slice_fusion.refs_0_), channel_id=1, source_target_pairs={{0,16},{16,0},{1,17},{17,1},{2,18},{18,2},{3,19},{19,3},{4,20},{20... | collective-permute-start | bytes 3145736 | tf_op jit(solution)/shard_map/ppermute | solution.py:308
  151.1 11.5 %collective-permute-done.3.refs_1_ = bf16[4,2,64,1024]{3,2,1,0:T(8,128)(2,1)} collective-permute-done((bf16[4,2,64,1024]{3,2,1,0:T(8,128)(2,1)S(1)}, bf16[4,2,64,1024]{3,2,1,0:T(8,128)(2,1)}, u32[]{:S(2)}, u32[]{:S(2)}) %collective-permute-start.3) | collective-permute-done | bytes 1048608 | tf_op jit(solution)/shard_map/ppermute | solution.py:307
  162.6 5.2 %collective-permute-start.7 = (bf16[4,2,64,1024]{3,2,1,0:T(8,128)(2,1)}, bf16[4,2,64,1024]{3,2,1,0:T(8,128)(2,1)}, u32[]{:S(2)}, u32[]{:S(2)}) collective-permute-start(bf16[4,2,64,1024]{3,2,1,0:T(8,128)(2,1)} %collective-permute-done.3.refs_1_), channel_id=1, source_target_pairs={{0,16},{16,0},{1,17},{17,1},{2,18},{18,2},{3,19},{19,3},{4,20},{20... | collective-permute-start | bytes 3145736 | tf_op jit(solution)/shard_map/ppermute | solution.py:308
  167.7 18.4 %collective-permute-done.4.refs_2_ = bf16[4,2,64,1024]{3,2,1,0:T(8,128)(2,1)} collective-permute-done((bf16[4,2,64,1024]{3,2,1,0:T(8,128)(2,1)S(1)}, bf16[4,2,64,1024]{3,2,1,0:T(8,128)(2,1)}, u32[]{:S(2)}, u32[]{:S(2)}) %collective-permute-start.4) | collective-permute-done | bytes 1048608 | tf_op jit(solution)/shard_map/ppermute | solution.py:307
  186.1 4.3 %collective-permute-start.8 = (bf16[4,2,64,1024]{3,2,1,0:T(8,128)(2,1)}, bf16[4,2,64,1024]{3,2,1,0:T(8,128)(2,1)}, u32[]{:S(2)}, u32[]{:S(2)}) collective-permute-start(bf16[4,2,64,1024]{3,2,1,0:T(8,128)(2,1)} %collective-permute-done.4.refs_2_), channel_id=1, source_target_pairs={{0,16},{16,0},{1,17},{17,1},{2,18},{18,2},{3,19},{19,3},{4,20},{20... | collective-permute-start | bytes 3145736 | tf_op jit(solution)/shard_map/ppermute | solution.py:308
  190.4 1.9 collective-permute-start.9
  193.1 2.3 collective-permute-done.9.refs_7_
  196.7 6.6 %hot_parts.1 = (f32[224,1024]{1,0:T(8,128)}, bf16[224,1024]{1,0:T(8,128)(2,1)}) custom-call(s32[3]{0:T(128)} %pad_add_fusion.place_ref, bf16[4096,256]{1,0:T(8,128)(2,1)} %bitcast.16, bf16[4,2,64,1024]{3,2,1,0:T(8,128)(2,1)} %copy-done.1, bf16[4,2,64,1024]{3,2,1,0:T(8,128)(2,1)} %collective-permute-done.3.refs_1_, ...), custom_call_target="tpu_custom_call" | custom-call | flops 939524096 | bytes 6291456 | tf_op jit(solution)/shard_map/hot_parts/pallas_call | solution.py:212
  203.3 12.0 %collective-permute-start.10 = (bf16[224,1024]{1,0:T(8,128)(2,1)}, bf16[224,1024]{1,0:T(8,128)(2,1)S(1)}, u32[]{:S(2)}, u32[]{:S(2)}) collective-permute-start(bf16[224,1024]{1,0:T(8,128)(2,1)} %get-tuple-element.5), channel_id=1, source_target_pairs={{0,8},{1,9},{2,10},{3,11},{4,12},{5,13},{6,14},{7,15},{8,0},{9,1},... | collective-permute-start | bytes 1376264 | tf_op jit(solution)/shard_map/ppermute | solution.py:317
  215.2 7.9 %gate_parts.1 = f32[8,4,1,128]{3,2,1,0:T(1,128)} custom-call(s32[3]{0:T(128)} %pad_add_fusion.place_ref, bf16[4096,256]{1,0:T(8,128)(2,1)} %bitcast.17, bf16[2,224,1024]{2,1,0:T(8,128)(2,1)} %weight_ref.1, bf16[4,2,64,1024]{3,2,1,0:T(8,128)(2,1)} %copy-done.1, bf16[4,2,64,1024]{3,2,1,0:T(8,128)(2,1)} %collective-permute-done.3.refs_1_, ...), custom_call_target="tpu_custom_call" | custom-call | flops 1879048192 | bytes 11403264 | tf_op jit(solution)/shard_map/gate_parts/pallas_call | solution.py:184
  223.2 9.2 %all_to_all.15.parts_ref = f32[8,4,1,128]{3,2,1,0:T(1,128)} all-to-all(f32[8,4,1,128]{3,2,1,0:T(1,128)} %gate_parts.1), channel_id=1, replica_groups=mesh['zl'=4,'y'=4,'c'=2,'zh'=4,'x'=4] {'y','c'}, dimensions={0} | all-to-all | bytes 32768 | tf_op jit(solution)/shard_map/all_to_all | solution.py:319
  233.8 13.4 %all-to-all-start.2 = ((f32[64,1,8]{2,1,0:T(1,128)}), f32[64,1,8]{2,1,0:T(1,128)S(1)}, u32[]{:S(2)}, u32[]{:S(2)}) async-start(f32[64,1,8]{2,1,0:T(1,128)} %gate_totals.1), calls=%async_computation.2 | async-start | bytes 65536 | tf_op jit(solution)/shard_map/all_to_all | solution.py:322
  247.3 6.4 %cold_parts.1 = bf16[2,224,1024]{2,1,0:T(8,128)(2,1)} custom-call(s32[3]{0:T(128)} %pad_add_fusion.place_ref, bf16[4096,256]{1,0:T(8,128)(2,1)} %bitcast.18, bf16[4,2,64,1024]{3,2,1,0:T(8,128)(2,1)} %copy-done.1, bf16[4,2,64,1024]{3,2,1,0:T(8,128)(2,1)} %collective-permute-done.3.refs_1_, bf16[4,2,64,1024]{3,2,1,0:T(8,128)(2,1)} %collective-permute-done.4.refs_2_, ...), custom_call_target="tpu_custom_call" | custom-call | flops 939524096 | bytes 6291456 | tf_op jit(solution)/shard_map/cold_parts/pallas_call | solution.py:212
  253.6 11.6 %all-to-all-done.2.back_ref = f32[64,1,8]{2,1,0:T(1,128)S(1)} async-done(((f32[64,1,8]{2,1,0:T(1,128)}), f32[64,1,8]{2,1,0:T(1,128)S(1)}, u32[]{:S(2)}, u32[]{:S(2)}) %all-to-all-start.2) | async-done | bytes 2080 | tf_op jit(solution)/shard_map/all_to_all | solution.py:322
  (27 shorter events, 7.0 us)
Async XLA Ops:
  5.4 24.3 %copy-start.3 = (bf16[1,16,2,4,1024]{4,3,2,1,0:T(4,128)(2,1)S(1)}, bf16[1,16,2,4,1024]{4,3,2,1,0:T(4,128)(2,1)}, u32[]{:S(2)}) copy-start(bf16[1,16,2,4,1024]{4,3,2,1,0:T(4,128)(2,1)} %param.12) | copy-start | bytes 786436
  5.4 189.9 %all-to-all-start = ((bf16[512,8,256]{2,1,0:T(8,128)(2,1)}), bf16[512,8,256]{2,1,0:T(8,128)(2,1)S(1)}, u32[]{:S(2)}, u32[]{:S(2)}) async-start(bf16[512,8,256]{2,1,0:T(8,128)(2,1)} %bitcast.19), calls=%async_computation | async-start | bytes 4194304 | tf_op jit(solution)/shard_map/all_to_all | solution.py:313
  29.9 95.7 %collective-permute-start = (bf16[1,2,64,1024]{3,2,1,0:T(8,128)(2,1)S(1)}, bf16[1,2,64,1024]{3,2,1,0:T(8,128)(2,1)S(1)}, u32[]{:S(2)}, u32[]{:S(2)}) collective-permute-start(bf16[1,2,64,1024]{3,2,1,0:T(8,128)(2,1)S(1)} %reshape.15), channel_id=1, source_target_pairs={{0,128},{128,256},{256,384},{384,0},{1,129},{129,257},{257,385},{3... | collective-permute-start | bytes 786440 | tf_op jit(solution)/shard_map/ppermute | solution.py:301
  33.3 102.8 %collective-permute-start.1 = (bf16[1,2,64,1024]{3,2,1,0:T(8,128)(2,1)S(1)}, bf16[1,2,64,1024]{3,2,1,0:T(8,128)(2,1)S(1)}, u32[]{:S(2)}, u32[]{:S(2)}) collective-permute-start(bf16[1,2,64,1024]{3,2,1,0:T(8,128)(2,1)S(1)} %reshape.15), channel_id=1, source_target_pairs={{0,256},{128,384},{256,0},{384,128},{1,257},{129,385},{257,1},{385... | collective-permute-start | bytes 786440 | tf_op jit(solution)/shard_map/ppermute | solution.py:301
  37.9 98.3 %collective-permute-start.2 = (bf16[1,2,64,1024]{3,2,1,0:T(8,128)(2,1)S(1)}, bf16[1,2,64,1024]{3,2,1,0:T(8,128)(2,1)S(1)}, u32[]{:S(2)}, u32[]{:S(2)}) collective-permute-start(bf16[1,2,64,1024]{3,2,1,0:T(8,128)(2,1)S(1)} %reshape.15), channel_id=1, source_target_pairs={{0,384},{128,0},{256,128},{384,256},{1,385},{129,1},{257,129},{385... | collective-permute-start | bytes 786440 | tf_op jit(solution)/shard_map/ppermute | solution.py:301
  136.2 59.2 %copy-start.1 = (bf16[4,2,64,1024]{3,2,1,0:T(8,128)(2,1)}, bf16[4,2,64,1024]{3,2,1,0:T(8,128)(2,1)S(1)}, u32[]{:S(2)}) copy-start(bf16[4,2,64,1024]{3,2,1,0:T(8,128)(2,1)S(1)} %constant_dynamic-update-slice_fusion.refs_0_) | copy-start | bytes 3145732
  136.2 26.4 %collective-permute-start.3 = (bf16[4,2,64,1024]{3,2,1,0:T(8,128)(2,1)S(1)}, bf16[4,2,64,1024]{3,2,1,0:T(8,128)(2,1)}, u32[]{:S(2)}, u32[]{:S(2)}) collective-permute-start(bf16[4,2,64,1024]{3,2,1,0:T(8,128)(2,1)S(1)} %constant_dynamic-update-slice_fusion.refs_0_), channel_id=1, source_target_pairs={{0,32},{32,64},{64,96},{96,0},{1,33},{33,65},{65,97},{97,1},{2,34}... | collective-permute-start | bytes 3145736 | tf_op jit(solution)/shard_map/ppermute | solution.py:307
  139.3 46.8 %collective-permute-start.4 = (bf16[4,2,64,1024]{3,2,1,0:T(8,128)(2,1)S(1)}, bf16[4,2,64,1024]{3,2,1,0:T(8,128)(2,1)}, u32[]{:S(2)}, u32[]{:S(2)}) collective-permute-start(bf16[4,2,64,1024]{3,2,1,0:T(8,128)(2,1)S(1)} %constant_dynamic-update-slice_fusion.refs_0_), channel_id=1, source_target_pairs={{0,64},{32,96},{64,0},{96,32},{1,65},{33,97},{65,1},{97,33},{2,66}... | collective-permute-start | bytes 3145736 | tf_op jit(solution)/shard_map/ppermute | solution.py:307
  143.8 46.7 %collective-permute-start.5 = (bf16[4,2,64,1024]{3,2,1,0:T(8,128)(2,1)S(1)}, bf16[4,2,64,1024]{3,2,1,0:T(8,128)(2,1)}, u32[]{:S(2)}, u32[]{:S(2)}) collective-permute-start(bf16[4,2,64,1024]{3,2,1,0:T(8,128)(2,1)S(1)} %constant_dynamic-update-slice_fusion.refs_0_), channel_id=1, source_target_pairs={{0,96},{32,0},{64,32},{96,64},{1,97},{33,1},{65,33},{97,65},{2,98}... | collective-permute-start | bytes 3145736 | tf_op jit(solution)/shard_map/ppermute | solution.py:307
  146.8 46.2 %collective-permute-start.6 = (bf16[4,2,64,1024]{3,2,1,0:T(8,128)(2,1)S(1)}, bf16[4,2,64,1024]{3,2,1,0:T(8,128)(2,1)}, u32[]{:S(2)}, u32[]{:S(2)}) collective-permute-start(bf16[4,2,64,1024]{3,2,1,0:T(8,128)(2,1)S(1)} %constant_dynamic-update-slice_fusion.refs_0_), channel_id=1, source_target_pairs={{0,16},{16,0},{1,17},{17,1},{2,18},{18,2},{3,19},{19,3},{4,20},{20... | collective-permute-start | bytes 3145736 | tf_op jit(solution)/shard_map/ppermute | solution.py:308
  162.6 30.5 %collective-permute-start.7 = (bf16[4,2,64,1024]{3,2,1,0:T(8,128)(2,1)}, bf16[4,2,64,1024]{3,2,1,0:T(8,128)(2,1)}, u32[]{:S(2)}, u32[]{:S(2)}) collective-permute-start(bf16[4,2,64,1024]{3,2,1,0:T(8,128)(2,1)} %collective-permute-done.3.refs_1_), channel_id=1, source_target_pairs={{0,16},{16,0},{1,17},{17,1},{2,18},{18,2},{3,19},{19,3},{4,20},{20... | collective-permute-start | bytes 3145736 | tf_op jit(solution)/shard_map/ppermute | solution.py:308
  186.1 6.9 %collective-permute-start.8 = (bf16[4,2,64,1024]{3,2,1,0:T(8,128)(2,1)}, bf16[4,2,64,1024]{3,2,1,0:T(8,128)(2,1)}, u32[]{:S(2)}, u32[]{:S(2)}) collective-permute-start(bf16[4,2,64,1024]{3,2,1,0:T(8,128)(2,1)} %collective-permute-done.4.refs_2_), channel_id=1, source_target_pairs={{0,16},{16,0},{1,17},{17,1},{2,18},{18,2},{3,19},{19,3},{4,20},{20... | collective-permute-start | bytes 3145736 | tf_op jit(solution)/shard_map/ppermute | solution.py:308
  190.4 4.9 %collective-permute-start.9 = (bf16[4,2,64,1024]{3,2,1,0:T(8,128)(2,1)}, bf16[4,2,64,1024]{3,2,1,0:T(8,128)(2,1)}, u32[]{:S(2)}, u32[]{:S(2)}) collective-permute-start(bf16[4,2,64,1024]{3,2,1,0:T(8,128)(2,1)} %collective-permute-done.5.refs_3_), channel_id=1, source_target_pairs={{0,16},{16,0},{1,17},{17,1},{2,18},{18,2},{3,19},{19,3},{4,20},{20... | collective-permute-start | bytes 3145736 | tf_op jit(solution)/shard_map/ppermute | solution.py:308
  195.3 1.3 copy-start
  203.3 64.3 %collective-permute-start.10 = (bf16[224,1024]{1,0:T(8,128)(2,1)}, bf16[224,1024]{1,0:T(8,128)(2,1)S(1)}, u32[]{:S(2)}, u32[]{:S(2)}) collective-permute-start(bf16[224,1024]{1,0:T(8,128)(2,1)} %get-tuple-element.5), channel_id=1, source_target_pairs={{0,8},{1,9},{2,10},{3,11},{4,12},{5,13},{6,14},{7,15},{8,0},{9,1},... | collective-permute-start | bytes 1376264 | tf_op jit(solution)/shard_map/ppermute | solution.py:317
  233.8 31.4 %all-to-all-start.2 = ((f32[64,1,8]{2,1,0:T(1,128)}), f32[64,1,8]{2,1,0:T(1,128)S(1)}, u32[]{:S(2)}, u32[]{:S(2)}) async-start(f32[64,1,8]{2,1,0:T(1,128)} %gate_totals.1), calls=%async_computation.2 | async-start | bytes 65536 | tf_op jit(solution)/shard_map/all_to_all | solution.py:322
  247.3 20.3 %copy-start.2 = (f32[224,1024]{1,0:T(8,128)S(1)}, f32[224,1024]{1,0:T(8,128)}, u32[]{:S(2)}) copy-start(f32[224,1024]{1,0:T(8,128)} %get-tuple-element.4) | copy-start | bytes 2752516
  265.2 0.6 copy-start.4

commit v8 on v7

--- a/solution.py
+++ b/solution.py
@@ -16,6 +16,7 @@
 SLOTS = INSTANCES * CAP
 PIECE = 224
 WIDE = 256
+GRANT = 24 * 2**20
 
 
 def route_masks(ids_ref, pick_ref, place_ref):
@@ -154,13 +155,12 @@
 
 
 def hot_kernel(place_ref, rows_ref, *refs):
-    pieces, (hot_ref, send_ref, acc_ref) = refs[:-3], refs[-3:]
+    pieces, (send_ref, acc_ref) = refs[:-2], refs[-2:]
     hidden = jnp.concatenate([piece[...] for piece in pieces], axis=0)
     add_grad(acc_ref, instance_rows(rows_ref, piece_lines(place_ref))[0], hidden)
 
     @pl.when(pl.program_id(0) == pl.num_programs(0) - 1)
     def _():
-        hot_ref[...] = acc_ref[...]
         send_ref[...] = acc_ref[...].astype(BF16)
 
 
@@ -199,6 +199,7 @@
             bytes_accessed=4 * lines * steps * span * ff + 2 * rows.size + 2 * weight.size,
             transcendentals=0,
         ),
+        compiler_params=pltpu.CompilerParams(vmem_limit_bytes=GRANT),
         name="gate_parts",
     )(place, rows, weight, *pieces)
 
@@ -216,17 +217,16 @@
             grid=(steps,),
             in_specs=[pl.BlockSpec((lines * span * 2, WIDE), lambda s, m: (s, 0))]
             + [pl.BlockSpec((None, None, span, ff), lambda s, m: piece_index(s, m, which))] * lines,
-            out_specs=[whole, whole] if hot else half,
+            out_specs=whole if hot else half,
             scratch_shapes=[pltpu.VMEM((PIECE, ff), F32)],
         ),
-        out_shape=[jax.ShapeDtypeStruct((PIECE, ff), t) for t in (F32, BF16)]
-        if hot
-        else jax.ShapeDtypeStruct((2, PIECE, ff), BF16),
+        out_shape=jax.ShapeDtypeStruct((PIECE, ff) if hot else (2, PIECE, ff), BF16),
         cost_estimate=pl.CostEstimate(
             flops=2 * lines * steps * span * PIECE * ff,
             bytes_accessed=2 * lines * steps * span * ff + 2 * rows.size,
             transcendentals=0,
         ),
+        compiler_params=pltpu.CompilerParams(vmem_limit_bytes=GRANT),
         name="hot_parts" if hot else "cold_parts",
     )(place, rows, *pieces)
 
@@ -247,6 +247,7 @@
         in_specs=[vmem],
         out_specs=vmem,
         out_shape=jax.ShapeDtypeStruct((parts.shape[1] * expert, 1, 2 * CAP), F32),
+        compiler_params=pltpu.CompilerParams(vmem_limit_bytes=GRANT),
         name="gate_totals",
     )(parts)
 
@@ -282,6 +283,7 @@
         in_specs=[pl.BlockSpec(memory_space=pltpu.SMEM)] + [vmem] * 4,
         out_specs=vmem,
         out_shape=jax.ShapeDtypeStruct((TOP, TOK), F32),
+        compiler_params=pltpu.CompilerParams(vmem_limit_bytes=GRANT),
         name="pick_gates",
     )(placement, ids, pick, gates, back)
 
@@ -312,16 +314,16 @@
     sent = sent.reshape(dp * expert, 2 * CAP, WIDE)
     rows = lax.all_to_all(sent, EVERY, split_axis=0, concat_axis=0, tiled=True)
     rows = rows.reshape(dp * expert * 2 * CAP, WIDE)
-    hot, hot_sent = weight_parts(0, place, rows, pieces)
+    hot = weight_parts(0, place, rows, pieces)
     half = expert // 2
-    other = lax.ppermute(hot_sent, EXPERT, [(e, (e + half) % expert) for e in range(expert)])
+    other = lax.ppermute(hot, EXPERT, [(e, (e + half) % expert) for e in range(expert)])
     parts = gate_parts(place, rows, pieces, down_proj)
     parts = lax.all_to_all(parts, LINES, split_axis=0, concat_axis=0, tiled=True)
     grad = weight_parts(1, place, rows, pieces)
     own = gate_totals(parts, expert)
     back = lax.all_to_all(own, ("zl",) + EXPERT, split_axis=0, concat_axis=0, tiled=True)
     grad_gate = pick_gates(placement, ids, pick, gates, back).T
-    pair = (hot + other.astype(F32)).astype(BF16)
+    pair = (hot.astype(F32) + other.astype(F32)).astype(BF16)
     return lax.dynamic_update_slice(grad, pair[None], (0, 0, 0)), grad_gate
 
 

time: 271 us -> 269 us (level)
  starting transfers between devices: 86.7 us -> 104 us
  waiting for transfers between devices: 139 us -> 127 us
  Pallas kernels: 28.9 us -> 24.6 us
    ppermute x4, starting transfers between devices: 15.7 us -> 34.4 us  [layer(): lax.ppermute(piece, 'c', [(0, 1), (1, 0)])]
    ppermute x3, waiting for transfers between devices: 29.9 us -> 14.1 us  [layer(): lax.ppermute(column, 'y', [(y, (y + d) % 4) for y in range(4)])]
    all_to_all x1, waiting for transfers between devices: 11.6 us -> 14.6 us  [layer(): lax.all_to_all(own, ('zl',) + EXPERT, split_axis=0, concat_axis=0, tiled=...]
  transfers between devices with their start and end apart: 13 -> 13, of which waited for: 6 -> 6; matrix products, arithmetic and copies ran while one was open for 0% -> 0% of each run, Pallas kernels for 7% -> 5%
where the time goes in v8:
time: 269 us; the launch traced here: 268 us
  waiting for transfers between devices  127 us (47%)
  starting transfers between devices  104 us (39%)
  Pallas kernels  24.6 us (9%)
  blocking collectives  9.21 us (3%)
    ppermute x3, waiting for transfers between devices, layer(): lax.ppermute(local, 'zl', [(z, (z + d) % depth) for z in range(depth)])  95.4 us
    ppermute x4, starting transfers between devices, layer(): lax.ppermute(piece, 'c', [(0, 1), (1, 0)])  34.4 us
    all_to_all x1, starting transfers between devices, layer(): rows = lax.all_to_all(sent, EVERY, split_axis=0, concat_axis=0, tiled=True)  24.3 us
    all_to_all x1, waiting for transfers between devices, layer(): lax.all_to_all(own, ('zl',) + EXPERT, split_axis=0, concat_axis=0, tiled=...  14.6 us
    ppermute x3, waiting for transfers between devices, layer(): lax.ppermute(column, 'y', [(y, (y + d) % 4) for y in range(4)])  14.1 us
    all_to_all x1, starting transfers between devices, layer(): lax.all_to_all(own, ('zl',) + EXPERT, split_axis=0, concat_axis=0, tiled=...  13.4 us
    ppermute x1, starting transfers between devices, layer(): lax.ppermute(hot, EXPERT, [(e, (e + half) % expert) for e in range(expert)])  12 us
    pallas_call x2, Pallas kernels, weight_parts(): pl.pallas_call(hot_kernel if hot else cold_kernel, grid_spec=pltpu.Prefet...  11.2 us
  transfers between devices with their start and end apart: 13, of which 6 were waited for; matrix products, arithmetic and copies ran while one was open for 0% of the time, Pallas kernels for 5%

profile of v8, /device:TPU:1, one launch (start us, length us, event | category | flops | bytes accessed | tf_op | source)
XLA Modules:
  0.0 268.0 jit_solution(9045851574922601091)
XLA Ops:
  0.6 4.8 %gather_rows.1 = bf16[32,128,256]{2,1,0:T(8,128)(2,1)} custom-call(s32[32]{0:T(128)} %place_ref.3, s32[8,128]{1,0:T(8,128)} %bitcast.19, s32[8,128]{1,0:T(8,128)} %bitcast.21, f32[8,128]{1,0:T(8,128)} %bitcast.23, bf16[128,7168]{1,0:T(8,128)(2,1)} %grad_ref.1), custom_call_target="tpu_custom_call" | custom-call | flops 234881024 | bytes 3670016 | tf_op jit(solution)/shard_map/gather_rows/pallas_call | solution.py:73
  5.4 24.3 %all-to-all-start = ((bf16[512,8,256]{2,1,0:T(8,128)(2,1)}), bf16[512,8,256]{2,1,0:T(8,128)(2,1)S(1)}, u32[]{:S(2)}, u32[]{:S(2)}) async-start(bf16[512,8,256]{2,1,0:T(8,128)(2,1)} %bitcast.25), calls=%async_computation | async-start | bytes 4194304 | tf_op jit(solution)/shard_map/all_to_all | solution.py:315
  29.9 3.4 %collective-permute-start = (bf16[1,2,64,1024]{3,2,1,0:T(8,128)(2,1)S(1)}, bf16[1,2,64,1024]{3,2,1,0:T(8,128)(2,1)S(1)}, u32[]{:S(2)}, u32[]{:S(2)}) collective-permute-start(bf16[1,2,64,1024]{3,2,1,0:T(8,128)(2,1)S(1)} %reshape.15), channel_id=1, source_target_pairs={{0,128},{128,256},{256,384},{384,0},{1,129},{129,257},{257,385},{3... | collective-permute-start | bytes 786440 | tf_op jit(solution)/shard_map/ppermute | solution.py:303
  33.3 4.5 %collective-permute-start.1 = (bf16[1,2,64,1024]{3,2,1,0:T(8,128)(2,1)S(1)}, bf16[1,2,64,1024]{3,2,1,0:T(8,128)(2,1)S(1)}, u32[]{:S(2)}, u32[]{:S(2)}) collective-permute-start(bf16[1,2,64,1024]{3,2,1,0:T(8,128)(2,1)S(1)} %reshape.15), channel_id=1, source_target_pairs={{0,256},{128,384},{256,0},{384,128},{1,257},{129,385},{257,1},{385... | collective-permute-start | bytes 786440 | tf_op jit(solution)/shard_map/ppermute | solution.py:303
  37.9 2.8 %collective-permute-start.2 = (bf16[1,2,64,1024]{3,2,1,0:T(8,128)(2,1)S(1)}, bf16[1,2,64,1024]{3,2,1,0:T(8,128)(2,1)S(1)}, u32[]{:S(2)}, u32[]{:S(2)}) collective-permute-start(bf16[1,2,64,1024]{3,2,1,0:T(8,128)(2,1)S(1)} %reshape.15), channel_id=1, source_target_pairs={{0,384},{128,0},{256,128},{384,256},{1,385},{129,1},{257,129},{385... | collective-permute-start | bytes 786440 | tf_op jit(solution)/shard_map/ppermute | solution.py:303
  40.7 84.9 %collective-permute-done = bf16[1,2,64,1024]{3,2,1,0:T(8,128)(2,1)S(1)} collective-permute-done((bf16[1,2,64,1024]{3,2,1,0:T(8,128)(2,1)S(1)}, bf16[1,2,64,1024]{3,2,1,0:T(8,128)(2,1)S(1)}, u32[]{:S(2)}, u32[]{:S(2)}) %collective-permute-start) | collective-permute-done | bytes 262176 | tf_op jit(solution)/shard_map/ppermute | solution.py:303
  125.6 10.5 %collective-permute-done.1 = bf16[1,2,64,1024]{3,2,1,0:T(8,128)(2,1)S(1)} collective-permute-done((bf16[1,2,64,1024]{3,2,1,0:T(8,128)(2,1)S(1)}, bf16[1,2,64,1024]{3,2,1,0:T(8,128)(2,1)S(1)}, u32[]{:S(2)}, u32[]{:S(2)}) %collective-permute-start.1) | collective-permute-done | bytes 262176 | tf_op jit(solution)/shard_map/ppermute | solution.py:303
  136.2 4.5 %collective-permute-start.5 = (bf16[4,2,64,1024]{3,2,1,0:T(8,128)(2,1)S(1)}, bf16[4,2,64,1024]{3,2,1,0:T(8,128)(2,1)}, u32[]{:S(2)}, u32[]{:S(2)}) collective-permute-start(bf16[4,2,64,1024]{3,2,1,0:T(8,128)(2,1)S(1)} %constant_dynamic-update-slice_fusion.refs_0_), channel_id=1, source_target_pairs={{0,96},{32,0},{64,32},{96,64},{1,97},{33,1},{65,33},{97,65},{2,98}... | collective-permute-start | bytes 3145736 | tf_op jit(solution)/shard_map/ppermute | solution.py:309
  140.7 2.4 collective-permute-start.4
  143.0 2.6 collective-permute-start.3
  145.6 4.3 %collective-permute-start.6 = (bf16[4,2,64,1024]{3,2,1,0:T(8,128)(2,1)S(1)}, bf16[4,2,64,1024]{3,2,1,0:T(8,128)(2,1)}, u32[]{:S(2)}, u32[]{:S(2)}) collective-permute-start(bf16[4,2,64,1024]{3,2,1,0:T(8,128)(2,1)S(1)} %constant_dynamic-update-slice_fusion.refs_0_), channel_id=1, source_target_pairs={{0,16},{16,0},{1,17},{17,1},{2,18},{18,2},{3,19},{19,3},{4,20},{20... | collective-permute-start | bytes 3145736 | tf_op jit(solution)/shard_map/ppermute | solution.py:310
  149.9 12.7 %collective-permute-done.5.refs_3_ = bf16[4,2,64,1024]{3,2,1,0:T(8,128)(2,1)} collective-permute-done((bf16[4,2,64,1024]{3,2,1,0:T(8,128)(2,1)S(1)}, bf16[4,2,64,1024]{3,2,1,0:T(8,128)(2,1)}, u32[]{:S(2)}, u32[]{:S(2)}) %collective-permute-start.5) | collective-permute-done | bytes 1048608 | tf_op jit(solution)/shard_map/ppermute | solution.py:309
  162.6 25.8 %collective-permute-start.9 = (bf16[4,2,64,1024]{3,2,1,0:T(8,128)(2,1)}, bf16[4,2,64,1024]{3,2,1,0:T(8,128)(2,1)}, u32[]{:S(2)}, u32[]{:S(2)}) collective-permute-start(bf16[4,2,64,1024]{3,2,1,0:T(8,128)(2,1)} %collective-permute-done.5.refs_3_), channel_id=1, source_target_pairs={{0,16},{16,0},{1,17},{17,1},{2,18},{18,2},{3,19},{19,3},{4,20},{20... | collective-permute-start | bytes 3145736 | tf_op jit(solution)/shard_map/ppermute | solution.py:310
  188.4 1.9 collective-permute-start.8
  191.7 2.4 collective-permute-start.7
  194.2 2.5 collective-permute-done.7.refs_5_
  196.7 5.6 %hot_parts.1 = bf16[224,1024]{1,0:T(8,128)(2,1)} custom-call(s32[3]{0:T(128)S(1)} %pad_add_fusion.place_ref, bf16[4096,256]{1,0:T(8,128)(2,1)S(1)} %bitcast.16, bf16[4,2,64,1024]{3,2,1,0:T(8,128)(2,1)S(1)} %constant_dynamic-update-slice_fusion.refs_0_, bf16[4,2,64,1024]{3,2,1,0:T(8,128)(2,1)} %collective-permute-done.3.refs_1_, ...), custom_call_target="tpu_custom_call" | custom-call | flops 939524096 | bytes 6291456 | tf_op jit(solution)/shard_map/hot_parts/pallas_call | solution.py:213
  202.4 12.0 %collective-permute-start.10 = (bf16[224,1024]{1,0:T(8,128)(2,1)}, bf16[224,1024]{1,0:T(8,128)(2,1)}, u32[]{:S(2)}, u32[]{:S(2)}) collective-permute-start(bf16[224,1024]{1,0:T(8,128)(2,1)} %hot_parts.1), channel_id=1, source_target_pairs={{0,8},{1,9},{2,10},{3,11},{4,12},{5,13},{6,14},{7,15},{8,0},{9,1},... | collective-permute-start | bytes 1376264 | tf_op jit(solution)/shard_map/ppermute | solution.py:319
  214.3 6.3 %gate_parts.1 = f32[8,4,1,128]{3,2,1,0:T(1,128)S(1)} custom-call(s32[3]{0:T(128)S(1)} %pad_add_fusion.place_ref, bf16[4096,256]{1,0:T(8,128)(2,1)S(1)} %bitcast.17, bf16[2,224,1024]{2,1,0:T(8,128)(2,1)S(1)} %copy-done, bf16[4,2,64,1024]{3,2,1,0:T(8,128)(2,1)S(1)} %constant_dynamic-update-slice_fusion.refs_0_, ...), custom_call_target="tpu_custom_call" | custom-call | flops 1879048192 | bytes 11403264 | tf_op jit(solution)/shard_map/gate_parts/pallas_call | solution.py:184
  220.7 9.2 %all_to_all.15.parts_ref = f32[8,4,1,128]{3,2,1,0:T(1,128)S(1)} all-to-all(f32[8,4,1,128]{3,2,1,0:T(1,128)S(1)} %gate_parts.1), channel_id=1, replica_groups=mesh['zl'=4,'y'=4,'c'=2,'zh'=4,'x'=4] {'y','c'}, dimensions={0} | all-to-all | bytes 32768 | tf_op jit(solution)/shard_map/all_to_all | solution.py:321
  230.6 13.4 %all-to-all-start.2 = ((f32[64,1,8]{2,1,0:T(1,128)}), f32[64,1,8]{2,1,0:T(1,128)S(1)}, u32[]{:S(2)}, u32[]{:S(2)}) async-start(f32[64,1,8]{2,1,0:T(1,128)} %gate_totals.1), calls=%async_computation.2 | async-start | bytes 65536 | tf_op jit(solution)/shard_map/all_to_all | solution.py:324
  244.1 5.6 %cold_parts.1 = bf16[2,224,1024]{2,1,0:T(8,128)(2,1)} custom-call(s32[3]{0:T(128)S(1)} %pad_add_fusion.place_ref, bf16[4096,256]{1,0:T(8,128)(2,1)S(1)} %bitcast.18, bf16[4,2,64,1024]{3,2,1,0:T(8,128)(2,1)S(1)} %constant_dynamic-update-slice_fusion.refs_0_, bf16[4,2,64,1024]{3,2,1,0:T(8,128)(2,1)} %collective-permute-done.3.refs_1_, ...), custom_call_target="tpu_custom_call" | custom-call | flops 939524096 | bytes 6291456 | tf_op jit(solution)/shard_map/cold_parts/pallas_call | solution.py:213
  249.7 14.6 %all-to-all-done.2.back_ref = f32[64,1,8]{2,1,0:T(1,128)S(1)} async-done(((f32[64,1,8]{2,1,0:T(1,128)}), f32[64,1,8]{2,1,0:T(1,128)S(1)}, u32[]{:S(2)}, u32[]{:S(2)}) %all-to-all-start.2) | async-done | bytes 2080 | tf_op jit(solution)/shard_map/all_to_all | solution.py:324
  265.9 2.1 fusion.1
  (29 shorter events, 4.0 us)
Async XLA Ops:
  5.4 24.3 %copy-start.5 = (bf16[1,16,2,4,1024]{4,3,2,1,0:T(4,128)(2,1)S(1)}, bf16[1,16,2,4,1024]{4,3,2,1,0:T(4,128)(2,1)}, u32[]{:S(2)}) copy-start(bf16[1,16,2,4,1024]{4,3,2,1,0:T(4,128)(2,1)} %param.12) | copy-start | bytes 786436
  5.4 191.3 %all-to-all-start = ((bf16[512,8,256]{2,1,0:T(8,128)(2,1)}), bf16[512,8,256]{2,1,0:T(8,128)(2,1)S(1)}, u32[]{:S(2)}, u32[]{:S(2)}) async-start(bf16[512,8,256]{2,1,0:T(8,128)(2,1)} %bitcast.25), calls=%async_computation | async-start | bytes 4194304 | tf_op jit(solution)/shard_map/all_to_all | solution.py:315
  29.9 95.7 %collective-permute-start = (bf16[1,2,64,1024]{3,2,1,0:T(8,128)(2,1)S(1)}, bf16[1,2,64,1024]{3,2,1,0:T(8,128)(2,1)S(1)}, u32[]{:S(2)}, u32[]{:S(2)}) collective-permute-start(bf16[1,2,64,1024]{3,2,1,0:T(8,128)(2,1)S(1)} %reshape.15), channel_id=1, source_target_pairs={{0,128},{128,256},{256,384},{384,0},{1,129},{129,257},{257,385},{3... | collective-permute-start | bytes 786440 | tf_op jit(solution)/shard_map/ppermute | solution.py:303
  33.3 102.8 %collective-permute-start.1 = (bf16[1,2,64,1024]{3,2,1,0:T(8,128)(2,1)S(1)}, bf16[1,2,64,1024]{3,2,1,0:T(8,128)(2,1)S(1)}, u32[]{:S(2)}, u32[]{:S(2)}) collective-permute-start(bf16[1,2,64,1024]{3,2,1,0:T(8,128)(2,1)S(1)} %reshape.15), channel_id=1, source_target_pairs={{0,256},{128,384},{256,0},{384,128},{1,257},{129,385},{257,1},{385... | collective-permute-start | bytes 786440 | tf_op jit(solution)/shard_map/ppermute | solution.py:303
  37.9 98.3 %collective-permute-start.2 = (bf16[1,2,64,1024]{3,2,1,0:T(8,128)(2,1)S(1)}, bf16[1,2,64,1024]{3,2,1,0:T(8,128)(2,1)S(1)}, u32[]{:S(2)}, u32[]{:S(2)}) collective-permute-start(bf16[1,2,64,1024]{3,2,1,0:T(8,128)(2,1)S(1)} %reshape.15), channel_id=1, source_target_pairs={{0,384},{128,0},{256,128},{384,256},{1,385},{129,1},{257,129},{385... | collective-permute-start | bytes 786440 | tf_op jit(solution)/shard_map/ppermute | solution.py:303
  136.2 26.4 %collective-permute-start.5 = (bf16[4,2,64,1024]{3,2,1,0:T(8,128)(2,1)S(1)}, bf16[4,2,64,1024]{3,2,1,0:T(8,128)(2,1)}, u32[]{:S(2)}, u32[]{:S(2)}) collective-permute-start(bf16[4,2,64,1024]{3,2,1,0:T(8,128)(2,1)S(1)} %constant_dynamic-update-slice_fusion.refs_0_), channel_id=1, source_target_pairs={{0,96},{32,0},{64,32},{96,64},{1,97},{33,1},{65,33},{97,65},{2,98}... | collective-permute-start | bytes 3145736 | tf_op jit(solution)/shard_map/ppermute | solution.py:309
  140.7 47.7 %collective-permute-start.4 = (bf16[4,2,64,1024]{3,2,1,0:T(8,128)(2,1)S(1)}, bf16[4,2,64,1024]{3,2,1,0:T(8,128)(2,1)}, u32[]{:S(2)}, u32[]{:S(2)}) collective-permute-start(bf16[4,2,64,1024]{3,2,1,0:T(8,128)(2,1)S(1)} %constant_dynamic-update-slice_fusion.refs_0_), channel_id=1, source_target_pairs={{0,64},{32,96},{64,0},{96,32},{1,65},{33,97},{65,1},{97,33},{2,66}... | collective-permute-start | bytes 3145736 | tf_op jit(solution)/shard_map/ppermute | solution.py:309
  143.0 48.7 %collective-permute-start.3 = (bf16[4,2,64,1024]{3,2,1,0:T(8,128)(2,1)S(1)}, bf16[4,2,64,1024]{3,2,1,0:T(8,128)(2,1)}, u32[]{:S(2)}, u32[]{:S(2)}) collective-permute-start(bf16[4,2,64,1024]{3,2,1,0:T(8,128)(2,1)S(1)} %constant_dynamic-update-slice_fusion.refs_0_), channel_id=1, source_target_pairs={{0,32},{32,64},{64,96},{96,0},{1,33},{33,65},{65,97},{97,1},{2,34}... | collective-permute-start | bytes 3145736 | tf_op jit(solution)/shard_map/ppermute | solution.py:309
  145.6 48.6 %collective-permute-start.6 = (bf16[4,2,64,1024]{3,2,1,0:T(8,128)(2,1)S(1)}, bf16[4,2,64,1024]{3,2,1,0:T(8,128)(2,1)}, u32[]{:S(2)}, u32[]{:S(2)}) collective-permute-start(bf16[4,2,64,1024]{3,2,1,0:T(8,128)(2,1)S(1)} %constant_dynamic-update-slice_fusion.refs_0_), channel_id=1, source_target_pairs={{0,16},{16,0},{1,17},{17,1},{2,18},{18,2},{3,19},{19,3},{4,20},{20... | collective-permute-start | bytes 3145736 | tf_op jit(solution)/shard_map/ppermute | solution.py:310
  162.6 31.7 %collective-permute-start.9 = (bf16[4,2,64,1024]{3,2,1,0:T(8,128)(2,1)}, bf16[4,2,64,1024]{3,2,1,0:T(8,128)(2,1)}, u32[]{:S(2)}, u32[]{:S(2)}) collective-permute-start(bf16[4,2,64,1024]{3,2,1,0:T(8,128)(2,1)} %collective-permute-done.5.refs_3_), channel_id=1, source_target_pairs={{0,16},{16,0},{1,17},{17,1},{2,18},{18,2},{3,19},{19,3},{4,20},{20... | collective-permute-start | bytes 3145736 | tf_op jit(solution)/shard_map/ppermute | solution.py:310
  188.4 5.8 %collective-permute-start.8 = (bf16[4,2,64,1024]{3,2,1,0:T(8,128)(2,1)}, bf16[4,2,64,1024]{3,2,1,0:T(8,128)(2,1)}, u32[]{:S(2)}, u32[]{:S(2)}) collective-permute-start(bf16[4,2,64,1024]{3,2,1,0:T(8,128)(2,1)} %collective-permute-done.4.refs_2_), channel_id=1, source_target_pairs={{0,16},{16,0},{1,17},{17,1},{2,18},{18,2},{3,19},{19,3},{4,20},{20... | collective-permute-start | bytes 3145736 | tf_op jit(solution)/shard_map/ppermute | solution.py:310
  191.7 5.0 %collective-permute-start.7 = (bf16[4,2,64,1024]{3,2,1,0:T(8,128)(2,1)}, bf16[4,2,64,1024]{3,2,1,0:T(8,128)(2,1)}, u32[]{:S(2)}, u32[]{:S(2)}) collective-permute-start(bf16[4,2,64,1024]{3,2,1,0:T(8,128)(2,1)} %collective-permute-done.3.refs_1_), channel_id=1, source_target_pairs={{0,16},{16,0},{1,17},{17,1},{2,18},{18,2},{3,19},{19,3},{4,20},{20... | collective-permute-start | bytes 3145736 | tf_op jit(solution)/shard_map/ppermute | solution.py:310
  196.7 17.6 %copy-start = (bf16[2,224,1024]{2,1,0:T(8,128)(2,1)S(1)}, bf16[2,224,1024]{2,1,0:T(8,128)(2,1)}, u32[]{:S(2)}) copy-start(bf16[2,224,1024]{2,1,0:T(8,128)(2,1)} %weight_ref.1) | copy-start | bytes 2752516
  202.4 63.5 %collective-permute-start.10 = (bf16[224,1024]{1,0:T(8,128)(2,1)}, bf16[224,1024]{1,0:T(8,128)(2,1)}, u32[]{:S(2)}, u32[]{:S(2)}) collective-permute-start(bf16[224,1024]{1,0:T(8,128)(2,1)} %hot_parts.1), channel_id=1, source_target_pairs={{0,8},{1,9},{2,10},{3,11},{4,12},{5,13},{6,14},{7,15},{8,0},{9,1},... | collective-permute-start | bytes 1376264 | tf_op jit(solution)/shard_map/ppermute | solution.py:319
  230.6 33.7 %all-to-all-start.2 = ((f32[64,1,8]{2,1,0:T(1,128)}), f32[64,1,8]{2,1,0:T(1,128)S(1)}, u32[]{:S(2)}, u32[]{:S(2)}) async-start(f32[64,1,8]{2,1,0:T(1,128)} %gate_totals.1), calls=%async_computation.2 | async-start | bytes 65536 | tf_op jit(solution)/shard_map/all_to_all | solution.py:324
  244.1 20.3 %copy-start.1 = (s32[128,8]{0,1:T(8,128)S(1)}, s32[128,8]{0,1:T(8,128)}, u32[]{:S(2)}) copy-start(s32[128,8]{0,1:T(8,128)} %param.9) | copy-start | bytes 12292
  244.1 20.3 %copy-start.2 = (s32[128,8]{0,1:T(8,128)S(1)}, s32[128,8]{0,1:T(8,128)}, u32[]{:S(2)}) copy-start(s32[128,8]{0,1:T(8,128)} %param.10) | copy-start | bytes 12292
  244.1 20.2 %copy-start.3 = (f32[128,8]{0,1:T(8,128)S(1)}, f32[128,8]{0,1:T(8,128)}, u32[]{:S(2)}) copy-start(f32[128,8]{0,1:T(8,128)} %param.8) | copy-start | bytes 12292
  244.1 20.2 %copy-start.4 = (s32[32]{0:T(128)S(1)}, s32[32]{0:T(128)}, u32[]{:S(2)}) copy-start(s32[32]{0:T(128)} %place_ref.3) | copy-start | bytes 388
